TPU v7x, 128 devices: a whole 4x4x4 slice. The times are simulated.
128 devices in a mesh: epoch: 4 (over z), patch: 32 (over x, y, core).
Axes of the slice: x: 4, y: 4, z: 4, core: 2. Of those that a mesh axis runs over, the one named last changes fastest.
Arguments:
- tile_image: bfloat16 [4096, 256, 256], P(('epoch', 'patch')), may hold values from -6 to 6
- tile_var: bfloat16 [4096, 256, 256], P(('epoch', 'patch')), may hold values from 0.25 to 4
- psf_coef: float32 [4096, 18], P(('epoch', 'patch')), may hold values from -3 to 3
- tile_patch: int32 [4096, 1], P(('epoch', 'patch')), may hold values from 0 to 31; in each aligned block of 32 rows (0 to 31, 32 to 63, ...) at most 2 rows name the same one
- tile_offset: int32 [4096, 2], P(('epoch', 'patch')), may hold values from 0 to 256
- tile_visit: int32 [4096], P(('epoch', 'patch')), may hold values from 0 to 7
- visit_scale: float32 [8], replicated, may hold values from 0.5 to 2
Outputs:
- numerator: float32 [32, 512, 512], P('patch', 'epoch')
- inv_variance: float32 [32, 512, 512], P('patch', 'epoch')
Inputs may be any that keep to these rules, and one draw needn't show every extreme that they name: `tile_patch`: among the rows of one device, no patch is named more than 2 times; some patch is named exactly 2 times.
All inputs are finite; a program needn't handle non-finite values.
Results may differ from a plain program's by a relative error of at most 0.019.
Values may be sent and summed in bfloat16 or wider, within the bound.
No kernel may reach another device: no remote copies, remote signals or barrier semaphores. Data moves between devices by JAX's collectives and lax.ppermute only.
A program may use at most 256 MiB of HBM per device.

v0:
```python
import jax
import jax.numpy as jnp
from jax import lax
from jax.sharding import PartitionSpec as P

VISITS = 8


sigmas = (1.0, 2.0, 3.5)
kernel_reach = 7


def kernels(tile_side):
    positions = jnp.arange(tile_side)
    distance = (positions[:, None] - positions[None, :]).astype(jnp.float32)
    tap_offsets = jnp.arange(-kernel_reach, kernel_reach + 1).astype(jnp.float32)
    tables = []
    for sigma in sigmas:
        profile = jnp.where(
            jnp.abs(distance) <= kernel_reach,
            jnp.exp(-distance * distance / (2.0 * sigma * sigma)),
            0.0,
        )
        summed = jnp.sum(jnp.exp(-tap_offsets * tap_offsets / (2.0 * sigma * sigma)))
        tables.append(profile / summed)
    return jnp.stack(tables).astype(jnp.bfloat16)


def poly_terms(tile_side):
    coordinate = (2.0 * jnp.arange(tile_side).astype(jnp.float32) + 1.0) / tile_side - 1.0
    row_coord = jnp.broadcast_to(coordinate[:, None], (tile_side, tile_side))
    column_coord = jnp.broadcast_to(coordinate[None, :], (tile_side, tile_side))
    return jnp.stack(
        [
            jnp.ones_like(row_coord),
            row_coord,
            column_coord,
            row_coord * row_coord,
            row_coord * column_coord,
            column_coord * column_coord,
        ]
    )


def match_tiles(image_tiles, variance, coefficients, visit_gain, present):
    tile_side = image_tiles.shape[-1]
    kernel = kernels(tile_side)
    terms = poly_terms(tile_side)
    factors = coefficients.reshape(-1, 3, 6).astype(jnp.float32)
    matched = jnp.zeros(image_tiles.shape, jnp.float32)
    for basis in range(3):
        row_pass = jnp.einsum(
            "nij,kj->nik", image_tiles, kernel[basis], preferred_element_type=jnp.float32
        ).astype(jnp.bfloat16)
        blurred = jnp.einsum(
            "li,nik->nlk", kernel[basis], row_pass, preferred_element_type=jnp.float32
        )
        spatial = jnp.einsum(
            "nj,jlk->nlk", factors[:, basis], terms, precision=lax.Precision.HIGHEST
        )
        matched = matched + spatial * blurred
    weights = present[:, None, None] / (
        variance.astype(jnp.float32) + (1.0 - present)[:, None, None]
    )
    weighted = visit_gain[:, None, None] * weights * matched
    return jnp.stack([weighted, weights], axis=1).astype(jnp.bfloat16)


def place_tiles(tiles, offsets, patch_side):
    tile_count = tiles.shape[0]
    channels = tiles.shape[1]
    tile_side = tiles.shape[-1]
    zero_index = jnp.zeros((), jnp.int32)

    def add_slot(member, summed):
        corner = (
            zero_index,
            offsets[member, 0].astype(jnp.int32),
            offsets[member, 1].astype(jnp.int32),
        )
        region = lax.dynamic_slice(summed, corner, (channels, tile_side, tile_side))
        region = region + tiles[member].astype(jnp.float32)
        return lax.dynamic_update_slice(summed, region, corner)

    initial = jnp.zeros((channels, patch_side, patch_side), jnp.float32)
    return lax.fori_loop(0, tile_count, add_slot, initial)


def shards(tile_image, tile_var, psf_coef, tile_patch, tile_offset, tile_visit, visit_scale):
    tile_count = tile_image.shape[0]
    tile_side = tile_image.shape[1]
    patch_side = 2 * tile_side
    peer_count = lax.axis_size("patch")
    capacity = 2 * tile_count // peer_count
    target = tile_patch[:, 0]
    onehot = (target[:, None] == jnp.arange(peer_count, dtype=jnp.int32)[None, :]).astype(jnp.int32)
    before = jnp.cumsum(onehot, axis=0) - onehot
    slot_index = jnp.sum(before * onehot, axis=1)
    position = target * capacity + slot_index
    visit_onehot = (tile_visit[:, None] == jnp.arange(VISITS, dtype=jnp.int32)[None, :]).astype(
        jnp.float32
    )
    visit_gain = jnp.dot(visit_onehot, visit_scale, precision=lax.Precision.HIGHEST)
    present = jnp.ones((tile_count,), jnp.float32)

    def packed(values):
        buffer = (
            jnp.zeros((peer_count * capacity,) + values.shape[1:], values.dtype)
            .at[position]
            .set(values)
        )
        return buffer.reshape((peer_count, capacity) + values.shape[1:])

    pixels = jnp.stack([tile_image, tile_var], axis=1)
    details = jnp.concatenate([psf_coef, visit_gain[:, None], present[:, None]], axis=1)
    slot_pixels = lax.all_to_all(packed(pixels), "patch", split_axis=0, concat_axis=0, tiled=True)
    slot_details = lax.all_to_all(
        packed(details).astype(jnp.bfloat16), "patch", split_axis=0, concat_axis=0, tiled=True
    ).astype(jnp.float32)
    slot_shifts = lax.all_to_all(
        packed(tile_offset), "patch", split_axis=0, concat_axis=0, tiled=True
    )
    leading = slot_pixels.shape[:2]
    flat_pixels = slot_pixels.reshape((-1,) + slot_pixels.shape[2:])
    flat_details = slot_details.reshape((-1, slot_details.shape[-1]))
    result_tiles = match_tiles(
        flat_pixels[:, 0],
        flat_pixels[:, 1],
        flat_details[:, :18],
        flat_details[:, 18],
        flat_details[:, 19],
    )
    matched = result_tiles.reshape(leading + result_tiles.shape[1:])
    shifts = slot_shifts
    matched = matched.reshape((-1, 2, tile_side, tile_side))
    shifts = shifts.reshape((-1, 2))
    partial_value = place_tiles(matched, shifts, patch_side)
    summed = lax.psum(partial_value.astype(jnp.bfloat16), "epoch").astype(jnp.float32)
    row_count = patch_side // lax.axis_size("epoch")
    result = lax.dynamic_slice_in_dim(summed, lax.axis_index("epoch") * row_count, row_count, 1)
    return (result[0][None], result[1][None])


def solution(mesh):
    placed = (
        P(("epoch", "patch"), None, None),
        P(("epoch", "patch"), None, None),
        P(("epoch", "patch"), None),
        P(("epoch", "patch"), None),
        P(("epoch", "patch"), None),
        P(("epoch", "patch")),
        P(),
    )
    return jax.shard_map(
        shards,
        mesh=mesh,
        in_specs=placed,
        out_specs=(P("patch", "epoch", None), P("patch", "epoch", None)),
        check_vma=False,
    )
```

profile of v0, /device:TPU:1, one launch (start us, length us, event | category | flops | bytes accessed | tf_op | source)
XLA Modules:
  0.0 1604.4 jit_solution(482598703645133494)
XLA Ops:
  52.6 21.4 %scatter_fusion = bf16[64,2,256,256]{3,2,1,0:T(8,128)(2,1)} fusion(bf16[64,2,256,256]{3,2,1,0:T(8,128)(2,1)} %broadcast_in_dim.20, s32[32]{0:T(128)S(1)} %fusion.75, bf16[32,2,256,256]{3,2,1,0:T(8,128)(2,1)} %copy.44), kind=kCustom, calls=%fused_computation.2 | custom fusion | bytes 25165952 | tf_op jit(solution)/shard_map/scatter | solution.py:110
  74.0 30.7 %copy.45 = bf16[32,2,2,256,256]{4,1,3,2,0:T(2,128)(2,1)} copy(bf16[32,2,2,256,256]{4,3,2,1,0:T(8,128)(2,1)} %bitcast.114) | data formatting | bytes 33554432 | tf_op jit(solution)/shard_map/reshape | solution.py:112
  121.6 9.6 fusion.73
  131.2 9.6 fusion.74
  140.8 202.6 %all-to-all-done.2 = bf16[32,2,2,256,256]{4,1,3,2,0:T(2,128)(2,1)} async-done(((bf16[32,2,2,256,256]{4,1,3,2,0:T(2,128)(2,1)}), bf16[32,2,2,256,256]{4,1,3,2,0:T(2,128)(2,1)}, u32[]{:S(2)}, u32[]{:S(2)}) %all-to-all-start.2) | async-done | bytes 16777248 | tf_op jit(solution)/shard_map/all_to_all | solution.py:116
  343.4 18.2 %copy.46 = bf16[32,2,2,256,256]{4,1,0,3,2:T(2,128)(2,1)} copy(bf16[32,2,2,256,256]{4,1,3,2,0:T(2,128)(2,1)} %all-to-all-done.2) | data formatting | bytes 33554432 | tf_op jit(solution)/shard_map/all_to_all | solution.py:116
  361.6 24.9 %reshape.185 = bf16[64,2,256,256]{3,0,2,1:T(8,128)(2,1)} reshape(bf16[32,2,2,256,256]{4,1,0,3,2:T(2,128)(2,1)} %copy.46) | data formatting | bytes 33554432 | tf_op jit(solution)/shard_map/reshape | solution.py:124
  394.7 19.8 %fusion.13 = f32[64,256,256]{2,1,0:T(8,128)} fusion(bf16[64,256,256]{2,0,1:T(8,128)(2,1)} %slice_bitcast_fusion, f32[]{:T(128)} %exponential_reduce_fusion.2), kind=kOutput, calls=%fused_computation.27 | convolution fusion | flops 4300472320 | bytes 25165828 | tf_op jit(solution)/shard_map/li,nik->nlk/dot_general | solution.py:55
  414.5 17.7 %copy.50 = f32[64,256,256]{1,0,2:T(8,128)} copy(f32[64,256,256]{2,1,0:T(8,128)} %fusion.13) | data formatting | bytes 33554432 | tf_op jit(solution)/shard_map/li,nik->nlk/dot_general | solution.py:55
  432.2 19.4 %fusion.11 = f32[64,256,256]{2,1,0:T(8,128)} fusion(bf16[64,256,256]{2,0,1:T(8,128)(2,1)} %slice_bitcast_fusion, f32[]{:T(128)} %exponential_reduce_fusion.1), kind=kOutput, calls=%fused_computation.25 | convolution fusion | flops 4300472320 | bytes 25165828 | tf_op jit(solution)/shard_map/li,nik->nlk/dot_general | solution.py:55
  451.6 17.7 %copy.53 = f32[64,256,256]{1,0,2:T(8,128)} copy(f32[64,256,256]{2,1,0:T(8,128)} %fusion.11) | data formatting | bytes 33554432 | tf_op jit(solution)/shard_map/li,nik->nlk/dot_general | solution.py:55
  469.3 19.4 %fusion.9 = f32[64,256,256]{2,1,0:T(8,128)} fusion(bf16[64,256,256]{2,0,1:T(8,128)(2,1)} %slice_bitcast_fusion, f32[]{:T(128)} %exponential_reduce_fusion), kind=kOutput, calls=%fused_computation.23 | convolution fusion | flops 4300472320 | bytes 25165828 | tf_op jit(solution)/shard_map/li,nik->nlk/dot_general | solution.py:55
  488.7 17.7 %copy.56 = f32[64,256,256]{1,0,2:T(8,128)} copy(f32[64,256,256]{2,1,0:T(8,128)} %fusion.9) | data formatting | bytes 33554432 | tf_op jit(solution)/shard_map/li,nik->nlk/dot_general | solution.py:55
  506.4 8.9 fusion.5
  515.3 34.2 %fusion.21 = bf16[64,1,256,256]{3,0,2,1:T(8,128)(2,1)} fusion(f32[64,256,256]{1,0,2:T(8,128)} %copy.56, f32[6,256,256]{2,0,1:T(8,128)S(1)} %stack.38, f32[64,256,256]{2,0,1:T(8,128)} %fusion.73, f32[64,256,256]{1,0,2:T(8,128)} %copy.53, f32[64,256,256]{2,0,1:T(8,128)} %fusion.74, f32[64,256,256]{1,0,2:T(8,128)} %copy.50, f32[64]{0:T(128)S(1)} %broadcast_subtract_fusion, ...), kind=kOutput, calls=%fused_computation.35 | convolution fusion | flops 348127232 | bytes 102764032 | tf_op jit(solution)/shard_map/nj,jlk->nlk/dot_general | solution.py:58
  557.6 21.4 %copy.57 = bf16[64,2,256,256]{3,2,1,0:T(8,128)(2,1)} copy(bf16[64,2,256,256]{3,0,2,1:T(8,128)(2,1)S(1)} %pad_maximum_fusion) | data formatting | bytes 33554432 | tf_op jit(solution)/shard_map/while | solution.py:86
  579.2 927.6 %while.13 = (s32[]{:T(128)}, f32[2,512,512]{2,1,0:T(8,128)S(1)}, s32[64,2]{0,1:T(2,128)S(1)}, bf16[64,2,256,256]{3,2,1,0:T(8,128)(2,1)}, s32[]{:T(128)}, /*index=5*/s32[]{:T(128)}, s32[]{:T(128)}) while((s32[]{:T(128)}, f32[2,512,512]{2,1,0:T(8,128)S(1)}, s32[64,2]{0,1:T(2,128)S(1)}, bf16[64,2,256,256]{3,2,1,0:T(8,128)(2,1)}, s32[]{:T(128)}, ...), condition=%wide.region_9.10_spmd, body=%wide.region_8.9_spmd.sunk | while | flops 262152 | bytes 2359477 | solution.py:86
  598.4 9.5 dynamic_update_slice.8
  625.7 9.5 dynamic_update_slice.8
  640.6 9.4 dynamic_update_slice.8
  655.5 9.5 dynamic_update_slice.8
  684.6 9.5 dynamic_update_slice.8
  699.5 8.8 dynamic_update_slice.8
  713.7 9.5 dynamic_update_slice.8
  742.0 9.5 dynamic_update_slice.8
  756.9 9.1 dynamic_update_slice.8
  771.5 9.5 dynamic_update_slice.8
  786.4 10.2 dynamic_update_slice.8
  802.0 9.5 dynamic_update_slice.8
  829.4 9.5 dynamic_update_slice.8
  858.4 9.5 dynamic_update_slice.8
  887.3 9.5 dynamic_update_slice.8
  916.0 9.5 dynamic_update_slice.8
  943.3 9.5 dynamic_update_slice.8
  972.1 9.5 dynamic_update_slice.8
  1000.8 9.5 dynamic_update_slice.8
  1028.9 9.5 dynamic_update_slice.8
  1057.1 9.5 dynamic_update_slice.8
  1072.0 9.7 dynamic_update_slice.8
  1087.1 9.5 dynamic_update_slice.8
  1102.0 9.5 dynamic_update_slice.8
  1116.9 9.5 dynamic_update_slice.8
  1131.8 9.1 dynamic_update_slice.8
  1146.3 9.5 dynamic_update_slice.8
  1174.7 9.5 dynamic_update_slice.8
  1203.0 9.5 dynamic_update_slice.8
  1232.1 9.5 dynamic_update_slice.8
  1260.1 9.5 dynamic_update_slice.8
  1288.1 9.5 dynamic_update_slice.8
  1303.0 9.1 dynamic_update_slice.8
  1317.5 9.5 dynamic_update_slice.8
  1332.4 9.5 dynamic_update_slice.8
  1347.3 9.5 dynamic_update_slice.8
  1362.2 10.0 dynamic_update_slice.8
  1377.6 9.5 dynamic_update_slice.8
  1392.5 9.5 dynamic_update_slice.8
  1407.4 9.5 dynamic_update_slice.8
  1422.3 9.5 dynamic_update_slice.8
  1437.2 9.5 dynamic_update_slice.8
  1452.2 10.4 dynamic_update_slice.8
  1468.0 9.5 dynamic_update_slice.8
  1482.9 9.0 dynamic_update_slice.8
  1497.3 9.5 dynamic_update_slice.8
  1508.0 87.5 %all-reduce.2.cloned.1.call-done = bf16[2,512,512]{2,1,0:T(8,128)(2,1)} async-done(((bf16[2,512,512]{2,1,0:T(8,128)(2,1)}), bf16[2,512,512]{2,1,0:T(8,128)(2,1)}) %all-reduce.2.cloned.1.call-update) | async-done | bytes 1048592 | tf_op jit(solution)/shard_map/psum | solution.py:138
  (198 shorter events, 338.8 us)
Async XLA Ops:
  7.2 13.3 copy-start
  11.8 15.9 all-to-all-start
  27.7 77.0 %all-to-all-start.1 = ((bf16[32,2,20]{2,1,0:T(2,128)(2,1)}), bf16[32,2,20]{2,1,0:T(2,128)(2,1)S(1)}, u32[]{:S(2)}, u32[]{:S(2)}) async-start(bf16[32,2,20]{2,1,0:T(2,128)(2,1)} %bitcast.10), calls=%async_computation.1 | async-start | bytes 32768 | tf_op jit(solution)/shard_map/all_to_all | solution.py:117
  104.7 238.7 %all-to-all-start.2 = ((bf16[32,2,2,256,256]{4,1,3,2,0:T(2,128)(2,1)}), bf16[32,2,2,256,256]{4,1,3,2,0:T(2,128)(2,1)}, u32[]{:S(2)}, u32[]{:S(2)}) async-start(bf16[32,2,2,256,256]{4,1,3,2,0:T(2,128)(2,1)} %copy.45), calls=%async_computation.2 | async-start | bytes 33554432 | tf_op jit(solution)/shard_map/all_to_all | solution.py:116
  112.2 1483.3 %all-reduce.2.cloned.1.call-start = ((), (), s32[]{:S(2)}) async-start(), calls=%async_computation.3 | async-start | bytes 2097152 | tf_op jit(solution)/shard_map/psum | solution.py:138
  579.2 1018.1 %copy-start.1 = (f32[8]{0:T(128)S(1)}, f32[8]{0:T(128)}, u32[]{:S(2)}) copy-start(f32[8]{0:T(128)} %param.15) | copy-start | bytes 100
Sparse Core Ops, SparseCore 0:
  1508.1 87.3 all-reduce.1
where the time goes:
time: 1620 us; the launch traced here: 1600 us
  local copies, waits for them, and re-layouts  821 us (51%)
  waiting for transfers between devices  294 us (18%)
  loops' own time  234 us (14%)
  matrix products  113 us (7%)
  other arithmetic  107 us (7%)
  starting transfers between devices  20.3 us (1%)
    dynamic_update_slice x64, local copies, waits for them, and re-layouts, add_slot(): return lax.dynamic_update_slice(summed, region, corner)  581 us
    another operation x1, loops' own time, place_tiles(): return lax.fori_loop(0, tile_count, add_slot, initial)  234 us
    all_to_all x1, waiting for transfers between devices, shards(): lax.all_to_all(packed(pixels), 'patch', split_axis=0, concat_axis=0, tile...  203 us
    psum x1, waiting for transfers between devices, shards(): lax.psum(partial_value.astype(jnp.bfloat16), 'epoch').astype(jnp.float32)  87.5 us
    add x64, other arithmetic, add_slot(): region = region + tiles[member].astype(jnp.float32)  75 us
    dot_general x3, matrix products, match_tiles(): jnp.einsum('li,nik->nlk', kernel[basis], row_pass, preferred_element_type...  58.6 us
    dot_general x3, matrix products, match_tiles(): jnp.einsum('nj,jlk->nlk', factors[:, basis], terms, precision=lax.Precisi...  53.5 us
    dot_general x3, local copies, waits for them, and re-layouts, match_tiles(): jnp.einsum('li,nik->nlk', kernel[basis], row_pass, preferred_element_type...  53.1 us
  transfers between devices with their start and end apart: 4, of which 3 were waited for; matrix products, arithmetic and copies ran while one was open for 7% of the time, Pallas kernels for 0%

commit v1 on v0

v1 whole, which is shorter than its diff:
```python
import functools

import jax
import jax.numpy as jnp
import numpy as np
from jax import lax
from jax.experimental import pallas as pl
from jax.experimental.pallas import tpu as pltpu
from jax.sharding import PartitionSpec as P

SIGMAS = (1.0, 2.0, 3.5)
REACH = 7
GROUP = 4
UNROLL = 4


def blur_kernels(side):
    place = np.arange(side)
    distance = (place[:, None] - place[None, :]).astype(np.float32)
    taps = np.arange(-REACH, REACH + 1).astype(np.float32)
    tables = []
    for sigma in SIGMAS:
        scale = np.float32(2.0 * sigma * sigma)
        profile = np.where(np.abs(distance) <= REACH, np.exp(-distance * distance / scale), np.float32(0.0))
        tables.append(profile / np.sum(np.exp(-taps * taps / scale), dtype=np.float32))
    return np.concatenate(tables, axis=1).astype(jnp.bfloat16)


def fold_rows(side, rows_ref):
    @pl.when(pl.program_id(0) == 0)
    def _():
        s = lax.broadcasted_iota(jnp.int32, (side, side), 0)
        rows_ref[...] = ((s >> 2) & 1) * (side // 2) + 4 * (s >> 3) + (s & 3)


def fold(tile, off_r, off_c, rows_ref):
    side = tile.shape[0]
    lanes = lax.broadcasted_iota(jnp.int32, (side, side), 1)
    pick = ((lanes + off_r) & (side - 1)) == rows_ref[...]
    turn = jnp.where(pick, 1.0, 0.0).astype(jnp.bfloat16)
    placed = jnp.dot(turn, tile, preferred_element_type=jnp.float32)
    return pltpu.roll(placed, off_c & (side - 1), 1)


def weight_body(off_ref, var_ref, out_ref, rows_ref):
    parts = out_ref.shape[0]
    side = var_ref.shape[-1]
    fold_rows(side, rows_ref)
    for t in range(GROUP):
        tile = pl.program_id(0) * GROUP + t
        weight = (1.0 / var_ref[t].astype(jnp.float32)).astype(jnp.bfloat16)
        placed = fold(weight, off_ref[0, tile], off_ref[1, tile], rows_ref)
        out_ref[:, t] = placed.reshape(parts, side // parts, side).astype(jnp.bfloat16)


def value_body(off_ref, visit_ref, scale_ref, coef_ref, kernel_ref, image_ref, var_ref, out_ref, rows_ref, blur_ref, tile_ref):
    parts = out_ref.shape[0]
    side = var_ref.shape[-1]
    fold_rows(side, rows_ref)
    chunk = 32
    x = (2.0 * lax.broadcasted_iota(jnp.int32, (chunk, side), 1).astype(jnp.float32) + 1.0) / side - 1.0
    rows = lax.broadcasted_iota(jnp.int32, (chunk, side), 0)
    for t in range(GROUP):
        tile = pl.program_id(0) * GROUP + t
        gain = scale_ref[visit_ref[tile]]
        row_pass = jnp.dot(image_ref[t], kernel_ref[...], preferred_element_type=jnp.float32).astype(jnp.bfloat16)
        for b in range(3):
            cols = slice(b * side, (b + 1) * side)
            blur_ref[b] = jnp.dot(kernel_ref[:, cols], row_pass[:, cols], preferred_element_type=jnp.float32)
        for c in range(side // chunk):
            band = slice(c * chunk, (c + 1) * chunk)
            y = (2.0 * (rows + c * chunk).astype(jnp.float32) + 1.0) / side - 1.0
            matched = None
            for b in range(3):
                k = [coef_ref[6 * b + j, tile] for j in range(6)]
                spatial = (k[0] + y * (k[1] + k[3] * y)) + x * ((k[2] + k[4] * y) + k[5] * x)
                term = spatial * blur_ref[b, band]
                matched = term if matched is None else matched + term
            weight = 1.0 / var_ref[t, band].astype(jnp.float32)
            tile_ref[band] = (gain * weight * matched).astype(jnp.bfloat16)
        placed = fold(tile_ref[...], off_ref[0, tile], off_ref[1, tile], rows_ref)
        out_ref[:, t] = placed.reshape(parts, side // parts, side).astype(jnp.bfloat16)


def sum_body(start_ref, order_ref, part_ref, data_ref, *refs):
    out_ref = refs[-1]
    patches = start_ref.shape[0] - 1
    height, side = data_ref.shape[-2:]
    s = lax.broadcasted_iota(jnp.int32, (height, side), 0)
    row = (s >> 2) * (side // 2) + 4 * part_ref[0] + (s & 3)
    lane = lax.broadcasted_iota(jnp.int32, (height, side), 1)
    first = lax.broadcasted_iota(jnp.int32, (height, 2 * side), 0) < height // 2
    zero = jnp.zeros((height, side), jnp.float32)

    def one_patch(p, unused):
        begin, end = start_ref[p], start_ref[p + 1]

        def some_tiles(step, sums):
            sums = list(sums)
            for u in range(UNROLL):
                k = begin + step * UNROLL + u
                word = order_ref[jnp.minimum(k, end - 1)]
                there = jnp.where(k < end, 1.0, 0.0)
                tile, off_r, off_c = word & 1023, (word >> 10) & 511, word >> 19
                value = data_ref[tile].astype(jnp.float32) * there
                left = jnp.where(lane >= off_c, value, 0.0)
                right = value - left
                upper = row >= off_r
                sums[0] += jnp.where(upper, left, 0.0)
                sums[1] += jnp.where(upper, right, 0.0)
                sums[2] += jnp.where(upper, 0.0, left)
                sums[3] += jnp.where(upper, 0.0, right)
            return tuple(sums)

        sums = lax.fori_loop(0, (end - begin + UNROLL - 1) // UNROLL, some_tiles, (zero,) * 4)
        for half in range(2):
            mine = jnp.concatenate([sums[2 * half], sums[2 * half + 1]], axis=1)
            if len(refs) == 1:
                out_ref[half, p] = mine
            else:
                other = refs[0][half, p]
                swap = height // 2
                out_ref[2 * half, p] = jnp.where(first, mine, pltpu.roll(other, swap, 0)).astype(jnp.bfloat16)
                out_ref[2 * half + 1, p] = jnp.where(first, pltpu.roll(mine, swap, 0), other).astype(jnp.bfloat16)
        return unused

    lax.fori_loop(0, patches, one_patch, 0)


def final_body(got_ref, value_ref, weight_ref):
    epochs, parts, height, width = got_ref.shape
    swap = height // 2
    first = lax.broadcasted_iota(jnp.int32, (height, width), 0) < swap
    for pair in range(parts // 2):
        both = []
        for part in (2 * pair, 2 * pair + 1):
            total = got_ref[0, part].astype(jnp.float32)
            for e in range(1, epochs):
                total = total + got_ref[e, part].astype(jnp.float32)
            both.append(total)
        rows = slice(pair * height, (pair + 1) * height)
        value_ref[0, rows] = jnp.where(first, both[0], pltpu.roll(both[1], swap, 0))
        weight_ref[0, rows] = jnp.where(first, pltpu.roll(both[0], swap, 0), both[1])


def shards(tile_image, tile_var, psf_coef, tile_patch, tile_offset, tile_visit, visit_scale):
    count, side = tile_image.shape[:2]
    parts = lax.axis_size("patch")
    epochs = lax.axis_size("epoch")
    height = side // parts
    me = lax.axis_index("patch")
    table = jnp.asarray(blur_kernels(side))

    brief = (tile_patch + (tile_offset[:, :1] << 5) + (tile_offset[:, 1:] << 14))[:, 0]
    known = lax.all_to_all(jnp.broadcast_to(brief[None], (parts, count)), "patch", split_axis=0, concat_axis=0, tiled=True)
    known = known.reshape(-1)
    place = jnp.arange(parts * count, dtype=jnp.int32)
    target, word = known & 31, (known >> 5 << 10) + place
    ahead = (target[None, :] < target[:, None]) | ((target[None, :] == target[:, None]) & (place[None, :] < place[:, None]))
    rank = jnp.sum(ahead.astype(jnp.int32), axis=1)
    order = jnp.sum(jnp.where(rank[None, :] == place[:, None], word[None, :], 0), axis=1)
    start = jnp.sum((target[None, :] < jnp.arange(parts + 1, dtype=jnp.int32)[:, None]).astype(jnp.int32), axis=1)

    smem = pl.BlockSpec(memory_space=pltpu.SMEM)
    whole = lambda shape: pl.BlockSpec(shape, lambda g: (0,) * len(shape))
    tiles = pl.BlockSpec((GROUP, side, side), lambda g: (g, 0, 0))
    sent = pl.BlockSpec((parts, GROUP, height, side), lambda g: (0, g, 0, 0))
    sent_shape = jax.ShapeDtypeStruct((parts, count, height, side), jnp.bfloat16)
    pixels = count * side * side
    weights = pl.pallas_call(
        weight_body,
        grid=(count // GROUP,),
        in_specs=[smem, tiles],
        out_specs=sent,
        out_shape=sent_shape,
        scratch_shapes=[pltpu.VMEM((side, side), jnp.int32)],
        cost_estimate=pl.CostEstimate(flops=2 * pixels * side, bytes_accessed=4 * pixels, transcendentals=0),
        name="weights",
    )(tile_offset.T, tile_var)
    tile_image, weights = lax.optimization_barrier((tile_image, weights))
    values = pl.pallas_call(
        value_body,
        grid=(count // GROUP,),
        in_specs=[smem, smem, smem, smem, whole((side, 3 * side)), tiles, tiles],
        out_specs=sent,
        out_shape=sent_shape,
        scratch_shapes=[pltpu.VMEM((side, side), jnp.int32), pltpu.VMEM((3, side, side), jnp.float32), pltpu.VMEM((side, side), jnp.bfloat16)],
        cost_estimate=pl.CostEstimate(flops=14 * pixels * side, bytes_accessed=6 * pixels, transcendentals=0),
        compiler_params=pltpu.CompilerParams(vmem_limit_bytes=40 << 20),
        name="values",
    )(tile_offset.T, tile_visit, visit_scale, psf_coef.T, table, tile_image, tile_var)

    vmem = pl.BlockSpec(memory_space=pltpu.VMEM)

    def by_patch(sent_rows, name, *other):
        got = lax.all_to_all(sent_rows, "patch", split_axis=0, concat_axis=0, tiled=True)
        got = got.reshape(parts * count, height, side)
        out = (4, jnp.bfloat16) if other else (2, jnp.float32)
        return pl.pallas_call(
            sum_body,
            in_specs=[smem, smem, smem, vmem] + [vmem] * len(other),
            out_specs=vmem,
            out_shape=jax.ShapeDtypeStruct((out[0], parts, height, 2 * side), out[1]),
            cost_estimate=pl.CostEstimate(flops=10 * pixels, bytes_accessed=3 * pixels, transcendentals=0),
            compiler_params=pltpu.CompilerParams(vmem_limit_bytes=32 << 20),
            name=name,
        )(start, order, me[None], got, *other)

    weight_sums = by_patch(weights, "weight_sums")
    sums = by_patch(values, "value_sums", weight_sums)
    sums = sums.reshape(epochs * parts, height, 2 * side)
    got = lax.all_to_all(sums, ("epoch", "patch"), split_axis=0, concat_axis=0, tiled=True)
    quarter = jax.ShapeDtypeStruct((1, 4 * parts, 2 * side), jnp.float32)
    return pl.pallas_call(
        final_body,
        in_specs=[vmem],
        out_specs=(vmem, vmem),
        out_shape=(quarter, quarter),
        name="final",
    )(got.reshape(epochs, parts, height, 2 * side))


def solution(mesh):
    placed = (
        P(("epoch", "patch"), None, None),
        P(("epoch", "patch"), None, None),
        P(("epoch", "patch"), None),
        P(("epoch", "patch"), None),
        P(("epoch", "patch"), None),
        P(("epoch", "patch")),
        P(),
    )
    return jax.shard_map(
        shards,
        mesh=mesh,
        in_specs=placed,
        out_specs=(P("patch", "epoch", None), P("patch", "epoch", None)),
        check_vma=False,
    )
```

time: 1620 us -> 179 us (0.11)
  local copies, waits for them, and re-layouts: 821 us -> 7.11 us
  loops' own time: 234 us -> 0 us
  waiting for transfers between devices: 294 us -> 64.8 us
  matrix products: 113 us -> 0 us
  other arithmetic: 107 us -> 2.33 us
  Pallas kernels: 0 us -> 51.6 us
  blocking collectives: 0 us -> 28.8 us
    dynamic_update_slice x64 -> x0, local copies, waits for them, and re-layouts: 581 us -> none  [add_slot(): return lax.dynamic_update_slice(summed, region, corner)]
    another operation x1 -> x0, loops' own time: 234 us -> none  [place_tiles(): return lax.fori_loop(0, tile_count, add_slot, initial)]
    all_to_all x3, waiting for transfers between devices: 207 us -> 64.8 us  [the longest x2 64.8 us: by_patch(): lax.all_to_all(sent_rows, 'patch', split_axis=0, concat_axis=0, tiled=True)]
    dot_general x7 -> x0, matrix products: 113 us -> none  [the longest x3 58.6 us: match_tiles(): jnp.einsum('li,nik->nlk', kernel[basis], row_pass, preferred_element_type...]
    psum x1 -> x0, waiting for transfers between devices: 87.5 us -> none  [shards(): lax.psum(partial_value.astype(jnp.bfloat16), 'epoch').astype(jnp.float32)]
    add x64 -> x1, other arithmetic: 75 us -> 0.01 us  [shards(): target, word = (known & 31, (known >> 5 << 10) + place)]
    reshape x5 -> x0, local copies, waits for them, and re-layouts: 56.6 us -> none  [the longest x2 31.6 us: packed(): return buffer.reshape((peer_count, capacity) + values.shape[1:])]
    dot_general x3 -> x0, local copies, waits for them, and re-layouts: 53.1 us -> none  [match_tiles(): jnp.einsum('li,nik->nlk', kernel[basis], row_pass, preferred_element_type...]
  transfers between devices with their start and end apart: 4 -> 3, of which waited for: 3 -> 2; matrix products, arithmetic and copies ran while one was open for 7% -> 1% of each run, Pallas kernels for 0% -> 22%
where the time goes in v1:
time: 179 us
  waiting for transfers between devices  64.8 us (36%)
  Pallas kernels  51.6 us (29%)
  blocking collectives  28.8 us (16%)
  starting transfers between devices  23.3 us (13%)
  local copies, waits for them, and re-layouts  7.11 us (4%)
  other arithmetic  2.33 us (1%)
    all_to_all x2, waiting for transfers between devices, by_patch(): lax.all_to_all(sent_rows, 'patch', split_axis=0, concat_axis=0, tiled=True)  64.8 us
    all_to_all x1, blocking collectives, shards(): lax.all_to_all(sums, ('epoch', 'patch'), split_axis=0, concat_axis=0, til...  28.8 us
    pallas_call x1, Pallas kernels, shards(): pl.pallas_call(value_body, grid=(count // GROUP,), in_specs=[smem, smem,...  21.9 us
    pallas_call x2, Pallas kernels, by_patch(): pl.pallas_call(sum_body, in_specs=[smem, smem, smem, vmem] + [vmem] * len...  19.4 us
    all_to_all x2, starting transfers between devices, by_patch(): lax.all_to_all(sent_rows, 'patch', split_axis=0, concat_axis=0, tiled=True)  14.8 us
    all_to_all x1, starting transfers between devices, shards(): lax.all_to_all(jnp.broadcast_to(brief[None], (parts, count)), 'patch', sp...  8.59 us
    pallas_call x1, Pallas kernels, shards(): pl.pallas_call(weight_body, grid=(count // GROUP,), in_specs=[smem, tiles...  8.21 us
    unnamed x16, local copies, waits for them, and re-layouts  6.35 us
  transfers between devices with their start and end apart: 3, of which 2 were waited for; matrix products, arithmetic and copies ran while one was open for 1% of the time, Pallas kernels for 22%

profile of v1, /device:TPU:1, one launch (start us, length us, event | category | flops | bytes accessed | tf_op | source)
XLA Modules:
  0.0 178.8 jit_solution(17889316631735138465)
XLA Ops:
  0.6 0.8 add_bitcast_fusion
  1.4 0.6 broadcast_in_dim.15
  2.0 8.6 %all-to-all-start = ((s32[32,1,32]{2,1,0:T(1,128)}), s32[32,1,32]{2,1,0:T(1,128)S(1)}, u32[]{:S(2)}, u32[]{:S(2)}) async-start(s32[32,1,32]{2,1,0:T(1,128)} %broadcast_in_dim.15), calls=%async_computation | async-start | bytes 32768 | tf_op jit(solution)/shard_map/all_to_all | solution.py:155
  10.6 8.2 %weights.1 = bf16[32,32,8,256]{3,2,1,0:T(8,128)(2,1)} custom-call(s32[2,32]{1,0:T(2,128)} %bitcast.10, bf16[32,256,256]{2,1,0:T(8,128)(2,1)} %var_ref.3), custom_call_target="tpu_custom_call" | custom-call | flops 1073741824 | bytes 8388608 | tf_op jit(solution)/shard_map/weights/pallas_call | solution.py:170
  18.8 0.0 copy-start.2
  18.8 0.0 copy-start.4
  18.8 0.0 copy-start.5
  18.8 0.0 copy-start.6
  18.8 0.0 copy-start.7
  18.8 0.0 all-to-all-done
  18.9 7.6 %all-to-all-start.2 = ((bf16[32,32,8,256]{3,2,1,0:T(8,128)(2,1)}), bf16[32,32,8,256]{3,2,1,0:T(8,128)(2,1)}, u32[]{:S(2)}, u32[]{:S(2)}) async-start(bf16[32,32,8,256]{3,2,1,0:T(8,128)(2,1)} %weights.1), calls=%async_computation.2 | async-start | bytes 8388608 | tf_op jit(solution)/shard_map/all_to_all | solution.py:196
  26.4 0.0 copy-done.2
  26.5 0.0 copy-done.4
  26.5 0.0 copy-done.5
  26.5 0.0 copy-done.6
  26.5 0.0 copy-done.7
  26.5 0.0 copy-start
  26.5 2.2 %copy-done = bf16[32,256,256]{2,1,0:T(8,128)(2,1)S(1)} copy-done((bf16[32,256,256]{2,1,0:T(8,128)(2,1)S(1)}, bf16[32,256,256]{2,1,0:T(8,128)(2,1)}, u32[]{:S(2)}) %copy-start) | copy-done | bytes 4194328
  28.7 0.0 copy-start.3
  28.7 2.2 %copy-done.3 = bf16[32,256,256]{2,1,0:T(8,128)(2,1)S(1)} copy-done((bf16[32,256,256]{2,1,0:T(8,128)(2,1)S(1)}, bf16[32,256,256]{2,1,0:T(8,128)(2,1)}, u32[]{:S(2)}) %copy-start.3) | copy-done | bytes 4194328
  30.9 21.9 %values.1 = bf16[32,32,8,256]{3,2,1,0:T(8,128)(2,1)S(1)} custom-call(s32[2,32]{1,0:T(2,128)S(1)} %bitcast.11, s32[32]{0:T(128)S(1)} %copy-done.5, f32[8]{0:T(128)S(1)} %copy-done.6, f32[18,32]{1,0:T(8,128)S(1)} %bitcast.12, bf16[256,768]{1,0:T(8,128)(2,1)S(1)} %copy-done.7, bf16[32,256,256]{2,1,0:T(8,128)(2,1)S(1)} %copy-done.3, ...), custom_call_target="tpu_custom_call" | custom-call | flops 7516192768 | bytes 12582912 | tf_op jit(solution)/shard_map/values/pallas_call | solution.py:181
  52.7 0.0 copy-start.1
  52.7 2.0 %copy-done.1 = bf16[32,32,8,256]{3,2,1,0:T(8,128)(2,1)} copy-done((bf16[32,32,8,256]{3,2,1,0:T(8,128)(2,1)}, bf16[32,32,8,256]{3,2,1,0:T(8,128)(2,1)S(1)}, u32[]{:S(2)}) %copy-start.1) | copy-done | bytes 4194328
  54.7 24.0 %all-to-all-done.2 = bf16[32,32,8,256]{3,2,1,0:T(8,128)(2,1)} async-done(((bf16[32,32,8,256]{3,2,1,0:T(8,128)(2,1)}), bf16[32,32,8,256]{3,2,1,0:T(8,128)(2,1)}, u32[]{:S(2)}, u32[]{:S(2)}) %all-to-all-start.2) | async-done | bytes 4194336 | tf_op jit(solution)/shard_map/all_to_all | solution.py:196
  78.7 7.2 %all-to-all-start.1 = ((bf16[32,32,8,256]{3,2,1,0:T(8,128)(2,1)}), bf16[32,32,8,256]{3,2,1,0:T(8,128)(2,1)}, u32[]{:S(2)}, u32[]{:S(2)}) async-start(bf16[32,32,8,256]{3,2,1,0:T(8,128)(2,1)} %copy-done.1), calls=%async_computation.1 | async-start | bytes 8388608 | tf_op jit(solution)/shard_map/all_to_all | solution.py:196
  85.8 0.1 shift-left_reduce_fusion
  85.9 0.1 shift_left.31
  86.0 0.1 and.23
  86.1 0.1 convert_reduce_fusion.1.start_ref
  86.2 0.8 convert_reduce_fusion
  87.1 0.5 select_reduce_fusion.order_ref
  87.6 9.7 %weight_sums.1.refs_0_ = f32[2,32,8,512]{3,2,1,0:T(8,128)S(1)} custom-call(s32[33]{0:T(128)S(1)} %convert_reduce_fusion.1.start_ref, s32[1024]{0:T(1024)S(1)} %select_reduce_fusion.order_ref, s32[1]{0:T(128)} %bitcast.1.part_ref, bf16[1024,8,256]{2,1,0:T(8,128)(2,1)} %bitcast.5.data_ref), custom_call_target="tpu_custom_call" | custom-call | flops 20971520 | bytes 6291456 | tf_op jit(solution)/shard_map/weight_sums/pallas_call | solution.py:199
  97.2 40.8 %all-to-all-done.1 = bf16[32,32,8,256]{3,2,1,0:T(8,128)(2,1)} async-done(((bf16[32,32,8,256]{3,2,1,0:T(8,128)(2,1)}), bf16[32,32,8,256]{3,2,1,0:T(8,128)(2,1)}, u32[]{:S(2)}, u32[]{:S(2)}) %all-to-all-start.1) | async-done | bytes 4194336 | tf_op jit(solution)/shard_map/all_to_all | solution.py:196
  138.1 9.8 %value_sums.1 = bf16[4,32,8,512]{3,2,1,0:T(8,128)(2,1)S(1)} custom-call(s32[33]{0:T(128)S(1)} %convert_reduce_fusion.1.start_ref, s32[1024]{0:T(1024)S(1)} %select_reduce_fusion.order_ref, s32[1]{0:T(128)} %bitcast.1.part_ref, bf16[1024,8,256]{2,1,0:T(8,128)(2,1)} %bitcast.4.data_ref, f32[2,32,8,512]{3,2,1,0:T(8,128)S(1)} %weight_sums.1.refs_0_), custom_call_target="tpu_custom_call" | custom-call | flops 20971520 | bytes 6291456 | tf_op jit(solution)/shard_map/value_sums/pallas_call | solution.py:199
  147.8 28.8 %all_to_all.21 = bf16[128,8,512]{2,1,0:T(8,128)(2,1)} all-to-all(bf16[128,8,512]{2,1,0:T(8,128)(2,1)S(1)} %bitcast.9), channel_id=1, replica_groups=mesh['epoch'=4,'patch'=32] {'epoch','patch'}, dimensions={0} | all-to-all | bytes 2097152 | tf_op jit(solution)/shard_map/all_to_all | solution.py:212
  176.6 2.2 %final.1 = (f32[1,128,512]{2,1,0:T(8,128)}, f32[1,128,512]{2,1,0:T(8,128)}) custom-call(bf16[4,32,8,512]{3,2,1,0:T(8,128)(2,1)} %bitcast.13), custom_call_target="tpu_custom_call" | custom-call | tf_op jit(solution)/shard_map/final/pallas_call | solution.py:214
  (1 shorter events, 0.0 us)
Async XLA Ops:
  2.0 16.8 %all-to-all-start = ((s32[32,1,32]{2,1,0:T(1,128)}), s32[32,1,32]{2,1,0:T(1,128)S(1)}, u32[]{:S(2)}, u32[]{:S(2)}) async-start(s32[32,1,32]{2,1,0:T(1,128)} %broadcast_in_dim.15), calls=%async_computation | async-start | bytes 32768 | tf_op jit(solution)/shard_map/all_to_all | solution.py:155
  18.8 7.6 %copy-start.2 = (s32[32,2]{0,1:T(2,128)S(1)}, s32[32,2]{0,1:T(2,128)}, u32[]{:S(2)}) copy-start(s32[32,2]{0,1:T(2,128)} %param.12) | copy-start | bytes 772
  18.8 7.6 %copy-start.4 = (f32[32,18]{0,1:T(8,128)S(1)}, f32[32,18]{0,1:T(8,128)}, u32[]{:S(2)}) copy-start(f32[32,18]{0,1:T(8,128)} %param.10) | copy-start | bytes 6916
  18.8 7.7 %copy-start.5 = (s32[32]{0:T(128)S(1)}, s32[32]{0:T(128)}, u32[]{:S(2)}) copy-start(s32[32]{0:T(128)} %visit_ref.1) | copy-start | bytes 388
  18.8 7.7 %copy-start.6 = (f32[8]{0:T(128)S(1)}, f32[8]{0:T(128)}, u32[]{:S(2)}) copy-start(f32[8]{0:T(128)} %scale_ref.1) | copy-start | bytes 100
  18.8 7.7 %copy-start.7 = (bf16[256,768]{1,0:T(8,128)(2,1)S(1)}, bf16[256,768]{1,0:T(8,128)(2,1)}, u32[]{:S(2)}) copy-start(bf16[256,768]{1,0:T(8,128)(2,1)} %constant.6.clone.kernel_ref) | copy-start | bytes 1179652
  18.9 59.8 %all-to-all-start.2 = ((bf16[32,32,8,256]{3,2,1,0:T(8,128)(2,1)}), bf16[32,32,8,256]{3,2,1,0:T(8,128)(2,1)}, u32[]{:S(2)}, u32[]{:S(2)}) async-start(bf16[32,32,8,256]{3,2,1,0:T(8,128)(2,1)} %weights.1), calls=%async_computation.2 | async-start | bytes 8388608 | tf_op jit(solution)/shard_map/all_to_all | solution.py:196
  26.5 2.2 %copy-start = (bf16[32,256,256]{2,1,0:T(8,128)(2,1)S(1)}, bf16[32,256,256]{2,1,0:T(8,128)(2,1)}, u32[]{:S(2)}) copy-start(bf16[32,256,256]{2,1,0:T(8,128)(2,1)} %var_ref.3) | copy-start | bytes 12582916
  28.7 2.2 %copy-start.3 = (bf16[32,256,256]{2,1,0:T(8,128)(2,1)S(1)}, bf16[32,256,256]{2,1,0:T(8,128)(2,1)}, u32[]{:S(2)}) copy-start(bf16[32,256,256]{2,1,0:T(8,128)(2,1)} %image_ref) | copy-start | bytes 12582916
  52.7 2.0 %copy-start.1 = (bf16[32,32,8,256]{3,2,1,0:T(8,128)(2,1)}, bf16[32,32,8,256]{3,2,1,0:T(8,128)(2,1)S(1)}, u32[]{:S(2)}) copy-start(bf16[32,32,8,256]{3,2,1,0:T(8,128)(2,1)S(1)} %values.1) | copy-start | bytes 12582916
  78.7 59.4 %all-to-all-start.1 = ((bf16[32,32,8,256]{3,2,1,0:T(8,128)(2,1)}), bf16[32,32,8,256]{3,2,1,0:T(8,128)(2,1)}, u32[]{:S(2)}, u32[]{:S(2)}) async-start(bf16[32,32,8,256]{3,2,1,0:T(8,128)(2,1)} %copy-done.1), calls=%async_computation.1 | async-start | bytes 8388608 | tf_op jit(solution)/shard_map/all_to_all | solution.py:196

commit v2 on v1

v2 whole, which is shorter than its diff:
```python
import jax
import jax.numpy as jnp
import numpy as np
from jax import lax
from jax.experimental import pallas as pl
from jax.experimental.pallas import tpu as pltpu
from jax.sharding import PartitionSpec as P

SIGMAS = (1.0, 2.0, 3.5)
REACH = 7
GROUP = 4


def blur_kernels(side):
    place = np.arange(side)
    distance = (place[:, None] - place[None, :]).astype(np.float32)
    taps = np.arange(-REACH, REACH + 1).astype(np.float32)
    tables = []
    for sigma in SIGMAS:
        scale = np.float32(2.0 * sigma * sigma)
        profile = np.where(np.abs(distance) <= REACH, np.exp(-distance * distance / scale), np.float32(0.0))
        tables.append(profile / np.sum(np.exp(-taps * taps / scale), dtype=np.float32))
    return np.concatenate(tables, axis=1).astype(jnp.bfloat16)


def keep_turned(value, off_c, wide_ref, first_row):
    rows, side = value.shape
    turned = pltpu.roll(value, off_c & (side - 1), 1)
    for h in range(2):
        lanes = turned[:, h * (side // 2) : (h + 1) * (side // 2)]
        wide_ref[h, first_row : first_row + rows] = lanes
        wide_ref[h, first_row + side : first_row + side + rows] = lanes


def table_of_tiles(patch_ref, off_ref, shape):
    lane = lax.broadcasted_iota(jnp.int32, shape, 1)
    row = lax.broadcasted_iota(jnp.int32, shape, 0)
    known = jnp.zeros(shape, jnp.int32)
    for t in range(patch_ref.shape[1]):
        mine = jnp.where(row == 0, patch_ref[0, t], jnp.where(row == 1, off_ref[0, t], off_ref[1, t]))
        known = jnp.where((lane == t) & (row < 3), mine, known)
    return known.astype(jnp.float32).astype(jnp.bfloat16)


def weight_body(patch_ref, off_ref, var_ref, out_ref, wide_ref):
    parts, group, height, side = out_ref.shape
    step = pl.program_id(0)
    half, swap = side // 2, height // 2
    chunk = 32

    @pl.when(step < pl.num_programs(0) - 1)
    def _():
        first = lax.broadcasted_iota(jnp.int32, (height, half), 0) < swap
        for t in range(group):
            tile = step * group + t
            off_r, off_c = off_ref[0, tile], off_ref[1, tile]
            for c in range(side // chunk):
                weight = 1.0 / var_ref[t, c * chunk : (c + 1) * chunk].astype(jnp.float32)
                keep_turned(weight, off_c, wide_ref.at[t], c * chunk)
            for part in range(parts):
                begins = [(4 * part - off_r) & (side - 1), (half + 4 * part - swap - off_r) & (side - 1)]
                for h in range(2):
                    rows = [wide_ref[t, h, pl.ds(begin, height)] for begin in begins]
                    out_ref[part, t, :, h * half : (h + 1) * half] = jnp.where(first, *rows).astype(jnp.bfloat16)

    @pl.when(step == pl.num_programs(0) - 1)
    def _():
        known = table_of_tiles(patch_ref, off_ref, (height, side))
        for part in range(parts):
            out_ref[part, 0] = known


def value_body(me_ref, patch_ref, off_ref, visit_ref, scale_ref, coef_ref, kernel_ref, image_ref, var_ref, *refs):
    outs, (blur_ref, wide_ref) = refs[:8], refs[8:]
    group, height, side = outs[0].shape
    step = pl.program_id(0)
    half, band = side // 2, height // 2
    chunk = 32

    @pl.when(step < pl.num_programs(0) - 1)
    def _():
        lane = lax.broadcasted_iota(jnp.int32, (chunk, half), 1)
        row = lax.broadcasted_iota(jnp.int32, (chunk, half), 0)
        xs = [(2.0 * (lane + h * half).astype(jnp.float32) + 1.0) / side - 1.0 for h in range(2)]
        for t in range(group):
            tile = step * group + t
            off_r, off_c = off_ref[0, tile], off_ref[1, tile]
            gain = scale_ref[visit_ref[tile]]
            k = [[coef_ref[6 * b + j, tile] for j in range(6)] for b in range(3)]
            square = [[k[b][5] * x for x in xs] for b in range(3)]
            row_pass = jnp.dot(image_ref[t], kernel_ref[...], preferred_element_type=jnp.float32).astype(jnp.bfloat16)
            for b in range(3):
                cols = slice(b * side, (b + 1) * side)
                blur_ref[t, b] = jnp.dot(kernel_ref[:, cols], row_pass[:, cols], preferred_element_type=jnp.float32)
            for c in range(side // chunk):
                rows = slice(c * chunk, (c + 1) * chunk)
                y = (2.0 * (row + c * chunk).astype(jnp.float32) + 1.0) / side - 1.0
                level = [k[b][0] + y * (k[b][1] + k[b][3] * y) for b in range(3)]
                slope = [k[b][2] + k[b][4] * y for b in range(3)]
                both = []
                for h in range(2):
                    cols = slice(h * half, (h + 1) * half)
                    matched = None
                    for b in range(3):
                        spatial = level[b] + xs[h] * (slope[b] + square[b][h])
                        term = spatial * blur_ref[t, b, rows, cols]
                        matched = term if matched is None else matched + term
                    both.append(gain * (1.0 / var_ref[t, rows, cols].astype(jnp.float32)) * matched)
                keep_turned(jnp.concatenate(both, axis=1), off_c, wide_ref.at[t], c * chunk)
            for m in range(8):
                member = (((me_ref[0] + (m & 3)) & 3) << 1) + (me_ref[1] ^ (m >> 2))
                for part in range(2):
                    begin = (part * half + (member << 4) - off_r) & (side - 1)
                    for h in range(2):
                        rows = wide_ref[t, h, pl.ds(begin, band)]
                        outs[m][t, part * band : (part + 1) * band, h * half : (h + 1) * half] = rows.astype(jnp.bfloat16)

    @pl.when(step == pl.num_programs(0) - 1)
    def _():
        known = table_of_tiles(patch_ref, off_ref, (height, side))
        for m in range(8):
            outs[m][0] = known


def sum_tiles(start_ref, order_ref, p, data_ref, row, lane, unroll):
    begin, end = start_ref[p], start_ref[p + 1]
    zero = jnp.zeros(row.shape, jnp.float32)

    def some_tiles(step, sums):
        sums = list(sums)
        for u in range(unroll):
            n = begin + step * unroll + u
            word = order_ref[jnp.minimum(n, end - 1)]
            there = jnp.where(n < end, 1.0, 0.0)
            tile, off_r, off_c = word & 2047, (word >> 11) & 511, word >> 20
            value = data_ref[tile].astype(jnp.float32) * there
            left = jnp.where(lane >= off_c, value, 0.0)
            right = value - left
            upper = row >= off_r
            sums[0] += jnp.where(upper, left, 0.0)
            sums[1] += jnp.where(upper, right, 0.0)
            sums[2] += jnp.where(upper, 0.0, left)
            sums[3] += jnp.where(upper, 0.0, right)
        return tuple(sums)

    return lax.fori_loop(0, (end - begin + unroll - 1) // unroll, some_tiles, (zero,) * 4)


def weight_sum_body(start_ref, order_ref, me_ref, data_ref, out_ref):
    height, side = data_ref.shape[-2:]
    s = lax.broadcasted_iota(jnp.int32, (height, side), 0)
    row = (s >> 2) * (side // 2) + 4 * me_ref[2] + (s & 3)
    lane = lax.broadcasted_iota(jnp.int32, (height, side), 1)
    swap = height // 2
    first = s < swap

    def one_patch(p, unused):
        sums = sum_tiles(start_ref, order_ref, p, data_ref, row, lane, 4)
        for half in range(2):
            left, right = sums[2 * half], sums[2 * half + 1]
            out_ref[2 * half, p] = jnp.where(first, left, pltpu.roll(right, swap, 0)).astype(jnp.bfloat16)
            out_ref[2 * half + 1, p] = jnp.where(first, pltpu.roll(left, swap, 0), right).astype(jnp.bfloat16)
        return unused

    lax.fori_loop(0, out_ref.shape[1], one_patch, 0)


def value_sum_body(start_ref, order_ref, me_ref, weight_ref, *refs):
    got, out_ref, (data_ref, sems) = refs[:8], refs[8], refs[9:]
    slots, height, side = got[0].shape
    copies = [pltpu.make_async_copy(got[m], data_ref.at[pl.ds(m * slots, slots)], sems.at[m]) for m in range(8)]
    for copy in copies:
        copy.start()
    s = lax.broadcasted_iota(jnp.int32, (height, side), 0)
    band = height // 2
    row = (s >> 4) * (side // 2) + (((me_ref[0] << 1) + me_ref[1]) << 4) + (s & 15)
    lane = lax.broadcasted_iota(jnp.int32, (height, side), 1)
    for copy in copies:
        copy.wait()

    def one_patch(p, unused):
        sums = sum_tiles(start_ref, order_ref, p, data_ref, row, lane, 2)
        for quarter in range(4):
            rows = slice((quarter & 1) * band, ((quarter & 1) + 1) * band)
            for h in range(2):
                part = sums[2 * (quarter >> 1) + h][rows]
                out_ref[quarter, p, h * band : (h + 1) * band] = part.astype(jnp.bfloat16)
            out_ref[quarter, p, height:] = weight_ref[quarter, p]
        return unused

    lax.fori_loop(0, out_ref.shape[1], one_patch, 0)


def final_body(got_ref, value_ref, weight_ref):
    epochs, parts, height, side = got_ref.shape
    band = 16
    for z in range(epochs):
        for core in range(2):
            rows = slice((2 * z + core) * band, (2 * z + core + 1) * band)
            for h in range(2):
                total = jnp.zeros((band, side), jnp.float32)
                for chip in range(parts // 2):
                    total += got_ref[z, 2 * chip + core, h * band : (h + 1) * band].astype(jnp.float32)
                value_ref[0, rows, h * side : (h + 1) * side] = total
    swap = 4
    first = lax.broadcasted_iota(jnp.int32, (8, side), 0) < swap
    for pair in range(parts // 2):
        both = []
        for part in (2 * pair, 2 * pair + 1):
            total = got_ref[0, part, 2 * band :].astype(jnp.float32)
            for e in range(1, epochs):
                total += got_ref[e, part, 2 * band :].astype(jnp.float32)
            both.append(total)
        rows = slice(pair * 8, (pair + 1) * 8)
        weight_ref[0, rows, :side] = jnp.where(first, both[0], pltpu.roll(both[1], swap, 0))
        weight_ref[0, rows, side:] = jnp.where(first, pltpu.roll(both[0], swap, 0), both[1])


def by_patch(known, slots, patches):
    known = known.astype(jnp.float32).astype(jnp.int32)
    sources, _, count = known.shape
    where = lax.broadcasted_iota(jnp.int32, (sources, count), 0) * slots + lax.broadcasted_iota(jnp.int32, (sources, count), 1)
    word = (where + (known[:, 1] << 11) + (known[:, 2] << 20)).reshape(-1)
    target = known[:, 0].reshape(-1)
    place = jnp.arange(sources * count, dtype=jnp.int32)
    ahead = (target[None, :] < target[:, None]) | ((target[None, :] == target[:, None]) & (place[None, :] < place[:, None]))
    rank = jnp.sum(ahead.astype(jnp.int32), axis=1)
    order = jnp.sum(jnp.where(rank[None, :] == place[:, None], word[None, :], 0), axis=1)
    start = jnp.sum((target[None, :] < jnp.arange(patches + 1, dtype=jnp.int32)[:, None]).astype(jnp.int32), axis=1)
    return start, order


def shards(tile_image, tile_var, psf_coef, tile_patch, tile_offset, tile_visit, visit_scale):
    count, side = tile_image.shape[:2]
    parts = lax.axis_size("patch")
    epochs = lax.axis_size("epoch")
    height = side // parts
    slots = count + 1
    z, j = lax.axis_index("epoch"), lax.axis_index("patch")
    me = jnp.stack([z, j & 1, j]).astype(jnp.int32)
    table = jnp.asarray(blur_kernels(side))

    smem = pl.BlockSpec(memory_space=pltpu.SMEM)
    vmem = pl.BlockSpec(memory_space=pltpu.VMEM)
    steps = count // GROUP
    tiles = pl.BlockSpec((GROUP, side, side), lambda g: (jnp.minimum(g, steps - 1), 0, 0))
    pixels = count * side * side
    weights = pl.pallas_call(
        weight_body,
        grid=(steps + 1,),
        in_specs=[smem, smem, tiles],
        out_specs=pl.BlockSpec((parts, GROUP, height, side), lambda g: (0, g, 0, 0)),
        out_shape=jax.ShapeDtypeStruct((parts, slots, height, side), jnp.bfloat16),
        scratch_shapes=[pltpu.VMEM((GROUP, 2, 2 * side, side // 2), jnp.float32)],
        cost_estimate=pl.CostEstimate(flops=20 * pixels, bytes_accessed=4 * pixels, transcendentals=0),
        name="weights",
    )(tile_patch.T, tile_offset.T, tile_var)
    tile_image, weights = lax.optimization_barrier((tile_image, weights))
    values = pl.pallas_call(
        value_body,
        grid=(steps + 1,),
        in_specs=[smem] * 6 + [pl.BlockSpec((side, 3 * side), lambda g: (0, 0)), tiles, tiles],
        out_specs=[pl.BlockSpec((GROUP, 32, side), lambda g: (g, 0, 0))] * 8,
        out_shape=[jax.ShapeDtypeStruct((slots, 32, side), jnp.bfloat16)] * 8,
        scratch_shapes=[
            pltpu.VMEM((GROUP, 3, side, side), jnp.float32),
            pltpu.VMEM((GROUP, 2, 2 * side, side // 2), jnp.float32),
        ],
        cost_estimate=pl.CostEstimate(flops=12 * pixels * side, bytes_accessed=6 * pixels, transcendentals=0),
        compiler_params=pltpu.CompilerParams(vmem_limit_bytes=60 << 20),
        name="values",
    )(me, tile_patch.T, tile_offset.T, tile_visit, visit_scale, psf_coef.T, table, tile_image, tile_var)

    def share(m, rows):
        turn, other = m & 3, m >> 2
        pairs = [
            (e * parts + d, ((e + turn) % epochs) * parts + (d ^ other)) for e in range(epochs) for d in range(parts)
        ]
        return lax.ppermute(rows, ("epoch", "patch"), pairs)

    got = [values[0]] + [share(m, values[m]) if m != 4 else None for m in range(1, 8)]
    got_weights = lax.all_to_all(weights, "patch", split_axis=0, concat_axis=0, tiled=True)
    got_weights, got[1], got[2] = lax.optimization_barrier((got_weights, got[1], got[2]))
    weight_sums = pl.pallas_call(
        weight_sum_body,
        in_specs=[smem, smem, smem, vmem],
        out_specs=vmem,
        out_shape=jax.ShapeDtypeStruct((4, parts, height, side), jnp.bfloat16),
        cost_estimate=pl.CostEstimate(flops=10 * pixels, bytes_accessed=3 * pixels, transcendentals=0),
        compiler_params=pltpu.CompilerParams(vmem_limit_bytes=60 << 20),
        name="weight_sums",
    )(*by_patch(got_weights[:, count, :3, :count], slots, parts), me, got_weights.reshape(parts * slots, height, side))

    core_share, weight_sums = lax.optimization_barrier((values[4], weight_sums))
    got[4] = share(4, core_share)
    known = jnp.stack([g[count, :3, :count] for g in got])
    hbm = pl.BlockSpec(memory_space=pl.ANY)
    sums = pl.pallas_call(
        value_sum_body,
        in_specs=[smem, smem, smem, vmem] + [hbm] * 8,
        out_specs=vmem,
        out_shape=jax.ShapeDtypeStruct((4, parts, 32 + height, side), jnp.bfloat16),
        scratch_shapes=[pltpu.VMEM((8 * slots, 32, side), jnp.bfloat16), pltpu.SemaphoreType.DMA((8,))],
        cost_estimate=pl.CostEstimate(flops=10 * pixels, bytes_accessed=4 * pixels, transcendentals=0),
        compiler_params=pltpu.CompilerParams(vmem_limit_bytes=56 << 20),
        name="value_sums",
    )(*by_patch(known, slots, parts), me, weight_sums, *got)

    sums = sums.reshape(epochs * parts, 32 + height, side)
    got = lax.all_to_all(sums, ("epoch", "patch"), split_axis=0, concat_axis=0, tiled=True)
    quarter = jax.ShapeDtypeStruct((1, 4 * parts, 2 * side), jnp.float32)
    return pl.pallas_call(
        final_body,
        in_specs=[vmem],
        out_specs=(vmem, vmem),
        out_shape=(quarter, quarter),
        compiler_params=pltpu.CompilerParams(vmem_limit_bytes=32 << 20),
        name="final",
    )(got.reshape(epochs, parts, 32 + height, side))


def solution(mesh):
    placed = (
        P(("epoch", "patch"), None, None),
        P(("epoch", "patch"), None, None),
        P(("epoch", "patch"), None),
        P(("epoch", "patch"), None),
        P(("epoch", "patch"), None),
        P(("epoch", "patch")),
        P(),
    )
    return jax.shard_map(
        shards,
        mesh=mesh,
        in_specs=placed,
        out_specs=(P("patch", "epoch", None), P("patch", "epoch", None)),
        check_vma=False,
    )
```

time: 179 us -> 150 us (0.84)
  waiting for transfers between devices: 64.8 us -> 26.1 us
  blocking collectives: 28.8 us -> 45.8 us
  local copies, waits for them, and re-layouts: 7.11 us -> 1.35 us
  other arithmetic: 2.33 us -> 6 us
  starting transfers between devices: 23.3 us -> 19.7 us
  Pallas kernels: 51.6 us -> 49.5 us
    all_to_all x3 -> x1, waiting for transfers between devices: 64.8 us -> 5.98 us  [shards(): lax.all_to_all(weights, 'patch', split_axis=0, concat_axis=0, tiled=True)]
    ppermute x0 -> x7, waiting for transfers between devices: none -> 20.2 us  [share(): return lax.ppermute(rows, ('epoch', 'patch'), pairs)]
    all_to_all x1, blocking collectives: 28.8 us -> 45.8 us  [shards(): lax.all_to_all(sums, ('epoch', 'patch'), split_axis=0, concat_axis=0, til...]
    all_to_all x3 -> x1, starting transfers between devices: 23.3 us -> 8.64 us  [shards(): lax.all_to_all(weights, 'patch', split_axis=0, concat_axis=0, tiled=True)]
    ppermute x0 -> x7, starting transfers between devices: none -> 11.1 us  [share(): return lax.ppermute(rows, ('epoch', 'patch'), pairs)]
    unnamed x16 -> x23, local copies, waits for them, and re-layouts: 6.35 us -> 0.74 us
    reduce_sum x3 -> x6, other arithmetic: 1.47 us -> 4.14 us  [the longest x2 1.79 us: by_patch(): jnp.sum(jnp.where(rank[None, :] == place[:, None], word[None, :], 0), axi...]
  transfers between devices with their start and end apart: 3 -> 8, of which waited for: 2 -> 5; matrix products, arithmetic and copies ran while one was open for 1% -> 4% of each run, Pallas kernels for 22% -> 19%
where the time goes in v2:
time: 150 us; the launch traced here: 149 us
  Pallas kernels  49.5 us (33%)
  blocking collectives  45.8 us (31%)
  waiting for transfers between devices  26.1 us (17%)
  starting transfers between devices  19.7 us (13%)
  other arithmetic  6 us (4%)
    all_to_all x1, blocking collectives, shards(): lax.all_to_all(sums, ('epoch', 'patch'), split_axis=0, concat_axis=0, til...  45.8 us
    ppermute x7, waiting for transfers between devices, share(): return lax.ppermute(rows, ('epoch', 'patch'), pairs)  20.2 us
    pallas_call x1, Pallas kernels, shards(): pl.pallas_call(value_body, grid=(steps + 1,), in_specs=[smem] * 6 + [pl.B...  18.1 us
    pallas_call x1, Pallas kernels, shards(): pl.pallas_call(value_sum_body, in_specs=[smem, smem, smem, vmem] + [hbm]...  11.1 us
    ppermute x7, starting transfers between devices, share(): return lax.ppermute(rows, ('epoch', 'patch'), pairs)  11.1 us
    pallas_call x1, Pallas kernels, shards(): pl.pallas_call(weight_sum_body, in_specs=[smem, smem, smem, vmem], out_sp...  10.5 us
    pallas_call x1, Pallas kernels, shards(): pl.pallas_call(weight_body, grid=(steps + 1,), in_specs=[smem, smem, tile...  8.77 us
    all_to_all x1, starting transfers between devices, shards(): lax.all_to_all(weights, 'patch', split_axis=0, concat_axis=0, tiled=True)  8.64 us
  transfers between devices with their start and end apart: 8, of which 5 were waited for; matrix products, arithmetic and copies ran while one was open for 4% of the time, Pallas kernels for 19%

profile of v2, /device:TPU:1, one launch (start us, length us, event | category | flops | bytes accessed | tf_op | source)
XLA Modules:
  0.0 149.3 jit_solution(13411395142236686586)
XLA Ops:
  0.6 8.8 %weights.1 = bf16[32,33,8,256]{3,2,1,0:T(8,128)(2,1)} custom-call(s32[1,32]{1,0:T(1,128)} %bitcast.15, s32[2,32]{1,0:T(2,128)} %bitcast.13, bf16[32,256,256]{2,1,0:T(8,128)(2,1)} %var_ref.3), custom_call_target="tpu_custom_call" | custom-call | flops 41943040 | bytes 8388608 | tf_op jit(solution)/shard_map/weights/pallas_call | solution.py:248
  9.4 8.6 %all-to-all-start = ((bf16[32,33,8,256]{3,2,1,0:T(8,128)(2,1)}), bf16[32,33,8,256]{3,2,1,0:T(8,128)(2,1)}, u32[]{:S(2)}, u32[]{:S(2)}) async-start(bf16[32,33,8,256]{3,2,1,0:T(8,128)(2,1)} %weights.1), calls=%async_computation | async-start | bytes 8650752 | tf_op jit(solution)/shard_map/all_to_all | solution.py:282
  18.0 0.6 pad_add_fusion.me_ref
  18.7 18.1 %values.1 = (bf16[33,32,256]{2,1,0:T(8,128)(2,1)}, bf16[33,32,256]{2,1,0:T(8,128)(2,1)}, bf16[33,32,256]{2,1,0:T(8,128)(2,1)}, bf16[33,32,256]{2,1,0:T(8,128)(2,...) custom-call(s32[3]{0:T(128)} %pad_add_fusion.me_ref, ...), custom_call_target="tpu_custom_call" | custom-call | flops 6442450944 | bytes 12582912 | tf_op jit(solution)/shard_map/values/pallas_call | solution.py:259
  36.8 1.7 %collective-permute-start = (bf16[33,32,256]{2,1,0:T(8,128)(2,1)}, bf16[33,32,256]{2,1,0:T(8,128)(2,1)S(1)}, u32[]{:S(2)}, u32[]{:S(2)}) collective-permute-start(bf16[33,32,256]{2,1,0:T(8,128)(2,1)} %get-tuple-element.20), channel_id=1, source_target_pairs={{0,32},{1,33},{2,34},{3,35},{4,36},{5,37},{6,38},{7,39},{8,40},{9,... | collective-permute-start | bytes 1622024 | tf_op jit(solution)/shard_map/ppermute | solution.py:279
  38.5 3.3 %collective-permute-start.1 = (bf16[33,32,256]{2,1,0:T(8,128)(2,1)}, bf16[33,32,256]{2,1,0:T(8,128)(2,1)S(1)}, u32[]{:S(2)}, u32[]{:S(2)}) collective-permute-start(bf16[33,32,256]{2,1,0:T(8,128)(2,1)} %get-tuple-element.21), channel_id=1, source_target_pairs={{0,64},{1,65},{2,66},{3,67},{4,68},{5,69},{6,70},{7,71},{8,72},{9,... | collective-permute-start | bytes 1622024 | tf_op jit(solution)/shard_map/ppermute | solution.py:279
  41.8 0.7 collective-permute-start.2
  42.5 1.8 %collective-permute-start.4 = (bf16[33,32,256]{2,1,0:T(8,128)(2,1)}, bf16[33,32,256]{2,1,0:T(8,128)(2,1)S(1)}, u32[]{:S(2)}, u32[]{:S(2)}) collective-permute-start(bf16[33,32,256]{2,1,0:T(8,128)(2,1)} %get-tuple-element.28), channel_id=1, source_target_pairs={{0,33},{1,32},{2,35},{3,34},{4,37},{5,36},{6,39},{7,38},{8,41},{9,... | collective-permute-start | bytes 1622024 | tf_op jit(solution)/shard_map/ppermute | solution.py:279
  44.3 0.0 collective-permute-start.5
  44.3 0.1 iota_add_fusion.1
  44.4 0.1 add.53
  44.4 0.1 iota_add_fusion
  44.5 0.1 add.49
  44.6 0.7 constant_dynamic-update-slice_fusion.7
  45.2 8.1 %collective-permute-done.refs_1_ = bf16[33,32,256]{2,1,0:T(8,128)(2,1)S(1)} collective-permute-done((bf16[33,32,256]{2,1,0:T(8,128)(2,1)}, bf16[33,32,256]{2,1,0:T(8,128)(2,1)S(1)}, u32[]{:S(2)}, u32[]{:S(2)}) %collective-permute-start) | collective-permute-done | bytes 540704 | tf_op jit(solution)/shard_map/ppermute | solution.py:279
  53.4 0.0 copy-start
  53.4 2.7 %collective-permute-start.6 = (bf16[33,32,256]{2,1,0:T(8,128)(2,1)}, bf16[33,32,256]{2,1,0:T(8,128)(2,1)S(1)}, u32[]{:S(2)}, u32[]{:S(2)}) collective-permute-start(bf16[33,32,256]{2,1,0:T(8,128)(2,1)} %get-tuple-element.30), channel_id=1, source_target_pairs={{0,97},{1,96},{2,99},{3,98},{4,101},{5,100},{6,103},{7,102},{8,105... | collective-permute-start | bytes 1622024 | tf_op jit(solution)/shard_map/ppermute | solution.py:279
  56.1 9.8 %collective-permute-done.1.refs_2_ = bf16[33,32,256]{2,1,0:T(8,128)(2,1)S(1)} collective-permute-done((bf16[33,32,256]{2,1,0:T(8,128)(2,1)}, bf16[33,32,256]{2,1,0:T(8,128)(2,1)S(1)}, u32[]{:S(2)}, u32[]{:S(2)}) %collective-permute-start.1) | collective-permute-done | bytes 540704 | tf_op jit(solution)/shard_map/ppermute | solution.py:279
  65.8 0.0 copy-start.1
  65.9 6.0 %all-to-all-done = bf16[32,33,8,256]{3,2,1,0:T(8,128)(2,1)} async-done(((bf16[32,33,8,256]{3,2,1,0:T(8,128)(2,1)}), bf16[32,33,8,256]{3,2,1,0:T(8,128)(2,1)}, u32[]{:S(2)}, u32[]{:S(2)}) %all-to-all-start) | async-done | bytes 4325408 | tf_op jit(solution)/shard_map/all_to_all | solution.py:282
  71.8 0.9 convert_bitcast_fusion
  72.7 0.1 fusion.5
  72.8 0.1 shift_left.54
  72.9 0.1 lt.86
  73.0 0.8 convert_reduce_fusion
  73.8 0.1 shift_left.57
  73.9 0.0 copy-start.7
  73.9 1.1 select_reduce_fusion.order_ref
  75.0 0.6 convert_reduce_fusion.2.start_ref
  75.6 10.5 %weight_sums.1.weight_ref = bf16[4,32,8,256]{3,2,1,0:T(8,128)(2,1)} custom-call(s32[33]{0:T(128)} %convert_reduce_fusion.2.start_ref, s32[1024]{0:T(1024)} %select_reduce_fusion.order_ref, s32[3]{0:T(128)} %pad_add_fusion.me_ref, bf16[1056,8,256]{2,1,0:T(8,128)(2,1)} %bitcast.7.data_ref), custom_call_target="tpu_custom_call" | custom-call | flops 20971520 | bytes 6291456 | tf_op jit(solution)/shard_map/weight_sums/pallas_call | solution.py:284
  86.1 0.0 copy-done.7
  86.1 0.8 collective-permute-start.3
  87.0 0.0 collective-permute-done.2.refs_3_
  87.0 0.0 copy-start.2
  87.0 1.5 %collective-permute-done.3.refs_4_ = bf16[33,32,256]{2,1,0:T(8,128)(2,1)S(1)} collective-permute-done((bf16[33,32,256]{2,1,0:T(8,128)(2,1)S(1)}, bf16[33,32,256]{2,1,0:T(8,128)(2,1)S(1)}, u32[]{:S(2)}, u32[]{:S(2)}) %collective-permute-start.3) | collective-permute-done | bytes 540704 | tf_op jit(solution)/shard_map/ppermute | solution.py:279
  88.5 0.0 copy-start.6
  88.5 0.0 collective-permute-done.4.refs_5_
  88.5 0.0 copy-start.3
  88.6 0.8 collective-permute-done.5.refs_6_
  89.3 0.0 copy-start.4
  89.3 0.0 collective-permute-done.6.refs_7_
  89.3 0.0 copy-done.6
  89.4 0.0 copy-start.5
  89.4 0.1 lt.97
  89.5 0.7 convert_reduce_fusion.3.start_ref
  90.2 0.2 convert_reduce_fusion.1
  90.4 0.1 shift_left.60
  90.5 0.1 shift_left.63
  90.5 0.7 select_reduce_fusion.1.order_ref
  91.2 0.0 copy-done
  91.2 0.0 copy-done.1
  91.2 0.0 copy-done.2
  91.2 0.0 copy-done.3
  91.3 0.0 copy-done.4
  91.3 0.0 copy-done.5
  91.3 11.1 %value_sums.1 = bf16[4,32,40,256]{3,2,1,0:T(8,128)(2,1)} custom-call(s32[33]{0:T(128)} %convert_reduce_fusion.3.start_ref, s32[256]{0:T(256)} %select_reduce_fusion.1.order_ref, s32[3]{0:T(128)} %pad_add_fusion.me_ref, bf16[4,32,8,256]{3,2,1,0:T(8,128)(2,1)} %weight_sums.1.weight_ref, bf16[33,32,256]{2,1,0:T(8,128)(2,1)} %get-tuple-element.18.refs_0_, ...), custom_call_target="tpu_custom_call" | custom-call | flops 20971520 | bytes 8388608 | tf_op jit(solution)/shard_map/value_sums/pallas_call | solution.py:298
  102.4 45.8 %all_to_all.10 = bf16[128,40,256]{2,1,0:T(8,128)(2,1)S(1)} all-to-all(bf16[128,40,256]{2,1,0:T(8,128)(2,1)} %bitcast.12), channel_id=1, replica_groups=mesh['epoch'=4,'patch'=32] {'epoch','patch'}, dimensions={0} | all-to-all | bytes 5242880 | tf_op jit(solution)/shard_map/all_to_all | solution.py:310
  148.2 1.1 final.1
  (13 shorter events, 0.1 us)
Async XLA Ops:
  9.4 62.4 %all-to-all-start = ((bf16[32,33,8,256]{3,2,1,0:T(8,128)(2,1)}), bf16[32,33,8,256]{3,2,1,0:T(8,128)(2,1)}, u32[]{:S(2)}, u32[]{:S(2)}) async-start(bf16[32,33,8,256]{3,2,1,0:T(8,128)(2,1)} %weights.1), calls=%async_computation | async-start | bytes 8650752 | tf_op jit(solution)/shard_map/all_to_all | solution.py:282
  36.8 16.6 %collective-permute-start = (bf16[33,32,256]{2,1,0:T(8,128)(2,1)}, bf16[33,32,256]{2,1,0:T(8,128)(2,1)S(1)}, u32[]{:S(2)}, u32[]{:S(2)}) collective-permute-start(bf16[33,32,256]{2,1,0:T(8,128)(2,1)} %get-tuple-element.20), channel_id=1, source_target_pairs={{0,32},{1,33},{2,34},{3,35},{4,36},{5,37},{6,38},{7,39},{8,40},{9,... | collective-permute-start | bytes 1622024 | tf_op jit(solution)/shard_map/ppermute | solution.py:279
  38.5 27.4 %collective-permute-start.1 = (bf16[33,32,256]{2,1,0:T(8,128)(2,1)}, bf16[33,32,256]{2,1,0:T(8,128)(2,1)S(1)}, u32[]{:S(2)}, u32[]{:S(2)}) collective-permute-start(bf16[33,32,256]{2,1,0:T(8,128)(2,1)} %get-tuple-element.21), channel_id=1, source_target_pairs={{0,64},{1,65},{2,66},{3,67},{4,68},{5,69},{6,70},{7,71},{8,72},{9,... | collective-permute-start | bytes 1622024 | tf_op jit(solution)/shard_map/ppermute | solution.py:279
  41.8 45.2 %collective-permute-start.2 = (bf16[33,32,256]{2,1,0:T(8,128)(2,1)}, bf16[33,32,256]{2,1,0:T(8,128)(2,1)S(1)}, u32[]{:S(2)}, u32[]{:S(2)}) collective-permute-start(bf16[33,32,256]{2,1,0:T(8,128)(2,1)} %get-tuple-element.24), channel_id=1, source_target_pairs={{0,96},{1,97},{2,98},{3,99},{4,100},{5,101},{6,102},{7,103},{8,104... | collective-permute-start | bytes 1622024 | tf_op jit(solution)/shard_map/ppermute | solution.py:279
  42.5 46.0 %collective-permute-start.4 = (bf16[33,32,256]{2,1,0:T(8,128)(2,1)}, bf16[33,32,256]{2,1,0:T(8,128)(2,1)S(1)}, u32[]{:S(2)}, u32[]{:S(2)}) collective-permute-start(bf16[33,32,256]{2,1,0:T(8,128)(2,1)} %get-tuple-element.28), channel_id=1, source_target_pairs={{0,33},{1,32},{2,35},{3,34},{4,37},{5,36},{6,39},{7,38},{8,41},{9,... | collective-permute-start | bytes 1622024 | tf_op jit(solution)/shard_map/ppermute | solution.py:279
  44.3 45.1 %collective-permute-start.5 = (bf16[33,32,256]{2,1,0:T(8,128)(2,1)}, bf16[33,32,256]{2,1,0:T(8,128)(2,1)S(1)}, u32[]{:S(2)}, u32[]{:S(2)}) collective-permute-start(bf16[33,32,256]{2,1,0:T(8,128)(2,1)} %get-tuple-element.29), channel_id=1, source_target_pairs={{0,65},{1,64},{2,67},{3,66},{4,69},{5,68},{6,71},{7,70},{8,73},{9,... | collective-permute-start | bytes 1622024 | tf_op jit(solution)/shard_map/ppermute | solution.py:279
  53.4 37.9 %copy-start = (bf16[33,32,256]{2,1,0:T(8,128)(2,1)}, bf16[33,32,256]{2,1,0:T(8,128)(2,1)S(1)}, u32[]{:S(2)}) copy-start(bf16[33,32,256]{2,1,0:T(8,128)(2,1)S(1)} %collective-permute-done.refs_1_) | copy-start | bytes 1622020
  53.4 36.0 %collective-permute-start.6 = (bf16[33,32,256]{2,1,0:T(8,128)(2,1)}, bf16[33,32,256]{2,1,0:T(8,128)(2,1)S(1)}, u32[]{:S(2)}, u32[]{:S(2)}) collective-permute-start(bf16[33,32,256]{2,1,0:T(8,128)(2,1)} %get-tuple-element.30), channel_id=1, source_target_pairs={{0,97},{1,96},{2,99},{3,98},{4,101},{5,100},{6,103},{7,102},{8,105... | collective-permute-start | bytes 1622024 | tf_op jit(solution)/shard_map/ppermute | solution.py:279
  65.8 25.4 %copy-start.1 = (bf16[33,32,256]{2,1,0:T(8,128)(2,1)}, bf16[33,32,256]{2,1,0:T(8,128)(2,1)S(1)}, u32[]{:S(2)}) copy-start(bf16[33,32,256]{2,1,0:T(8,128)(2,1)S(1)} %collective-permute-done.1.refs_2_) | copy-start | bytes 1622020
  73.9 12.2 %copy-start.7 = (bf16[33,32,256]{2,1,0:T(8,128)(2,1)S(1)}, bf16[33,32,256]{2,1,0:T(8,128)(2,1)}, u32[]{:S(2)}) copy-start(bf16[33,32,256]{2,1,0:T(8,128)(2,1)} %get-tuple-element.27) | copy-start | bytes 1622020
  86.1 2.4 %collective-permute-start.3 = (bf16[33,32,256]{2,1,0:T(8,128)(2,1)S(1)}, bf16[33,32,256]{2,1,0:T(8,128)(2,1)S(1)}, u32[]{:S(2)}, u32[]{:S(2)}) collective-permute-start(bf16[33,32,256]{2,1,0:T(8,128)(2,1)S(1)} %copy-done.7), channel_id=1, source_target_pairs={{0,1},{1,0},{2,3},{3,2},{4,5},{5,4},{6,7},{7,6},{8,9},{9,8},{10,11... | collective-permute-start | bytes 1622024 | tf_op jit(solution)/shard_map/ppermute | solution.py:279
  87.0 4.3 %copy-start.2 = (bf16[33,32,256]{2,1,0:T(8,128)(2,1)}, bf16[33,32,256]{2,1,0:T(8,128)(2,1)S(1)}, u32[]{:S(2)}) copy-start(bf16[33,32,256]{2,1,0:T(8,128)(2,1)S(1)} %collective-permute-done.2.refs_3_) | copy-start | bytes 1622020
  88.5 0.8 copy-start.6
  88.5 2.7 %copy-start.3 = (bf16[33,32,256]{2,1,0:T(8,128)(2,1)}, bf16[33,32,256]{2,1,0:T(8,128)(2,1)S(1)}, u32[]{:S(2)}) copy-start(bf16[33,32,256]{2,1,0:T(8,128)(2,1)S(1)} %collective-permute-done.4.refs_5_) | copy-start | bytes 1622020
  89.3 1.9 %copy-start.4 = (bf16[33,32,256]{2,1,0:T(8,128)(2,1)}, bf16[33,32,256]{2,1,0:T(8,128)(2,1)S(1)}, u32[]{:S(2)}) copy-start(bf16[33,32,256]{2,1,0:T(8,128)(2,1)S(1)} %collective-permute-done.5.refs_6_) | copy-start | bytes 1622020
  89.4 1.9 %copy-start.5 = (bf16[33,32,256]{2,1,0:T(8,128)(2,1)}, bf16[33,32,256]{2,1,0:T(8,128)(2,1)S(1)}, u32[]{:S(2)}) copy-start(bf16[33,32,256]{2,1,0:T(8,128)(2,1)S(1)} %collective-permute-done.6.refs_7_) | copy-start | bytes 1622020

commit v3 on v2

--- a/solution.py
+++ b/solution.py
@@ -1,3 +1,5 @@
+import functools
+
 import jax
 import jax.numpy as jnp
 import numpy as np
@@ -9,6 +11,8 @@
 SIGMAS = (1.0, 2.0, 3.5)
 REACH = 7
 GROUP = 4
+WEIGHT_GROUP = 8
+FIRST = 12
 
 
 def blur_kernels(side):
@@ -70,20 +74,20 @@
             out_ref[part, 0] = known
 
 
-def value_body(me_ref, patch_ref, off_ref, visit_ref, scale_ref, coef_ref, kernel_ref, image_ref, var_ref, *refs):
+def value_body(begin, tables, me_ref, patch_ref, off_ref, visit_ref, scale_ref, coef_ref, kernel_ref, image_ref, var_ref, *refs):
     outs, (blur_ref, wide_ref) = refs[:8], refs[8:]
     group, height, side = outs[0].shape
     step = pl.program_id(0)
     half, band = side // 2, height // 2
     chunk = 32
 
-    @pl.when(step < pl.num_programs(0) - 1)
+    @pl.when(step < pl.num_programs(0) - tables)
     def _():
         lane = lax.broadcasted_iota(jnp.int32, (chunk, half), 1)
         row = lax.broadcasted_iota(jnp.int32, (chunk, half), 0)
         xs = [(2.0 * (lane + h * half).astype(jnp.float32) + 1.0) / side - 1.0 for h in range(2)]
         for t in range(group):
-            tile = step * group + t
+            tile = begin + step * group + t
             off_r, off_c = off_ref[0, tile], off_ref[1, tile]
             gain = scale_ref[visit_ref[tile]]
             k = [[coef_ref[6 * b + j, tile] for j in range(6)] for b in range(3)]
@@ -110,82 +114,134 @@
             for m in range(8):
                 member = (((me_ref[0] + (m & 3)) & 3) << 1) + (me_ref[1] ^ (m >> 2))
                 for part in range(2):
-                    begin = (part * half + (member << 4) - off_r) & (side - 1)
+                    top = (part * half + (member << 4) - off_r) & (side - 1)
                     for h in range(2):
-                        rows = wide_ref[t, h, pl.ds(begin, band)]
+                        rows = wide_ref[t, h, pl.ds(top, band)]
                         outs[m][t, part * band : (part + 1) * band, h * half : (h + 1) * half] = rows.astype(jnp.bfloat16)
 
-    @pl.when(step == pl.num_programs(0) - 1)
-    def _():
-        known = table_of_tiles(patch_ref, off_ref, (height, side))
-        for m in range(8):
-            outs[m][0] = known
-
-
-def sum_tiles(start_ref, order_ref, p, data_ref, row, lane, unroll):
-    begin, end = start_ref[p], start_ref[p + 1]
-    zero = jnp.zeros(row.shape, jnp.float32)
-
-    def some_tiles(step, sums):
-        sums = list(sums)
-        for u in range(unroll):
-            n = begin + step * unroll + u
-            word = order_ref[jnp.minimum(n, end - 1)]
-            there = jnp.where(n < end, 1.0, 0.0)
-            tile, off_r, off_c = word & 2047, (word >> 11) & 511, word >> 20
-            value = data_ref[tile].astype(jnp.float32) * there
-            left = jnp.where(lane >= off_c, value, 0.0)
-            right = value - left
-            upper = row >= off_r
-            sums[0] += jnp.where(upper, left, 0.0)
-            sums[1] += jnp.where(upper, right, 0.0)
-            sums[2] += jnp.where(upper, 0.0, left)
-            sums[3] += jnp.where(upper, 0.0, right)
-        return tuple(sums)
-
-    return lax.fori_loop(0, (end - begin + unroll - 1) // unroll, some_tiles, (zero,) * 4)
-
-
-def weight_sum_body(start_ref, order_ref, me_ref, data_ref, out_ref):
-    height, side = data_ref.shape[-2:]
+    if tables:
+
+        @pl.when(step == pl.num_programs(0) - 1)
+        def _():
+            known = table_of_tiles(patch_ref, off_ref, (height, side))
+            for m in range(8):
+                outs[m][0] = known
+
+
+def clear_sums(sums_ref):
+    zero = jnp.zeros(sums_ref.shape[1:], jnp.float32)
+
+    def clear(p, unused):
+        sums_ref[p] = zero
+        return unused
+
+    lax.fori_loop(0, sums_ref.shape[0], clear, 0)
+
+
+def weight_sum_body(known_ref, me_ref, got_ref, out_ref, data_ref, sems, *sums_refs):
+    sources, slots, height, side = got_ref.shape
+    tiles, patches = slots - 1, out_ref.shape[1]
+    bunch = sources // sems.shape[0]
+    copies = [
+        pltpu.make_async_copy(got_ref.at[pl.ds(n * bunch, bunch)], data_ref.at[pl.ds(n * bunch, bunch)], sems.at[n])
+        for n in range(sems.shape[0])
+    ]
+    for copy in copies:
+        copy.start()
     s = lax.broadcasted_iota(jnp.int32, (height, side), 0)
     row = (s >> 2) * (side // 2) + 4 * me_ref[2] + (s & 3)
     lane = lax.broadcasted_iota(jnp.int32, (height, side), 1)
     swap = height // 2
     first = s < swap
+    for sums_ref in sums_refs:
+        clear_sums(sums_ref)
+
+    def add_source(source, unused):
+        for t in range(tiles):
+            p, off_r, off_c = known_ref[source, 0, t], known_ref[source, 1, t], known_ref[source, 2, t]
+            sums_ref = sums_refs[t % len(sums_refs)]
+            value = data_ref[source, t].astype(jnp.float32)
+            left = jnp.where(lane >= off_c, value, 0.0)
+            right = value - left
+            upper = row >= off_r
+            upper_left, upper_right = jnp.where(upper, left, 0.0), jnp.where(upper, right, 0.0)
+            sums_ref[p, 0] += upper_left
+            sums_ref[p, 1] += upper_right
+            sums_ref[p, 2] += left - upper_left
+            sums_ref[p, 3] += right - upper_right
+        return unused
+
+    for n, copy in enumerate(copies):
+        copy.wait()
+        lax.fori_loop(n * bunch, (n + 1) * bunch, add_source, 0)
 
     def one_patch(p, unused):
-        sums = sum_tiles(start_ref, order_ref, p, data_ref, row, lane, 4)
         for half in range(2):
-            left, right = sums[2 * half], sums[2 * half + 1]
+            left, right = (sum(sums_ref[p, 2 * half + h] for sums_ref in sums_refs) for h in range(2))
             out_ref[2 * half, p] = jnp.where(first, left, pltpu.roll(right, swap, 0)).astype(jnp.bfloat16)
             out_ref[2 * half + 1, p] = jnp.where(first, pltpu.roll(left, swap, 0), right).astype(jnp.bfloat16)
         return unused
 
-    lax.fori_loop(0, out_ref.shape[1], one_patch, 0)
-
-
-def value_sum_body(start_ref, order_ref, me_ref, weight_ref, *refs):
+    lax.fori_loop(0, patches, one_patch, 0)
+
+
+def add_values(known_ref, me_ref, begin, tiles, copies, data_ref, sums_ref):
+    _, _, height, side = data_ref.shape
+    band = height // 2
+    s = lax.broadcasted_iota(jnp.int32, (band, side), 0) + (((me_ref[0] << 1) + me_ref[1]) << 4)
+    lane = lax.broadcasted_iota(jnp.int32, (band, side), 1)
+
+    for m, copy in enumerate(copies):
+        copy.wait()
+
+        def some_tiles(step, unused):
+            for u in range(4):
+                t = 4 * step + u
+                p, off_r, off_c = (known_ref[m, n, begin + t] for n in range(3))
+                for part in range(2):
+                    value = data_ref[m, t, part * band : (part + 1) * band].astype(jnp.float32)
+                    left = jnp.where(lane >= off_c, value, 0.0)
+                    right = value - left
+                    upper = s >= off_r - part * (side // 2)
+                    upper_left, upper_right = jnp.where(upper, left, 0.0), jnp.where(upper, right, 0.0)
+                    sums_ref[p, part, 0] += upper_left
+                    sums_ref[p, part, 1] += upper_right
+                    sums_ref[p, 2 + part, 0] += left - upper_left
+                    sums_ref[p, 2 + part, 1] += right - upper_right
+            return unused
+
+        lax.fori_loop(0, tiles // 4, some_tiles, 0)
+
+
+def first_values_body(known_ref, me_ref, *refs):
     got, out_ref, (data_ref, sems) = refs[:8], refs[8], refs[9:]
-    slots, height, side = got[0].shape
-    copies = [pltpu.make_async_copy(got[m], data_ref.at[pl.ds(m * slots, slots)], sems.at[m]) for m in range(8)]
+    tiles = got[0].shape[0] - 1
+    copies = [pltpu.make_async_copy(got[m].at[pl.ds(0, tiles)], data_ref.at[m], sems.at[m]) for m in range(8)]
     for copy in copies:
         copy.start()
-    s = lax.broadcasted_iota(jnp.int32, (height, side), 0)
-    band = height // 2
-    row = (s >> 4) * (side // 2) + (((me_ref[0] << 1) + me_ref[1]) << 4) + (s & 15)
-    lane = lax.broadcasted_iota(jnp.int32, (height, side), 1)
+    clear_sums(out_ref)
+    add_values(known_ref, me_ref, 0, tiles, copies, data_ref, out_ref)
+
+
+def last_values_body(known_ref, me_ref, weight_ref, before_ref, *refs):
+    got, out_ref, (data_ref, first_ref, sums_ref, sems, first_sem) = refs[:8], refs[8], refs[9:]
+    tiles = got[0].shape[0]
+    band = sums_ref.shape[3]
+    copies = [pltpu.make_async_copy(got[m], data_ref.at[m], sems.at[m]) for m in range(8)]
     for copy in copies:
-        copy.wait()
+        copy.start()
+    earlier = pltpu.make_async_copy(before_ref, first_ref, first_sem)
+    earlier.start()
+    clear_sums(sums_ref)
+    add_values(known_ref, me_ref, known_ref.shape[2] - tiles, tiles, copies, data_ref, sums_ref)
+    earlier.wait()
 
     def one_patch(p, unused):
-        sums = sum_tiles(start_ref, order_ref, p, data_ref, row, lane, 2)
         for quarter in range(4):
-            rows = slice((quarter & 1) * band, ((quarter & 1) + 1) * band)
             for h in range(2):
-                part = sums[2 * (quarter >> 1) + h][rows]
-                out_ref[quarter, p, h * band : (h + 1) * band] = part.astype(jnp.bfloat16)
-            out_ref[quarter, p, height:] = weight_ref[quarter, p]
+                both = sums_ref[p, quarter, h] + first_ref[p, quarter, h]
+                out_ref[quarter, p, h * band : (h + 1) * band] = both.astype(jnp.bfloat16)
+            out_ref[quarter, p, 2 * band :] = weight_ref[quarter, p]
         return unused
 
     lax.fori_loop(0, out_ref.shape[1], one_patch, 0)
@@ -216,20 +272,6 @@
         weight_ref[0, rows, side:] = jnp.where(first, pltpu.roll(both[0], swap, 0), both[1])
 
 
-def by_patch(known, slots, patches):
-    known = known.astype(jnp.float32).astype(jnp.int32)
-    sources, _, count = known.shape
-    where = lax.broadcasted_iota(jnp.int32, (sources, count), 0) * slots + lax.broadcasted_iota(jnp.int32, (sources, count), 1)
-    word = (where + (known[:, 1] << 11) + (known[:, 2] << 20)).reshape(-1)
-    target = known[:, 0].reshape(-1)
-    place = jnp.arange(sources * count, dtype=jnp.int32)
-    ahead = (target[None, :] < target[:, None]) | ((target[None, :] == target[:, None]) & (place[None, :] < place[:, None]))
-    rank = jnp.sum(ahead.astype(jnp.int32), axis=1)
-    order = jnp.sum(jnp.where(rank[None, :] == place[:, None], word[None, :], 0), axis=1)
-    start = jnp.sum((target[None, :] < jnp.arange(patches + 1, dtype=jnp.int32)[:, None]).astype(jnp.int32), axis=1)
-    return start, order
-
-
 def shards(tile_image, tile_var, psf_coef, tile_patch, tile_offset, tile_visit, visit_scale):
     count, side = tile_image.shape[:2]
     parts = lax.axis_size("patch")
@@ -242,34 +284,37 @@
 
     smem = pl.BlockSpec(memory_space=pltpu.SMEM)
     vmem = pl.BlockSpec(memory_space=pltpu.VMEM)
-    steps = count // GROUP
-    tiles = pl.BlockSpec((GROUP, side, side), lambda g: (jnp.minimum(g, steps - 1), 0, 0))
+    steps = count // WEIGHT_GROUP
+    tiles = pl.BlockSpec((WEIGHT_GROUP, side, side), lambda g: (jnp.minimum(g, steps - 1), 0, 0))
     pixels = count * side * side
     weights = pl.pallas_call(
         weight_body,
         grid=(steps + 1,),
         in_specs=[smem, smem, tiles],
-        out_specs=pl.BlockSpec((parts, GROUP, height, side), lambda g: (0, g, 0, 0)),
+        out_specs=pl.BlockSpec((parts, WEIGHT_GROUP, height, side), lambda g: (0, g, 0, 0)),
         out_shape=jax.ShapeDtypeStruct((parts, slots, height, side), jnp.bfloat16),
-        scratch_shapes=[pltpu.VMEM((GROUP, 2, 2 * side, side // 2), jnp.float32)],
+        scratch_shapes=[pltpu.VMEM((WEIGHT_GROUP, 2, 2 * side, side // 2), jnp.float32)],
         cost_estimate=pl.CostEstimate(flops=20 * pixels, bytes_accessed=4 * pixels, transcendentals=0),
+        compiler_params=pltpu.CompilerParams(vmem_limit_bytes=60 << 20),
         name="weights",
     )(tile_patch.T, tile_offset.T, tile_var)
-    tile_image, weights = lax.optimization_barrier((tile_image, weights))
-    values = pl.pallas_call(
-        value_body,
-        grid=(steps + 1,),
-        in_specs=[smem] * 6 + [pl.BlockSpec((side, 3 * side), lambda g: (0, 0)), tiles, tiles],
-        out_specs=[pl.BlockSpec((GROUP, 32, side), lambda g: (g, 0, 0))] * 8,
-        out_shape=[jax.ShapeDtypeStruct((slots, 32, side), jnp.bfloat16)] * 8,
-        scratch_shapes=[
-            pltpu.VMEM((GROUP, 3, side, side), jnp.float32),
-            pltpu.VMEM((GROUP, 2, 2 * side, side // 2), jnp.float32),
-        ],
-        cost_estimate=pl.CostEstimate(flops=12 * pixels * side, bytes_accessed=6 * pixels, transcendentals=0),
-        compiler_params=pltpu.CompilerParams(vmem_limit_bytes=60 << 20),
-        name="values",
-    )(me, tile_patch.T, tile_offset.T, tile_visit, visit_scale, psf_coef.T, table, tile_image, tile_var)
+    def some_values(begin, end, tables, image):
+        steps, group = (end - begin) // GROUP, begin // GROUP
+        taken = pl.BlockSpec((GROUP, side, side), lambda g: (group + jnp.minimum(g, steps - 1), 0, 0))
+        return pl.pallas_call(
+            functools.partial(value_body, begin, tables),
+            grid=(steps + tables,),
+            in_specs=[smem] * 6 + [pl.BlockSpec((side, 3 * side), lambda g: (0, 0)), taken, taken],
+            out_specs=[pl.BlockSpec((GROUP, 32, side), lambda g: (g, 0, 0))] * 8,
+            out_shape=[jax.ShapeDtypeStruct((end - begin + tables, 32, side), jnp.bfloat16)] * 8,
+            scratch_shapes=[
+                pltpu.VMEM((GROUP, 3, side, side), jnp.float32),
+                pltpu.VMEM((GROUP, 2, 2 * side, side // 2), jnp.float32),
+            ],
+            cost_estimate=pl.CostEstimate(flops=6 * pixels * side, bytes_accessed=3 * pixels, transcendentals=0),
+            compiler_params=pltpu.CompilerParams(vmem_limit_bytes=60 << 20),
+            name="values",
+        )(me, tile_patch.T, tile_offset.T, tile_visit, visit_scale, psf_coef.T, table, image, tile_var)
 
     def share(m, rows):
         turn, other = m & 3, m >> 2
@@ -278,33 +323,67 @@
         ]
         return lax.ppermute(rows, ("epoch", "patch"), pairs)
 
-    got = [values[0]] + [share(m, values[m]) if m != 4 else None for m in range(1, 8)]
+    ints = lambda rows: rows.astype(jnp.float32).astype(jnp.int32)
+    hbm = pl.BlockSpec(memory_space=pl.ANY)
+    mine = jax.ShapeDtypeStruct((parts, 4, 2, 16, side), jnp.float32)
+    tile_image, weights = lax.optimization_barrier((tile_image, weights))
     got_weights = lax.all_to_all(weights, "patch", split_axis=0, concat_axis=0, tiled=True)
-    got_weights, got[1], got[2] = lax.optimization_barrier((got_weights, got[1], got[2]))
+
+    early = some_values(0, FIRST, 1, tile_image)
+    got = {0: early[0]}
+    for m in (1, 3, 2, 7, 5, 6, 4):
+        got[m] = share(m, early[m])
+    got = [got[m] for m in range(8)]
+    tile_image, early_0 = lax.optimization_barrier((tile_image, early[0]))
+    late = some_values(FIRST, count, 0, tile_image)
+    more = {0: late[0]}
+    for m in (1, 3, 2, 7, 5):
+        more[m] = share(m, late[m])
+    known = ints(jnp.stack([g[FIRST, :3, :count] for g in got]))
+    value_sums = pl.pallas_call(
+        first_values_body,
+        in_specs=[smem, smem] + [hbm] * 8,
+        out_specs=vmem,
+        out_shape=mine,
+        scratch_shapes=[pltpu.VMEM((8, FIRST, 32, side), jnp.bfloat16), pltpu.SemaphoreType.DMA((8,))],
+        cost_estimate=pl.CostEstimate(flops=5 * pixels, bytes_accessed=3 * pixels, transcendentals=0),
+        compiler_params=pltpu.CompilerParams(vmem_limit_bytes=56 << 20),
+        name="first_value_sums",
+    )(known, me, *got)
+
+    late_6, late_4, value_sums = lax.optimization_barrier((late[6], late[4], value_sums))
+    more[6], more[4] = share(6, late_6), share(4, late_4)
+    got_weights, more[1], more[3], value_sums = lax.optimization_barrier((got_weights, more[1], more[3], value_sums))
     weight_sums = pl.pallas_call(
         weight_sum_body,
-        in_specs=[smem, smem, smem, vmem],
+        in_specs=[smem, smem, hbm],
         out_specs=vmem,
         out_shape=jax.ShapeDtypeStruct((4, parts, height, side), jnp.bfloat16),
+        scratch_shapes=[
+            pltpu.VMEM((parts, slots, height, side), jnp.bfloat16),
+            pltpu.SemaphoreType.DMA((4,)),
+            *[pltpu.VMEM((parts, 4, height, side), jnp.float32)] * 4,
+        ],
         cost_estimate=pl.CostEstimate(flops=10 * pixels, bytes_accessed=3 * pixels, transcendentals=0),
         compiler_params=pltpu.CompilerParams(vmem_limit_bytes=60 << 20),
         name="weight_sums",
-    )(*by_patch(got_weights[:, count, :3, :count], slots, parts), me, got_weights.reshape(parts * slots, height, side))
-
-    core_share, weight_sums = lax.optimization_barrier((values[4], weight_sums))
-    got[4] = share(4, core_share)
-    known = jnp.stack([g[count, :3, :count] for g in got])
-    hbm = pl.BlockSpec(memory_space=pl.ANY)
+    )(ints(got_weights[:, count, :3, :count]), me, got_weights)
     sums = pl.pallas_call(
-        value_sum_body,
-        in_specs=[smem, smem, smem, vmem] + [hbm] * 8,
+        last_values_body,
+        in_specs=[smem, smem, vmem, hbm] + [hbm] * 8,
         out_specs=vmem,
         out_shape=jax.ShapeDtypeStruct((4, parts, 32 + height, side), jnp.bfloat16),
-        scratch_shapes=[pltpu.VMEM((8 * slots, 32, side), jnp.bfloat16), pltpu.SemaphoreType.DMA((8,))],
-        cost_estimate=pl.CostEstimate(flops=10 * pixels, bytes_accessed=4 * pixels, transcendentals=0),
+        scratch_shapes=[
+            pltpu.VMEM((8, count - FIRST, 32, side), jnp.bfloat16),
+            pltpu.VMEM(mine.shape, jnp.float32),
+            pltpu.VMEM(mine.shape, jnp.float32),
+            pltpu.SemaphoreType.DMA((8,)),
+            pltpu.SemaphoreType.DMA,
+        ],
+        cost_estimate=pl.CostEstimate(flops=5 * pixels, bytes_accessed=3 * pixels, transcendentals=0),
         compiler_params=pltpu.CompilerParams(vmem_limit_bytes=56 << 20),
-        name="value_sums",
-    )(*by_patch(known, slots, parts), me, weight_sums, *got)
+        name="last_value_sums",
+    )(known, me, weight_sums, value_sums, *[more[m] for m in range(8)])
 
     sums = sums.reshape(epochs * parts, 32 + height, side)
     got = lax.all_to_all(sums, ("epoch", "patch"), split_axis=0, concat_axis=0, tiled=True)

time: 150 us -> 141 us (0.940)
  waiting for transfers between devices: 26.1 us -> 12.2 us
  starting transfers between devices: 19.7 us -> 25.3 us
  blocking collectives: 45.8 us -> 49.3 us
  other arithmetic: 6 us -> 2.74 us
    ppermute x7 -> x14, waiting for transfers between devices: 20.2 us -> 9.78 us  [share(): return lax.ppermute(rows, ('epoch', 'patch'), pairs)]
    ppermute x7 -> x14, starting transfers between devices: 11.1 us -> 16.7 us  [share(): return lax.ppermute(rows, ('epoch', 'patch'), pairs)]
    reduce_sum x6 -> x0, other arithmetic: 4.14 us -> none  [the longest x2 1.79 us: by_patch(): jnp.sum(jnp.where(rank[None, :] == place[:, None], word[None, :], 0), axi...]
    all_to_all x1, waiting for transfers between devices: 5.98 us -> 2.43 us  [shards(): lax.all_to_all(weights, 'patch', split_axis=0, concat_axis=0, tiled=True)]
    all_to_all x1, blocking collectives: 45.8 us -> 49.3 us  [shards(): lax.all_to_all(sums, ('epoch', 'patch'), split_axis=0, concat_axis=0, til...]
    pallas_call x1, Pallas kernels: 8.77 us -> 7.22 us  [shards(): pl.pallas_call(weight_body, grid=(steps + 1,), in_specs=[smem, smem, tile...]
    pallas_call x3 -> x5, Pallas kernels: 39.7 us -> 40 us  [the longest x2 19.8 us: some_values(): pl.pallas_call(functools.partial(value_body, begin, tables), grid=(steps...]
  transfers between devices with their start and end apart: 8 -> 15, of which waited for: 5 -> 4; matrix products, arithmetic and copies ran while one was open for 4% -> 3% of each run, Pallas kernels for 19% -> 24%
where the time goes in v3:
time: 141 us; the launch traced here: 140 us
  blocking collectives  49.3 us (35%)
  Pallas kernels  48.3 us (34%)
  starting transfers between devices  25.3 us (18%)
  waiting for transfers between devices  12.2 us (9%)
  other arithmetic  2.74 us (2%)
  local copies, waits for them, and re-layouts  1.55 us (1%)
    all_to_all x1, blocking collectives, shards(): lax.all_to_all(sums, ('epoch', 'patch'), split_axis=0, concat_axis=0, til...  49.3 us
    pallas_call x2, Pallas kernels, some_values(): pl.pallas_call(functools.partial(value_body, begin, tables), grid=(steps...  19.8 us
    ppermute x14, starting transfers between devices, share(): return lax.ppermute(rows, ('epoch', 'patch'), pairs)  16.7 us
    ppermute x14, waiting for transfers between devices, share(): return lax.ppermute(rows, ('epoch', 'patch'), pairs)  9.78 us
    all_to_all x1, starting transfers between devices, shards(): lax.all_to_all(weights, 'patch', split_axis=0, concat_axis=0, tiled=True)  8.64 us
    pallas_call x1, Pallas kernels, shards(): pl.pallas_call(weight_sum_body, in_specs=[smem, smem, hbm], out_specs=vme...  8.03 us
    pallas_call x1, Pallas kernels, shards(): pl.pallas_call(weight_body, grid=(steps + 1,), in_specs=[smem, smem, tile...  7.22 us
    pallas_call x1, Pallas kernels, shards(): pl.pallas_call(last_values_body, in_specs=[smem, smem, vmem, hbm] + [hbm]...  6.68 us
  transfers between devices with their start and end apart: 15, of which 4 were waited for; matrix products, arithmetic and copies ran while one was open for 3% of the time, Pallas kernels for 24%

profile of v3, /device:TPU:1, one launch (start us, length us, event | category | flops | bytes accessed | tf_op | source)
XLA Modules:
  0.0 140.2 jit_solution(12091898692521534656)
XLA Ops:
  0.6 7.2 %weights.1 = bf16[32,33,8,256]{3,2,1,0:T(8,128)(2,1)} custom-call(s32[1,32]{1,0:T(1,128)} %bitcast.15, s32[2,32]{1,0:T(2,128)} %bitcast.12, bf16[32,256,256]{2,1,0:T(8,128)(2,1)} %var_ref.5), custom_call_target="tpu_custom_call" | custom-call | flops 41943040 | bytes 8388608 | tf_op jit(solution)/shard_map/weights/pallas_call | solution.py:290
  7.9 8.6 %all-to-all-start = ((bf16[32,33,8,256]{3,2,1,0:T(8,128)(2,1)}), bf16[32,33,8,256]{3,2,1,0:T(8,128)(2,1)}, u32[]{:S(2)}, u32[]{:S(2)}) async-start(bf16[32,33,8,256]{3,2,1,0:T(8,128)(2,1)} %weights.1), calls=%async_computation | async-start | bytes 8650752 | tf_op jit(solution)/shard_map/all_to_all | solution.py:330
  16.5 0.7 pad_add_fusion.me_ref
  17.2 8.1 %values.2 = (bf16[13,32,256]{2,1,0:T(8,128)(2,1)}, bf16[13,32,256]{2,1,0:T(8,128)(2,1)}, bf16[13,32,256]{2,1,0:T(8,128)(2,1)}, bf16[13,32,256]{2,1,0:T(8,128)(2,...) custom-call(s32[3]{0:T(128)} %pad_add_fusion.me_ref, ...), custom_call_target="tpu_custom_call" | custom-call | flops 3221225472 | bytes 6291456 | tf_op jit(solution)/shard_map/values/pallas_call | solution.py:304
  25.3 1.7 %collective-permute-start = (bf16[13,32,256]{2,1,0:T(8,128)(2,1)}, bf16[13,32,256]{2,1,0:T(8,128)(2,1)S(1)}, u32[]{:S(2)}, u32[]{:S(2)}) collective-permute-start(bf16[13,32,256]{2,1,0:T(8,128)(2,1)} %get-tuple-element.30), channel_id=1, source_target_pairs={{0,32},{1,33},{2,34},{3,35},{4,36},{5,37},{6,38},{7,39},{8,40},{9,... | collective-permute-start | bytes 638984 | tf_op jit(solution)/shard_map/ppermute | solution.py:324
  27.0 3.3 %collective-permute-start.1 = (bf16[13,32,256]{2,1,0:T(8,128)(2,1)}, bf16[13,32,256]{2,1,0:T(8,128)(2,1)S(1)}, u32[]{:S(2)}, u32[]{:S(2)}) collective-permute-start(bf16[13,32,256]{2,1,0:T(8,128)(2,1)} %get-tuple-element.31), channel_id=1, source_target_pairs={{0,64},{1,65},{2,66},{3,67},{4,68},{5,69},{6,70},{7,71},{8,72},{9,... | collective-permute-start | bytes 638984 | tf_op jit(solution)/shard_map/ppermute | solution.py:324
  30.3 0.7 collective-permute-start.2
  31.0 1.1 collective-permute-start.3
  32.1 0.6 collective-permute-start.4
  32.8 11.7 %values.3 = (bf16[20,32,256]{2,1,0:T(8,128)(2,1)}, bf16[20,32,256]{2,1,0:T(8,128)(2,1)}, bf16[20,32,256]{2,1,0:T(8,128)(2,1)}, bf16[20,32,256]{2,1,0:T(8,128)(2,...) custom-call(s32[3]{0:T(128)} %pad_add_fusion.me_ref, ...), custom_call_target="tpu_custom_call" | custom-call | flops 3221225472 | bytes 6291456 | tf_op jit(solution)/shard_map/values/pallas_call | solution.py:304
  44.4 0.0 copy-start.15
  44.4 0.0 copy-start.14
  44.5 0.7 constant_dynamic-update-slice_fusion.7
  45.2 0.0 collective-permute-done.refs_1_
  45.2 0.0 copy-done.17
  45.2 0.6 collective-permute-start.5
  45.9 0.0 collective-permute-done.1.refs_2_
  45.9 0.0 copy-done.16
  45.9 2.3 %collective-permute-start.6 = (bf16[13,32,256]{2,1,0:T(8,128)(2,1)S(1)}, bf16[13,32,256]{2,1,0:T(8,128)(2,1)S(1)}, u32[]{:S(2)}, u32[]{:S(2)}) collective-permute-start(bf16[13,32,256]{2,1,0:T(8,128)(2,1)S(1)} %copy-done.16), channel_id=1, source_target_pairs={{0,97},{1,96},{2,99},{3,98},{4,101},{5,100},{6,103},{7,102},{8,105... | collective-permute-start | bytes 638984 | tf_op jit(solution)/shard_map/ppermute | solution.py:324
  48.2 0.0 collective-permute-done.2.refs_3_
  48.2 0.2 collective-permute-start.7
  48.4 0.0 collective-permute-done.3.refs_4_
  48.4 2.6 %collective-permute-start.8 = (bf16[20,32,256]{2,1,0:T(8,128)(2,1)}, bf16[20,32,256]{2,1,0:T(8,128)(2,1)S(1)}, u32[]{:S(2)}, u32[]{:S(2)}) collective-permute-start(bf16[20,32,256]{2,1,0:T(8,128)(2,1)} %get-tuple-element.40), channel_id=1, source_target_pairs={{0,96},{1,97},{2,98},{3,99},{4,100},{5,101},{6,102},{7,103},{8,104... | collective-permute-start | bytes 983048 | tf_op jit(solution)/shard_map/ppermute | solution.py:324
  51.0 0.0 collective-permute-done.4.refs_5_
  51.0 0.6 collective-permute-start.9
  51.7 3.1 %collective-permute-done.5.refs_6_ = bf16[13,32,256]{2,1,0:T(8,128)(2,1)S(1)} collective-permute-done((bf16[13,32,256]{2,1,0:T(8,128)(2,1)S(1)}, bf16[13,32,256]{2,1,0:T(8,128)(2,1)S(1)}, u32[]{:S(2)}, u32[]{:S(2)}) %collective-permute-start.5) | collective-permute-done | bytes 213024 | tf_op jit(solution)/shard_map/ppermute | solution.py:324
  54.8 0.0 collective-permute-start.11
  54.8 4.1 %collective-permute-done.6.refs_7_ = bf16[13,32,256]{2,1,0:T(8,128)(2,1)S(1)} collective-permute-done((bf16[13,32,256]{2,1,0:T(8,128)(2,1)S(1)}, bf16[13,32,256]{2,1,0:T(8,128)(2,1)S(1)}, u32[]{:S(2)}, u32[]{:S(2)}) %collective-permute-start.6) | collective-permute-done | bytes 213024 | tf_op jit(solution)/shard_map/ppermute | solution.py:324
  58.9 2.3 %collective-permute-start.13 = (bf16[20,32,256]{2,1,0:T(8,128)(2,1)}, bf16[20,32,256]{2,1,0:T(8,128)(2,1)S(1)}, u32[]{:S(2)}, u32[]{:S(2)}) collective-permute-start(bf16[20,32,256]{2,1,0:T(8,128)(2,1)} %get-tuple-element.53), channel_id=1, source_target_pairs={{0,97},{1,96},{2,99},{3,98},{4,101},{5,100},{6,103},{7,102},{8,105... | collective-permute-start | bytes 983048 | tf_op jit(solution)/shard_map/ppermute | solution.py:324
  61.2 0.6 convert_convert_fusion.known_ref
  61.8 0.0 copy-done.7
  61.8 0.0 copy-done.8
  61.8 0.0 copy-done.9
  61.8 0.0 copy-done.10
  61.8 0.0 copy-done.11
  61.8 0.0 copy-done.12
  61.9 0.0 copy-done.13
  61.9 5.5 %first_value_sums.1.before_ref = f32[32,4,2,16,256]{4,3,2,1,0:T(8,128)} custom-call(s32[8,3,32]{2,1,0:T(4,128)} %convert_convert_fusion.known_ref, s32[3]{0:T(128)} %pad_add_fusion.me_ref, bf16[13,32,256]{2,1,0:T(8,128)(2,1)} %get-tuple-element.29.refs_0_, bf16[13,32,256]{2,1,0:T(8,128)(2,1)} %copy-done.7, bf16[13,32,256]{2,1,0:T(8,128)(2,1)} %copy-done.8, ...), custom_call_target="tpu_custom_call" | custom-call | flops 10485760 | bytes 6291456 | tf_op jit(solution)/shard_map/first_value_sums/pallas_call | solution.py:343
  67.4 0.0 collective-permute-done.7.refs_1_
  67.4 0.0 copy-done.15
  67.4 0.0 copy-start
  67.4 0.3 collective-permute-start.10
  67.8 0.0 collective-permute-done.8.refs_3_
  67.8 0.0 copy-done.14
  67.8 0.1 collective-permute-start.12
  67.9 2.4 %all-to-all-done.got_ref = bf16[32,33,8,256]{3,2,1,0:T(8,128)(2,1)} async-done(((bf16[32,33,8,256]{3,2,1,0:T(8,128)(2,1)}), bf16[32,33,8,256]{3,2,1,0:T(8,128)(2,1)}, u32[]{:S(2)}, u32[]{:S(2)}) %all-to-all-start) | async-done | bytes 4325408 | tf_op jit(solution)/shard_map/all_to_all | solution.py:330
  70.3 1.5 %convert_bitcast_fusion.known_ref = s32[32,3,32]{2,1,0:T(4,128)} fusion(bf16[32,33,8,256]{3,2,1,0:T(8,128)(2,1)} %all-to-all-done.got_ref), kind=kLoop, calls=%fused_computation | loop fusion | flops 6144 | bytes 18432 | tf_op jit(solution)/shard_map/convert_element_type | solution.py:326
  71.8 8.0 %weight_sums.1.weight_ref = bf16[4,32,8,256]{3,2,1,0:T(8,128)(2,1)} custom-call(s32[32,3,32]{2,1,0:T(4,128)} %convert_bitcast_fusion.known_ref, s32[3]{0:T(128)} %pad_add_fusion.me_ref, bf16[32,33,8,256]{3,2,1,0:T(8,128)(2,1)} %all-to-all-done.got_ref), custom_call_target="tpu_custom_call" | custom-call | flops 20971520 | bytes 6291456 | tf_op jit(solution)/shard_map/weight_sums/pallas_call | solution.py:357
  79.8 0.0 collective-permute-done.9.refs_2_
  79.8 0.0 copy-start.2
  79.8 0.0 collective-permute-done.11.refs_5_
  79.8 0.0 copy-start.3
  79.9 0.0 collective-permute-done.13.refs_7_
  79.9 0.0 collective-permute-done.10.refs_4_
  79.9 2.5 %collective-permute-done.12.refs_6_ = bf16[20,32,256]{2,1,0:T(8,128)(2,1)S(1)} collective-permute-done((bf16[20,32,256]{2,1,0:T(8,128)(2,1)S(1)}, bf16[20,32,256]{2,1,0:T(8,128)(2,1)S(1)}, u32[]{:S(2)}, u32[]{:S(2)}) %collective-permute-start.12) | collective-permute-done | bytes 327712 | tf_op jit(solution)/shard_map/ppermute | solution.py:324
  82.4 0.0 copy-done
  82.4 0.0 copy-done.1
  82.4 0.0 copy-done.3
  82.4 0.0 copy-done.4
  82.5 0.0 copy-done.5
  82.5 0.7 copy-done.6
  83.1 6.7 %last_value_sums.1 = bf16[4,32,40,256]{3,2,1,0:T(8,128)(2,1)} custom-call(s32[8,3,32]{2,1,0:T(4,128)} %convert_convert_fusion.known_ref, s32[3]{0:T(128)} %pad_add_fusion.me_ref, bf16[4,32,8,256]{3,2,1,0:T(8,128)(2,1)} %weight_sums.1.weight_ref, f32[32,4,2,16,256]{4,3,2,1,0:T(8,128)} %first_value_sums.1.before_ref, ...), custom_call_target="tpu_custom_call" | custom-call | flops 10485760 | bytes 6291456 | tf_op jit(solution)/shard_map/last_value_sums/pallas_call | solution.py:371
  89.8 49.3 %all_to_all.10 = bf16[128,40,256]{2,1,0:T(8,128)(2,1)S(1)} all-to-all(bf16[128,40,256]{2,1,0:T(8,128)(2,1)} %bitcast.11), channel_id=1, replica_groups=mesh['epoch'=4,'patch'=32] {'epoch','patch'}, dimensions={0} | all-to-all | bytes 5242880 | tf_op jit(solution)/shard_map/all_to_all | solution.py:389
  139.1 1.1 final.1
  (21 shorter events, 0.1 us)
Async XLA Ops:
  7.9 62.4 %all-to-all-start = ((bf16[32,33,8,256]{3,2,1,0:T(8,128)(2,1)}), bf16[32,33,8,256]{3,2,1,0:T(8,128)(2,1)}, u32[]{:S(2)}, u32[]{:S(2)}) async-start(bf16[32,33,8,256]{3,2,1,0:T(8,128)(2,1)} %weights.1), calls=%async_computation | async-start | bytes 8650752 | tf_op jit(solution)/shard_map/all_to_all | solution.py:330
  25.3 20.0 %collective-permute-start = (bf16[13,32,256]{2,1,0:T(8,128)(2,1)}, bf16[13,32,256]{2,1,0:T(8,128)(2,1)S(1)}, u32[]{:S(2)}, u32[]{:S(2)}) collective-permute-start(bf16[13,32,256]{2,1,0:T(8,128)(2,1)} %get-tuple-element.30), channel_id=1, source_target_pairs={{0,32},{1,33},{2,34},{3,35},{4,36},{5,37},{6,38},{7,39},{8,40},{9,... | collective-permute-start | bytes 638984 | tf_op jit(solution)/shard_map/ppermute | solution.py:324
  27.0 18.9 %collective-permute-start.1 = (bf16[13,32,256]{2,1,0:T(8,128)(2,1)}, bf16[13,32,256]{2,1,0:T(8,128)(2,1)S(1)}, u32[]{:S(2)}, u32[]{:S(2)}) collective-permute-start(bf16[13,32,256]{2,1,0:T(8,128)(2,1)} %get-tuple-element.31), channel_id=1, source_target_pairs={{0,64},{1,65},{2,66},{3,67},{4,68},{5,69},{6,70},{7,71},{8,72},{9,... | collective-permute-start | bytes 638984 | tf_op jit(solution)/shard_map/ppermute | solution.py:324
  30.3 17.9 %collective-permute-start.2 = (bf16[13,32,256]{2,1,0:T(8,128)(2,1)}, bf16[13,32,256]{2,1,0:T(8,128)(2,1)S(1)}, u32[]{:S(2)}, u32[]{:S(2)}) collective-permute-start(bf16[13,32,256]{2,1,0:T(8,128)(2,1)} %get-tuple-element.32), channel_id=1, source_target_pairs={{0,96},{1,97},{2,98},{3,99},{4,100},{5,101},{6,102},{7,103},{8,104... | collective-permute-start | bytes 638984 | tf_op jit(solution)/shard_map/ppermute | solution.py:324
  31.0 17.4 %collective-permute-start.3 = (bf16[13,32,256]{2,1,0:T(8,128)(2,1)}, bf16[13,32,256]{2,1,0:T(8,128)(2,1)S(1)}, u32[]{:S(2)}, u32[]{:S(2)}) collective-permute-start(bf16[13,32,256]{2,1,0:T(8,128)(2,1)} %get-tuple-element.33), channel_id=1, source_target_pairs={{0,1},{1,0},{2,3},{3,2},{4,5},{5,4},{6,7},{7,6},{8,9},{9,8},{10,11... | collective-permute-start | bytes 638984 | tf_op jit(solution)/shard_map/ppermute | solution.py:324
  32.1 18.9 %collective-permute-start.4 = (bf16[13,32,256]{2,1,0:T(8,128)(2,1)}, bf16[13,32,256]{2,1,0:T(8,128)(2,1)S(1)}, u32[]{:S(2)}, u32[]{:S(2)}) collective-permute-start(bf16[13,32,256]{2,1,0:T(8,128)(2,1)} %get-tuple-element.34), channel_id=1, source_target_pairs={{0,33},{1,32},{2,35},{3,34},{4,37},{5,36},{6,39},{7,38},{8,41},{9,... | collective-permute-start | bytes 638984 | tf_op jit(solution)/shard_map/ppermute | solution.py:324
  32.8 12.4 %copy-start.17 = (bf16[13,32,256]{2,1,0:T(8,128)(2,1)S(1)}, bf16[13,32,256]{2,1,0:T(8,128)(2,1)}, u32[]{:S(2)}) copy-start(bf16[13,32,256]{2,1,0:T(8,128)(2,1)} %get-tuple-element.35) | copy-start | bytes 638980
  32.8 13.1 %copy-start.16 = (bf16[13,32,256]{2,1,0:T(8,128)(2,1)S(1)}, bf16[13,32,256]{2,1,0:T(8,128)(2,1)}, u32[]{:S(2)}) copy-start(bf16[13,32,256]{2,1,0:T(8,128)(2,1)} %get-tuple-element.36) | copy-start | bytes 638980
  44.4 23.0 %copy-start.15 = (bf16[20,32,256]{2,1,0:T(8,128)(2,1)S(1)}, bf16[20,32,256]{2,1,0:T(8,128)(2,1)}, u32[]{:S(2)}) copy-start(bf16[20,32,256]{2,1,0:T(8,128)(2,1)} %get-tuple-element.50) | copy-start | bytes 983044
  44.4 23.3 %copy-start.14 = (bf16[20,32,256]{2,1,0:T(8,128)(2,1)S(1)}, bf16[20,32,256]{2,1,0:T(8,128)(2,1)}, u32[]{:S(2)}) copy-start(bf16[20,32,256]{2,1,0:T(8,128)(2,1)} %get-tuple-element.52) | copy-start | bytes 983044
  45.2 16.6 %copy-start.7 = (bf16[13,32,256]{2,1,0:T(8,128)(2,1)}, bf16[13,32,256]{2,1,0:T(8,128)(2,1)S(1)}, u32[]{:S(2)}) copy-start(bf16[13,32,256]{2,1,0:T(8,128)(2,1)S(1)} %collective-permute-done.refs_1_) | copy-start | bytes 638980
  45.2 9.6 %collective-permute-start.5 = (bf16[13,32,256]{2,1,0:T(8,128)(2,1)S(1)}, bf16[13,32,256]{2,1,0:T(8,128)(2,1)S(1)}, u32[]{:S(2)}, u32[]{:S(2)}) collective-permute-start(bf16[13,32,256]{2,1,0:T(8,128)(2,1)S(1)} %copy-done.17), channel_id=1, source_target_pairs={{0,65},{1,64},{2,67},{3,66},{4,69},{5,68},{6,71},{7,70},{8,73},{9,... | collective-permute-start | bytes 638984 | tf_op jit(solution)/shard_map/ppermute | solution.py:324
  45.9 16.0 %copy-start.8 = (bf16[13,32,256]{2,1,0:T(8,128)(2,1)}, bf16[13,32,256]{2,1,0:T(8,128)(2,1)S(1)}, u32[]{:S(2)}) copy-start(bf16[13,32,256]{2,1,0:T(8,128)(2,1)S(1)} %collective-permute-done.1.refs_2_) | copy-start | bytes 638980
  45.9 13.0 %collective-permute-start.6 = (bf16[13,32,256]{2,1,0:T(8,128)(2,1)S(1)}, bf16[13,32,256]{2,1,0:T(8,128)(2,1)S(1)}, u32[]{:S(2)}, u32[]{:S(2)}) collective-permute-start(bf16[13,32,256]{2,1,0:T(8,128)(2,1)S(1)} %copy-done.16), channel_id=1, source_target_pairs={{0,97},{1,96},{2,99},{3,98},{4,101},{5,100},{6,103},{7,102},{8,105... | collective-permute-start | bytes 638984 | tf_op jit(solution)/shard_map/ppermute | solution.py:324
  48.2 13.6 %copy-start.9 = (bf16[13,32,256]{2,1,0:T(8,128)(2,1)}, bf16[13,32,256]{2,1,0:T(8,128)(2,1)S(1)}, u32[]{:S(2)}) copy-start(bf16[13,32,256]{2,1,0:T(8,128)(2,1)S(1)} %collective-permute-done.2.refs_3_) | copy-start | bytes 638980
  48.2 19.2 %collective-permute-start.7 = (bf16[20,32,256]{2,1,0:T(8,128)(2,1)}, bf16[20,32,256]{2,1,0:T(8,128)(2,1)S(1)}, u32[]{:S(2)}, u32[]{:S(2)}) collective-permute-start(bf16[20,32,256]{2,1,0:T(8,128)(2,1)} %get-tuple-element.39), channel_id=1, source_target_pairs={{0,32},{1,33},{2,34},{3,35},{4,36},{5,37},{6,38},{7,39},{8,40},{9,... | collective-permute-start | bytes 983048 | tf_op jit(solution)/shard_map/ppermute | solution.py:324
  48.4 13.4 %copy-start.10 = (bf16[13,32,256]{2,1,0:T(8,128)(2,1)}, bf16[13,32,256]{2,1,0:T(8,128)(2,1)S(1)}, u32[]{:S(2)}) copy-start(bf16[13,32,256]{2,1,0:T(8,128)(2,1)S(1)} %collective-permute-done.3.refs_4_) | copy-start | bytes 638980
  48.4 19.4 %collective-permute-start.8 = (bf16[20,32,256]{2,1,0:T(8,128)(2,1)}, bf16[20,32,256]{2,1,0:T(8,128)(2,1)S(1)}, u32[]{:S(2)}, u32[]{:S(2)}) collective-permute-start(bf16[20,32,256]{2,1,0:T(8,128)(2,1)} %get-tuple-element.40), channel_id=1, source_target_pairs={{0,96},{1,97},{2,98},{3,99},{4,100},{5,101},{6,102},{7,103},{8,104... | collective-permute-start | bytes 983048 | tf_op jit(solution)/shard_map/ppermute | solution.py:324
  51.0 10.8 %copy-start.11 = (bf16[13,32,256]{2,1,0:T(8,128)(2,1)}, bf16[13,32,256]{2,1,0:T(8,128)(2,1)S(1)}, u32[]{:S(2)}) copy-start(bf16[13,32,256]{2,1,0:T(8,128)(2,1)S(1)} %collective-permute-done.4.refs_5_) | copy-start | bytes 638980
  51.0 28.8 %collective-permute-start.9 = (bf16[20,32,256]{2,1,0:T(8,128)(2,1)}, bf16[20,32,256]{2,1,0:T(8,128)(2,1)S(1)}, u32[]{:S(2)}, u32[]{:S(2)}) collective-permute-start(bf16[20,32,256]{2,1,0:T(8,128)(2,1)} %get-tuple-element.48), channel_id=1, source_target_pairs={{0,64},{1,65},{2,66},{3,67},{4,68},{5,69},{6,70},{7,71},{8,72},{9,... | collective-permute-start | bytes 983048 | tf_op jit(solution)/shard_map/ppermute | solution.py:324
  54.8 7.1 %copy-start.12 = (bf16[13,32,256]{2,1,0:T(8,128)(2,1)}, bf16[13,32,256]{2,1,0:T(8,128)(2,1)S(1)}, u32[]{:S(2)}) copy-start(bf16[13,32,256]{2,1,0:T(8,128)(2,1)S(1)} %collective-permute-done.5.refs_6_) | copy-start | bytes 638980
  54.8 25.0 %collective-permute-start.11 = (bf16[20,32,256]{2,1,0:T(8,128)(2,1)}, bf16[20,32,256]{2,1,0:T(8,128)(2,1)S(1)}, u32[]{:S(2)}, u32[]{:S(2)}) collective-permute-start(bf16[20,32,256]{2,1,0:T(8,128)(2,1)} %get-tuple-element.51), channel_id=1, source_target_pairs={{0,33},{1,32},{2,35},{3,34},{4,37},{5,36},{6,39},{7,38},{8,41},{9,... | collective-permute-start | bytes 983048 | tf_op jit(solution)/shard_map/ppermute | solution.py:324
  58.9 3.0 %copy-start.13 = (bf16[13,32,256]{2,1,0:T(8,128)(2,1)}, bf16[13,32,256]{2,1,0:T(8,128)(2,1)S(1)}, u32[]{:S(2)}) copy-start(bf16[13,32,256]{2,1,0:T(8,128)(2,1)S(1)} %collective-permute-done.6.refs_7_) | copy-start | bytes 638980
  58.9 21.0 %collective-permute-start.13 = (bf16[20,32,256]{2,1,0:T(8,128)(2,1)}, bf16[20,32,256]{2,1,0:T(8,128)(2,1)S(1)}, u32[]{:S(2)}, u32[]{:S(2)}) collective-permute-start(bf16[20,32,256]{2,1,0:T(8,128)(2,1)} %get-tuple-element.53), channel_id=1, source_target_pairs={{0,97},{1,96},{2,99},{3,98},{4,101},{5,100},{6,103},{7,102},{8,105... | collective-permute-start | bytes 983048 | tf_op jit(solution)/shard_map/ppermute | solution.py:324
  67.4 15.0 %copy-start = (bf16[20,32,256]{2,1,0:T(8,128)(2,1)}, bf16[20,32,256]{2,1,0:T(8,128)(2,1)S(1)}, u32[]{:S(2)}) copy-start(bf16[20,32,256]{2,1,0:T(8,128)(2,1)S(1)} %collective-permute-done.7.refs_1_) | copy-start | bytes 983044
  67.4 12.5 %collective-permute-start.10 = (bf16[20,32,256]{2,1,0:T(8,128)(2,1)S(1)}, bf16[20,32,256]{2,1,0:T(8,128)(2,1)S(1)}, u32[]{:S(2)}, u32[]{:S(2)}) collective-permute-start(bf16[20,32,256]{2,1,0:T(8,128)(2,1)S(1)} %copy-done.15), channel_id=1, source_target_pairs={{0,1},{1,0},{2,3},{3,2},{4,5},{5,4},{6,7},{7,6},{8,9},{9,8},{10,11... | collective-permute-start | bytes 983048 | tf_op jit(solution)/shard_map/ppermute | solution.py:324
  67.8 14.7 %copy-start.1 = (bf16[20,32,256]{2,1,0:T(8,128)(2,1)}, bf16[20,32,256]{2,1,0:T(8,128)(2,1)S(1)}, u32[]{:S(2)}) copy-start(bf16[20,32,256]{2,1,0:T(8,128)(2,1)S(1)} %collective-permute-done.8.refs_3_) | copy-start | bytes 983044
  67.8 14.7 %collective-permute-start.12 = (bf16[20,32,256]{2,1,0:T(8,128)(2,1)S(1)}, bf16[20,32,256]{2,1,0:T(8,128)(2,1)S(1)}, u32[]{:S(2)}, u32[]{:S(2)}) collective-permute-start(bf16[20,32,256]{2,1,0:T(8,128)(2,1)S(1)} %copy-done.14), channel_id=1, source_target_pairs={{0,65},{1,64},{2,67},{3,66},{4,69},{5,68},{6,71},{7,70},{8,73},{9,... | collective-permute-start | bytes 983048 | tf_op jit(solution)/shard_map/ppermute | solution.py:324
  79.8 2.6 %copy-start.2 = (bf16[20,32,256]{2,1,0:T(8,128)(2,1)}, bf16[20,32,256]{2,1,0:T(8,128)(2,1)S(1)}, u32[]{:S(2)}) copy-start(bf16[20,32,256]{2,1,0:T(8,128)(2,1)S(1)} %collective-permute-done.9.refs_2_) | copy-start | bytes 983044
  79.8 2.6 %copy-start.3 = (bf16[20,32,256]{2,1,0:T(8,128)(2,1)}, bf16[20,32,256]{2,1,0:T(8,128)(2,1)S(1)}, u32[]{:S(2)}) copy-start(bf16[20,32,256]{2,1,0:T(8,128)(2,1)S(1)} %collective-permute-done.11.refs_5_) | copy-start | bytes 983044
  79.9 2.5 %copy-start.4 = (bf16[20,32,256]{2,1,0:T(8,128)(2,1)}, bf16[20,32,256]{2,1,0:T(8,128)(2,1)S(1)}, u32[]{:S(2)}) copy-start(bf16[20,32,256]{2,1,0:T(8,128)(2,1)S(1)} %collective-permute-done.13.refs_7_) | copy-start | bytes 983044
  79.9 2.6 %copy-start.5 = (bf16[20,32,256]{2,1,0:T(8,128)(2,1)}, bf16[20,32,256]{2,1,0:T(8,128)(2,1)S(1)}, u32[]{:S(2)}) copy-start(bf16[20,32,256]{2,1,0:T(8,128)(2,1)S(1)} %collective-permute-done.10.refs_4_) | copy-start | bytes 983044
  82.4 0.7 copy-start.6

commit v4 on v3

--- a/solution.py
+++ b/solution.py
@@ -13,6 +13,7 @@
 GROUP = 4
 WEIGHT_GROUP = 8
 FIRST = 12
+EARLY = (0,)
 
 
 def blur_kernels(side):
@@ -74,7 +75,7 @@
             out_ref[part, 0] = known
 
 
-def value_body(begin, tables, me_ref, patch_ref, off_ref, visit_ref, scale_ref, coef_ref, kernel_ref, image_ref, var_ref, *refs):
+def value_body(begin, tables, z_ref, core_ref, patch_ref, off_ref, visit_ref, scale_ref, coef_ref, kernel_ref, image_ref, var_ref, *refs):
     outs, (blur_ref, wide_ref) = refs[:8], refs[8:]
     group, height, side = outs[0].shape
     step = pl.program_id(0)
@@ -112,7 +113,7 @@
                     both.append(gain * (1.0 / var_ref[t, rows, cols].astype(jnp.float32)) * matched)
                 keep_turned(jnp.concatenate(both, axis=1), off_c, wide_ref.at[t], c * chunk)
             for m in range(8):
-                member = (((me_ref[0] + (m & 3)) & 3) << 1) + (me_ref[1] ^ (m >> 2))
+                member = (((z_ref[0] + (m & 3)) & 3) << 1) + (core_ref[0] ^ (m >> 2))
                 for part in range(2):
                     top = (part * half + (member << 4) - off_r) & (side - 1)
                     for h in range(2):
@@ -138,7 +139,7 @@
     lax.fori_loop(0, sums_ref.shape[0], clear, 0)
 
 
-def weight_sum_body(known_ref, me_ref, got_ref, out_ref, data_ref, sems, *sums_refs):
+def weight_sum_body(known_ref, part_ref, got_ref, out_ref, data_ref, sems, *sums_refs):
     sources, slots, height, side = got_ref.shape
     tiles, patches = slots - 1, out_ref.shape[1]
     bunch = sources // sems.shape[0]
@@ -149,7 +150,7 @@
     for copy in copies:
         copy.start()
     s = lax.broadcasted_iota(jnp.int32, (height, side), 0)
-    row = (s >> 2) * (side // 2) + 4 * me_ref[2] + (s & 3)
+    row = (s >> 2) * (side // 2) + 4 * part_ref[0] + (s & 3)
     lane = lax.broadcasted_iota(jnp.int32, (height, side), 1)
     swap = height // 2
     first = s < swap
@@ -185,21 +186,34 @@
     lax.fori_loop(0, patches, one_patch, 0)
 
 
-def add_values(known_ref, me_ref, begin, tiles, copies, data_ref, sums_ref):
+def add_values(known_ref, z_ref, core_ref, shares, got, data_ref, sums_ref, sems):
     _, _, height, side = data_ref.shape
     band = height // 2
-    s = lax.broadcasted_iota(jnp.int32, (band, side), 0) + (((me_ref[0] << 1) + me_ref[1]) << 4)
+    copies = [
+        pltpu.make_async_copy(rows.at[pl.ds(0, tiles)], data_ref.at[n, pl.ds(0, tiles)], sems.at[n])
+        for n, (rows, (m, begin, tiles)) in enumerate(zip(got, shares))
+    ]
+    for copy in copies:
+        copy.start()
+    zero = jnp.zeros(sums_ref.shape[1:], jnp.float32)
+
+    def clear(p, unused):
+        sums_ref[p] = zero
+        return unused
+
+    lax.fori_loop(0, sums_ref.shape[0], clear, 0)
+    s = lax.broadcasted_iota(jnp.int32, (band, side), 0) + (((z_ref[0] << 1) + core_ref[0]) << 4)
     lane = lax.broadcasted_iota(jnp.int32, (band, side), 1)
 
-    for m, copy in enumerate(copies):
-        copy.wait()
+    for n, (m, begin, tiles) in enumerate(shares):
+        copies[n].wait()
 
         def some_tiles(step, unused):
             for u in range(4):
                 t = 4 * step + u
-                p, off_r, off_c = (known_ref[m, n, begin + t] for n in range(3))
+                p, off_r, off_c = (known_ref[m, k, begin + t] for k in range(3))
                 for part in range(2):
-                    value = data_ref[m, t, part * band : (part + 1) * band].astype(jnp.float32)
+                    value = data_ref[n, t, part * band : (part + 1) * band].astype(jnp.float32)
                     left = jnp.where(lane >= off_c, value, 0.0)
                     right = value - left
                     upper = s >= off_r - part * (side // 2)
@@ -213,27 +227,17 @@
         lax.fori_loop(0, tiles // 4, some_tiles, 0)
 
 
-def first_values_body(known_ref, me_ref, *refs):
-    got, out_ref, (data_ref, sems) = refs[:8], refs[8], refs[9:]
-    tiles = got[0].shape[0] - 1
-    copies = [pltpu.make_async_copy(got[m].at[pl.ds(0, tiles)], data_ref.at[m], sems.at[m]) for m in range(8)]
-    for copy in copies:
-        copy.start()
-    clear_sums(out_ref)
-    add_values(known_ref, me_ref, 0, tiles, copies, data_ref, out_ref)
-
-
-def last_values_body(known_ref, me_ref, weight_ref, before_ref, *refs):
-    got, out_ref, (data_ref, first_ref, sums_ref, sems, first_sem) = refs[:8], refs[8], refs[9:]
-    tiles = got[0].shape[0]
+def first_values_body(shares, known_ref, z_ref, core_ref, *refs):
+    got, (out_ref, data_ref, sems) = refs[: len(shares)], refs[len(shares) :]
+    add_values(known_ref, z_ref, core_ref, shares, got, data_ref, out_ref, sems)
+
+
+def last_values_body(shares, known_ref, z_ref, core_ref, weight_ref, before_ref, *refs):
+    got, (out_ref, data_ref, first_ref, sums_ref, sems, first_sem) = refs[: len(shares)], refs[len(shares) :]
     band = sums_ref.shape[3]
-    copies = [pltpu.make_async_copy(got[m], data_ref.at[m], sems.at[m]) for m in range(8)]
-    for copy in copies:
-        copy.start()
     earlier = pltpu.make_async_copy(before_ref, first_ref, first_sem)
     earlier.start()
-    clear_sums(sums_ref)
-    add_values(known_ref, me_ref, known_ref.shape[2] - tiles, tiles, copies, data_ref, sums_ref)
+    add_values(known_ref, z_ref, core_ref, shares, got, data_ref, sums_ref, sems)
     earlier.wait()
 
     def one_patch(p, unused):
@@ -279,7 +283,7 @@
     height = side // parts
     slots = count + 1
     z, j = lax.axis_index("epoch"), lax.axis_index("patch")
-    me = jnp.stack([z, j & 1, j]).astype(jnp.int32)
+    place = [jnp.reshape(n, (1,)).astype(jnp.int32) for n in (z, j & 1, j)]
     table = jnp.asarray(blur_kernels(side))
 
     smem = pl.BlockSpec(memory_space=pltpu.SMEM)
@@ -304,7 +308,7 @@
         return pl.pallas_call(
             functools.partial(value_body, begin, tables),
             grid=(steps + tables,),
-            in_specs=[smem] * 6 + [pl.BlockSpec((side, 3 * side), lambda g: (0, 0)), taken, taken],
+            in_specs=[smem] * 7 + [pl.BlockSpec((side, 3 * side), lambda g: (0, 0)), taken, taken],
             out_specs=[pl.BlockSpec((GROUP, 32, side), lambda g: (g, 0, 0))] * 8,
             out_shape=[jax.ShapeDtypeStruct((end - begin + tables, 32, side), jnp.bfloat16)] * 8,
             scratch_shapes=[
@@ -314,7 +318,7 @@
             cost_estimate=pl.CostEstimate(flops=6 * pixels * side, bytes_accessed=3 * pixels, transcendentals=0),
             compiler_params=pltpu.CompilerParams(vmem_limit_bytes=60 << 20),
             name="values",
-        )(me, tile_patch.T, tile_offset.T, tile_visit, visit_scale, psf_coef.T, table, image, tile_var)
+        )(*place[:2], tile_patch.T, tile_offset.T, tile_visit, visit_scale, psf_coef.T, table, image, tile_var)
 
     def share(m, rows):
         turn, other = m & 3, m >> 2
@@ -337,23 +341,28 @@
     tile_image, early_0 = lax.optimization_barrier((tile_image, early[0]))
     late = some_values(FIRST, count, 0, tile_image)
     more = {0: late[0]}
-    for m in (1, 3, 2, 7, 5):
+    for m in (1, 3, 2, 7, 5, 6):
         more[m] = share(m, late[m])
     known = ints(jnp.stack([g[FIRST, :3, :count] for g in got]))
+    shares = [(m, 0, FIRST) for m in range(8)] + [(m, FIRST, count - FIRST) for m in EARLY]
+    more[1], got[0], late_4 = lax.optimization_barrier((more[1], got[0], late[4]))
     value_sums = pl.pallas_call(
-        first_values_body,
-        in_specs=[smem, smem] + [hbm] * 8,
+        functools.partial(first_values_body, shares),
+        in_specs=[smem] * 3 + [hbm] * len(shares),
         out_specs=vmem,
         out_shape=mine,
-        scratch_shapes=[pltpu.VMEM((8, FIRST, 32, side), jnp.bfloat16), pltpu.SemaphoreType.DMA((8,))],
+        scratch_shapes=[
+            pltpu.VMEM((len(shares), count - FIRST, 32, side), jnp.bfloat16),
+            pltpu.SemaphoreType.DMA((len(shares),)),
+        ],
         cost_estimate=pl.CostEstimate(flops=5 * pixels, bytes_accessed=3 * pixels, transcendentals=0),
         compiler_params=pltpu.CompilerParams(vmem_limit_bytes=56 << 20),
         name="first_value_sums",
-    )(known, me, *got)
-
-    late_6, late_4, value_sums = lax.optimization_barrier((late[6], late[4], value_sums))
-    more[6], more[4] = share(6, late_6), share(4, late_4)
-    got_weights, more[1], more[3], value_sums = lax.optimization_barrier((got_weights, more[1], more[3], value_sums))
+    )(known, *place[:2], *got, *[more[m] for m in EARLY])
+
+    late_4, value_sums = lax.optimization_barrier((late_4, value_sums))
+    more[4] = share(4, late_4)
+    got_weights, value_sums = lax.optimization_barrier((got_weights, value_sums))
     weight_sums = pl.pallas_call(
         weight_sum_body,
         in_specs=[smem, smem, hbm],
@@ -361,29 +370,30 @@
         out_shape=jax.ShapeDtypeStruct((4, parts, height, side), jnp.bfloat16),
         scratch_shapes=[
             pltpu.VMEM((parts, slots, height, side), jnp.bfloat16),
-            pltpu.SemaphoreType.DMA((4,)),
+            pltpu.SemaphoreType.DMA((8,)),
             *[pltpu.VMEM((parts, 4, height, side), jnp.float32)] * 4,
         ],
         cost_estimate=pl.CostEstimate(flops=10 * pixels, bytes_accessed=3 * pixels, transcendentals=0),
         compiler_params=pltpu.CompilerParams(vmem_limit_bytes=60 << 20),
         name="weight_sums",
-    )(ints(got_weights[:, count, :3, :count]), me, got_weights)
+    )(ints(got_weights[:, count, :3, :count]), place[2], got_weights)
+    shares = [(m, FIRST, count - FIRST) for m in range(8) if m not in EARLY]
     sums = pl.pallas_call(
-        last_values_body,
-        in_specs=[smem, smem, vmem, hbm] + [hbm] * 8,
+        functools.partial(last_values_body, shares),
+        in_specs=[smem] * 3 + [vmem, hbm] + [hbm] * len(shares),
         out_specs=vmem,
         out_shape=jax.ShapeDtypeStruct((4, parts, 32 + height, side), jnp.bfloat16),
         scratch_shapes=[
-            pltpu.VMEM((8, count - FIRST, 32, side), jnp.bfloat16),
+            pltpu.VMEM((len(shares), count - FIRST, 32, side), jnp.bfloat16),
             pltpu.VMEM(mine.shape, jnp.float32),
             pltpu.VMEM(mine.shape, jnp.float32),
-            pltpu.SemaphoreType.DMA((8,)),
+            pltpu.SemaphoreType.DMA((len(shares),)),
             pltpu.SemaphoreType.DMA,
         ],
         cost_estimate=pl.CostEstimate(flops=5 * pixels, bytes_accessed=3 * pixels, transcendentals=0),
         compiler_params=pltpu.CompilerParams(vmem_limit_bytes=56 << 20),
         name="last_value_sums",
-    )(known, me, weight_sums, value_sums, *[more[m] for m in range(8)])
+    )(known, *place[:2], weight_sums, value_sums, *[more[m] for m, _, _ in shares])
 
     sums = sums.reshape(epochs * parts, 32 + height, side)
     got = lax.all_to_all(sums, ("epoch", "patch"), split_axis=0, concat_axis=0, tiled=True)

time: 141 us -> 141 us (level)
  waiting for transfers between devices: 12.2 us -> 16.4 us
  blocking collectives: 49.3 us -> 45.2 us
    ppermute x14, waiting for transfers between devices: 9.78 us -> 14.7 us  [share(): return lax.ppermute(rows, ('epoch', 'patch'), pairs)]
    all_to_all x1, blocking collectives: 49.3 us -> 45.2 us  [shards(): lax.all_to_all(sums, ('epoch', 'patch'), split_axis=0, concat_axis=0, til...]
  transfers between devices with their start and end apart: 15 -> 15, of which waited for: 4 -> 6; matrix products, arithmetic and copies ran while one was open for 3% -> 2% of each run, Pallas kernels for 24% -> 24%
where the time goes in v4:
time: 141 us; the launch traced here: 140 us
  Pallas kernels  48.2 us (34%)
  blocking collectives  45.2 us (32%)
  starting transfers between devices  25.1 us (18%)
  waiting for transfers between devices  16.4 us (12%)
  local copies, waits for them, and re-layouts  2.26 us (2%)
  other arithmetic  2.09 us (1%)
    all_to_all x1, blocking collectives, shards(): lax.all_to_all(sums, ('epoch', 'patch'), split_axis=0, concat_axis=0, til...  45.2 us
    pallas_call x2, Pallas kernels, some_values(): pl.pallas_call(functools.partial(value_body, begin, tables), grid=(steps...  19.8 us
    ppermute x14, starting transfers between devices, share(): return lax.ppermute(rows, ('epoch', 'patch'), pairs)  16.5 us
    ppermute x14, waiting for transfers between devices, share(): return lax.ppermute(rows, ('epoch', 'patch'), pairs)  14.7 us
    all_to_all x1, starting transfers between devices, shards(): lax.all_to_all(weights, 'patch', split_axis=0, concat_axis=0, tiled=True)  8.63 us
    pallas_call x1, Pallas kernels, shards(): pl.pallas_call(weight_sum_body, in_specs=[smem, smem, hbm], out_specs=vme...  7.87 us
    pallas_call x1, Pallas kernels, shards(): pl.pallas_call(weight_body, grid=(steps + 1,), in_specs=[smem, smem, tile...  7.24 us
    pallas_call x1, Pallas kernels, shards(): pl.pallas_call(functools.partial(last_values_body, shares), in_specs=[sme...  6.36 us
  transfers between devices with their start and end apart: 15, of which 6 were waited for; matrix products, arithmetic and copies ran while one was open for 2% of the time, Pallas kernels for 24%

profile of v4, /device:TPU:1, one launch (start us, length us, event | category | flops | bytes accessed | tf_op | source)
XLA Modules:
  0.0 140.1 jit_solution(832438375682262262)
XLA Ops:
  0.6 7.2 %weights.1 = bf16[32,33,8,256]{3,2,1,0:T(8,128)(2,1)} custom-call(s32[1,32]{1,0:T(1,128)} %bitcast.15, s32[2,32]{1,0:T(2,128)} %bitcast.12, bf16[32,256,256]{2,1,0:T(8,128)(2,1)} %var_ref.5), custom_call_target="tpu_custom_call" | custom-call | flops 41943040 | bytes 8388608 | tf_op jit(solution)/shard_map/weights/pallas_call | solution.py:294
  7.9 8.6 %all-to-all-start = ((bf16[32,33,8,256]{3,2,1,0:T(8,128)(2,1)}), bf16[32,33,8,256]{3,2,1,0:T(8,128)(2,1)}, u32[]{:S(2)}, u32[]{:S(2)}) async-start(bf16[32,33,8,256]{3,2,1,0:T(8,128)(2,1)} %weights.1), calls=%async_computation | async-start | bytes 8650752 | tf_op jit(solution)/shard_map/all_to_all | solution.py:334
  16.5 8.1 %values.2 = (bf16[13,32,256]{2,1,0:T(8,128)(2,1)}, bf16[13,32,256]{2,1,0:T(8,128)(2,1)}, bf16[13,32,256]{2,1,0:T(8,128)(2,1)}, bf16[13,32,256]{2,1,0:T(8,128)(2,...) custom-call(s32[1]{0:T(128)} %bitcast.z_ref, ...), custom_call_target="tpu_custom_call" | custom-call | flops 3221225472 | bytes 6291456 | tf_op jit(solution)/shard_map/values/pallas_call | solution.py:308
  24.6 1.7 %collective-permute-start = (bf16[13,32,256]{2,1,0:T(8,128)(2,1)}, bf16[13,32,256]{2,1,0:T(8,128)(2,1)S(1)}, u32[]{:S(2)}, u32[]{:S(2)}) collective-permute-start(bf16[13,32,256]{2,1,0:T(8,128)(2,1)} %get-tuple-element.30), channel_id=1, source_target_pairs={{0,32},{1,33},{2,34},{3,35},{4,36},{5,37},{6,38},{7,39},{8,40},{9,... | collective-permute-start | bytes 638984 | tf_op jit(solution)/shard_map/ppermute | solution.py:328
  26.3 3.3 %collective-permute-start.1 = (bf16[13,32,256]{2,1,0:T(8,128)(2,1)}, bf16[13,32,256]{2,1,0:T(8,128)(2,1)S(1)}, u32[]{:S(2)}, u32[]{:S(2)}) collective-permute-start(bf16[13,32,256]{2,1,0:T(8,128)(2,1)} %get-tuple-element.31), channel_id=1, source_target_pairs={{0,64},{1,65},{2,66},{3,67},{4,68},{5,69},{6,70},{7,71},{8,72},{9,... | collective-permute-start | bytes 638984 | tf_op jit(solution)/shard_map/ppermute | solution.py:328
  29.6 0.7 collective-permute-start.2
  30.4 1.1 collective-permute-start.3
  31.5 0.6 collective-permute-start.4
  32.1 0.0 copy-start.15
  32.1 11.7 %values.3 = (bf16[20,32,256]{2,1,0:T(8,128)(2,1)}, bf16[20,32,256]{2,1,0:T(8,128)(2,1)}, bf16[20,32,256]{2,1,0:T(8,128)(2,1)}, bf16[20,32,256]{2,1,0:T(8,128)(2,...) custom-call(s32[1]{0:T(128)} %bitcast.z_ref, ...), custom_call_target="tpu_custom_call" | custom-call | flops 3221225472 | bytes 6291456 | tf_op jit(solution)/shard_map/values/pallas_call | solution.py:308
  43.8 0.0 copy-start.14
  43.9 0.7 constant_dynamic-update-slice_fusion.7
  44.6 0.0 collective-permute-done.refs_1_
  44.6 0.0 copy-start.7
  44.6 0.0 copy-done.16
  44.6 0.7 collective-permute-start.5
  45.3 0.0 collective-permute-done.1.refs_2_
  45.3 0.0 copy-done.15
  45.3 2.3 %collective-permute-start.6 = (bf16[13,32,256]{2,1,0:T(8,128)(2,1)S(1)}, bf16[13,32,256]{2,1,0:T(8,128)(2,1)S(1)}, u32[]{:S(2)}, u32[]{:S(2)}) collective-permute-start(bf16[13,32,256]{2,1,0:T(8,128)(2,1)S(1)} %copy-done.15), channel_id=1, source_target_pairs={{0,97},{1,96},{2,99},{3,98},{4,101},{5,100},{6,103},{7,102},{8,105... | collective-permute-start | bytes 638984 | tf_op jit(solution)/shard_map/ppermute | solution.py:328
  47.6 0.0 collective-permute-done.2.refs_3_
  47.6 0.2 collective-permute-start.7
  47.8 0.0 collective-permute-done.3.refs_4_
  47.8 1.8 %collective-permute-start.8 = (bf16[20,32,256]{2,1,0:T(8,128)(2,1)}, bf16[20,32,256]{2,1,0:T(8,128)(2,1)S(1)}, u32[]{:S(2)}, u32[]{:S(2)}) collective-permute-start(bf16[20,32,256]{2,1,0:T(8,128)(2,1)} %get-tuple-element.48), channel_id=1, source_target_pairs={{0,64},{1,65},{2,66},{3,67},{4,68},{5,69},{6,70},{7,71},{8,72},{9,... | collective-permute-start | bytes 983048 | tf_op jit(solution)/shard_map/ppermute | solution.py:328
  49.7 0.0 collective-permute-done.4.refs_5_
  49.7 2.0 %collective-permute-start.9 = (bf16[20,32,256]{2,1,0:T(8,128)(2,1)}, bf16[20,32,256]{2,1,0:T(8,128)(2,1)S(1)}, u32[]{:S(2)}, u32[]{:S(2)}) collective-permute-start(bf16[20,32,256]{2,1,0:T(8,128)(2,1)} %get-tuple-element.49), channel_id=1, source_target_pairs={{0,96},{1,97},{2,98},{3,99},{4,100},{5,101},{6,102},{7,103},{8,104... | collective-permute-start | bytes 983048 | tf_op jit(solution)/shard_map/ppermute | solution.py:328
  51.7 2.5 %collective-permute-done.5.refs_6_ = bf16[13,32,256]{2,1,0:T(8,128)(2,1)S(1)} collective-permute-done((bf16[13,32,256]{2,1,0:T(8,128)(2,1)S(1)}, bf16[13,32,256]{2,1,0:T(8,128)(2,1)S(1)}, u32[]{:S(2)}, u32[]{:S(2)}) %collective-permute-start.5) | collective-permute-done | bytes 213024 | tf_op jit(solution)/shard_map/ppermute | solution.py:328
  54.2 0.0 collective-permute-start.11
  54.2 4.1 %collective-permute-done.6.refs_7_ = bf16[13,32,256]{2,1,0:T(8,128)(2,1)S(1)} collective-permute-done((bf16[13,32,256]{2,1,0:T(8,128)(2,1)S(1)}, bf16[13,32,256]{2,1,0:T(8,128)(2,1)S(1)}, u32[]{:S(2)}, u32[]{:S(2)}) %collective-permute-start.6) | collective-permute-done | bytes 213024 | tf_op jit(solution)/shard_map/ppermute | solution.py:328
  58.3 0.3 collective-permute-start.12
  58.6 0.6 convert_convert_fusion.known_ref
  59.2 1.8 %collective-permute-done.7.refs_0_ = bf16[20,32,256]{2,1,0:T(8,128)(2,1)S(1)} collective-permute-done((bf16[20,32,256]{2,1,0:T(8,128)(2,1)}, bf16[20,32,256]{2,1,0:T(8,128)(2,1)S(1)}, u32[]{:S(2)}, u32[]{:S(2)}) %collective-permute-start.7) | collective-permute-done | bytes 327712 | tf_op jit(solution)/shard_map/ppermute | solution.py:328
  61.0 1.1 collective-permute-start.13
  62.1 0.0 copy-done.7
  62.1 0.0 copy-done.8
  62.1 0.0 copy-done.9
  62.1 0.0 copy-done.10
  62.1 0.0 copy-done.11
  62.1 0.0 copy-done.12
  62.1 0.0 copy-done.13
  62.2 5.8 %first_value_sums.1.before_ref = f32[32,4,2,16,256]{4,3,2,1,0:T(8,128)} custom-call(s32[8,3,32]{2,1,0:T(4,128)} %convert_convert_fusion.known_ref, s32[1]{0:T(128)} %bitcast.z_ref, s32[1]{0:T(128)} %bitcast.1.core_ref, bf16[13,32,256]{2,1,0:T(8,128)(2,1)} %get-tuple-element.42.refs_0_, bf16[13,32,256]{2,1,0:T(8,128)(2,1)} %copy-done.7, ...), custom_call_target="tpu_custom_call" | custom-call | flops 10485760 | bytes 6291456 | tf_op jit(solution)/shard_map/first_value_sums/pallas_call | solution.py:349
  68.0 0.0 collective-permute-done.8.refs_1_
  68.0 0.0 copy-done.14
  68.0 0.0 copy-start.1
  68.0 0.5 collective-permute-start.10
  68.6 1.7 %all-to-all-done.got_ref = bf16[32,33,8,256]{3,2,1,0:T(8,128)(2,1)} async-done(((bf16[32,33,8,256]{3,2,1,0:T(8,128)(2,1)}), bf16[32,33,8,256]{3,2,1,0:T(8,128)(2,1)}, u32[]{:S(2)}, u32[]{:S(2)}) %all-to-all-start) | async-done | bytes 4325408 | tf_op jit(solution)/shard_map/all_to_all | solution.py:334
  70.3 1.5 %convert_bitcast_fusion.known_ref = s32[32,3,32]{2,1,0:T(4,128)} fusion(bf16[32,33,8,256]{3,2,1,0:T(8,128)(2,1)} %all-to-all-done.got_ref), kind=kLoop, calls=%fused_computation | loop fusion | flops 6144 | bytes 18432 | tf_op jit(solution)/shard_map/convert_element_type | solution.py:330
  71.8 7.9 %weight_sums.1.weight_ref = bf16[4,32,8,256]{3,2,1,0:T(8,128)(2,1)} custom-call(s32[32,3,32]{2,1,0:T(4,128)} %convert_bitcast_fusion.known_ref, s32[1]{0:T(128)} %bitcast.6.part_ref, bf16[32,33,8,256]{3,2,1,0:T(8,128)(2,1)} %all-to-all-done.got_ref), custom_call_target="tpu_custom_call" | custom-call | flops 20971520 | bytes 6291456 | tf_op jit(solution)/shard_map/weight_sums/pallas_call | solution.py:366
  79.7 0.0 copy-done
  79.7 0.0 collective-permute-done.9.refs_2_
  79.7 0.0 copy-start.2
  79.7 0.0 collective-permute-done.11.refs_4_
  79.7 0.0 copy-start.3
  79.7 2.1 %collective-permute-done.12.refs_5_ = bf16[20,32,256]{2,1,0:T(8,128)(2,1)S(1)} collective-permute-done((bf16[20,32,256]{2,1,0:T(8,128)(2,1)}, bf16[20,32,256]{2,1,0:T(8,128)(2,1)S(1)}, u32[]{:S(2)}, u32[]{:S(2)}) %collective-permute-start.12) | collective-permute-done | bytes 327712 | tf_op jit(solution)/shard_map/ppermute | solution.py:328
  81.8 4.2 %collective-permute-done.13.refs_6_ = bf16[20,32,256]{2,1,0:T(8,128)(2,1)S(1)} collective-permute-done((bf16[20,32,256]{2,1,0:T(8,128)(2,1)}, bf16[20,32,256]{2,1,0:T(8,128)(2,1)S(1)}, u32[]{:S(2)}, u32[]{:S(2)}) %collective-permute-start.13) | collective-permute-done | bytes 327712 | tf_op jit(solution)/shard_map/ppermute | solution.py:328
  86.0 0.0 collective-permute-done.10.refs_3_
  86.0 0.0 copy-done.1
  86.0 0.0 copy-done.2
  86.0 0.0 copy-done.3
  86.0 0.0 copy-done.4
  86.1 0.7 copy-done.5
  86.7 0.7 copy-done.6
  87.5 6.4 %last_value_sums.1 = bf16[4,32,40,256]{3,2,1,0:T(8,128)(2,1)} custom-call(s32[8,3,32]{2,1,0:T(4,128)} %convert_convert_fusion.known_ref, s32[1]{0:T(128)} %bitcast.z_ref, s32[1]{0:T(128)} %bitcast.1.core_ref, bf16[4,32,8,256]{3,2,1,0:T(8,128)(2,1)} %weight_sums.1.weight_ref, f32[32,4,2,16,256]{4,3,2,1,0:T(8,128)} %first_value_sums.1.before_ref, ...), custom_call_target="tpu_custom_call" | custom-call | flops 10485760 | bytes 6291456 | tf_op jit(solution)/shard_map/last_value_sums/pallas_call | solution.py:381
  93.8 45.2 %all_to_all.10 = bf16[128,40,256]{2,1,0:T(8,128)(2,1)S(1)} all-to-all(bf16[128,40,256]{2,1,0:T(8,128)(2,1)} %bitcast.11), channel_id=1, replica_groups=mesh['epoch'=4,'patch'=32] {'epoch','patch'}, dimensions={0} | all-to-all | bytes 5242880 | tf_op jit(solution)/shard_map/all_to_all | solution.py:399
  139.0 1.1 final.1
  (18 shorter events, 0.1 us)
Async XLA Ops:
  7.9 62.4 %all-to-all-start = ((bf16[32,33,8,256]{3,2,1,0:T(8,128)(2,1)}), bf16[32,33,8,256]{3,2,1,0:T(8,128)(2,1)}, u32[]{:S(2)}, u32[]{:S(2)}) async-start(bf16[32,33,8,256]{3,2,1,0:T(8,128)(2,1)} %weights.1), calls=%async_computation | async-start | bytes 8650752 | tf_op jit(solution)/shard_map/all_to_all | solution.py:334
  24.6 19.9 %collective-permute-start = (bf16[13,32,256]{2,1,0:T(8,128)(2,1)}, bf16[13,32,256]{2,1,0:T(8,128)(2,1)S(1)}, u32[]{:S(2)}, u32[]{:S(2)}) collective-permute-start(bf16[13,32,256]{2,1,0:T(8,128)(2,1)} %get-tuple-element.30), channel_id=1, source_target_pairs={{0,32},{1,33},{2,34},{3,35},{4,36},{5,37},{6,38},{7,39},{8,40},{9,... | collective-permute-start | bytes 638984 | tf_op jit(solution)/shard_map/ppermute | solution.py:328
  26.3 18.9 %collective-permute-start.1 = (bf16[13,32,256]{2,1,0:T(8,128)(2,1)}, bf16[13,32,256]{2,1,0:T(8,128)(2,1)S(1)}, u32[]{:S(2)}, u32[]{:S(2)}) collective-permute-start(bf16[13,32,256]{2,1,0:T(8,128)(2,1)} %get-tuple-element.31), channel_id=1, source_target_pairs={{0,64},{1,65},{2,66},{3,67},{4,68},{5,69},{6,70},{7,71},{8,72},{9,... | collective-permute-start | bytes 638984 | tf_op jit(solution)/shard_map/ppermute | solution.py:328
  29.6 17.9 %collective-permute-start.2 = (bf16[13,32,256]{2,1,0:T(8,128)(2,1)}, bf16[13,32,256]{2,1,0:T(8,128)(2,1)S(1)}, u32[]{:S(2)}, u32[]{:S(2)}) collective-permute-start(bf16[13,32,256]{2,1,0:T(8,128)(2,1)} %get-tuple-element.32), channel_id=1, source_target_pairs={{0,96},{1,97},{2,98},{3,99},{4,100},{5,101},{6,102},{7,103},{8,104... | collective-permute-start | bytes 638984 | tf_op jit(solution)/shard_map/ppermute | solution.py:328
  30.4 17.4 %collective-permute-start.3 = (bf16[13,32,256]{2,1,0:T(8,128)(2,1)}, bf16[13,32,256]{2,1,0:T(8,128)(2,1)S(1)}, u32[]{:S(2)}, u32[]{:S(2)}) collective-permute-start(bf16[13,32,256]{2,1,0:T(8,128)(2,1)} %get-tuple-element.33), channel_id=1, source_target_pairs={{0,1},{1,0},{2,3},{3,2},{4,5},{5,4},{6,7},{7,6},{8,9},{9,8},{10,11... | collective-permute-start | bytes 638984 | tf_op jit(solution)/shard_map/ppermute | solution.py:328
  31.5 18.1 %collective-permute-start.4 = (bf16[13,32,256]{2,1,0:T(8,128)(2,1)}, bf16[13,32,256]{2,1,0:T(8,128)(2,1)S(1)}, u32[]{:S(2)}, u32[]{:S(2)}) collective-permute-start(bf16[13,32,256]{2,1,0:T(8,128)(2,1)} %get-tuple-element.34), channel_id=1, source_target_pairs={{0,33},{1,32},{2,35},{3,34},{4,37},{5,36},{6,39},{7,38},{8,41},{9,... | collective-permute-start | bytes 638984 | tf_op jit(solution)/shard_map/ppermute | solution.py:328
  32.1 12.5 %copy-start.16 = (bf16[13,32,256]{2,1,0:T(8,128)(2,1)S(1)}, bf16[13,32,256]{2,1,0:T(8,128)(2,1)}, u32[]{:S(2)}) copy-start(bf16[13,32,256]{2,1,0:T(8,128)(2,1)} %get-tuple-element.35) | copy-start | bytes 638980
  32.1 13.1 %copy-start.15 = (bf16[13,32,256]{2,1,0:T(8,128)(2,1)S(1)}, bf16[13,32,256]{2,1,0:T(8,128)(2,1)}, u32[]{:S(2)}) copy-start(bf16[13,32,256]{2,1,0:T(8,128)(2,1)} %get-tuple-element.36) | copy-start | bytes 638980
  43.8 24.2 %copy-start.14 = (bf16[20,32,256]{2,1,0:T(8,128)(2,1)S(1)}, bf16[20,32,256]{2,1,0:T(8,128)(2,1)}, u32[]{:S(2)}) copy-start(bf16[20,32,256]{2,1,0:T(8,128)(2,1)} %get-tuple-element.50) | copy-start | bytes 983044
  44.6 17.5 %copy-start.7 = (bf16[13,32,256]{2,1,0:T(8,128)(2,1)}, bf16[13,32,256]{2,1,0:T(8,128)(2,1)S(1)}, u32[]{:S(2)}) copy-start(bf16[13,32,256]{2,1,0:T(8,128)(2,1)S(1)} %collective-permute-done.refs_1_) | copy-start | bytes 638980
  44.6 9.6 %collective-permute-start.5 = (bf16[13,32,256]{2,1,0:T(8,128)(2,1)S(1)}, bf16[13,32,256]{2,1,0:T(8,128)(2,1)S(1)}, u32[]{:S(2)}, u32[]{:S(2)}) collective-permute-start(bf16[13,32,256]{2,1,0:T(8,128)(2,1)S(1)} %copy-done.16), channel_id=1, source_target_pairs={{0,65},{1,64},{2,67},{3,66},{4,69},{5,68},{6,71},{7,70},{8,73},{9,... | collective-permute-start | bytes 638984 | tf_op jit(solution)/shard_map/ppermute | solution.py:328
  45.3 16.9 %copy-start.8 = (bf16[13,32,256]{2,1,0:T(8,128)(2,1)}, bf16[13,32,256]{2,1,0:T(8,128)(2,1)S(1)}, u32[]{:S(2)}) copy-start(bf16[13,32,256]{2,1,0:T(8,128)(2,1)S(1)} %collective-permute-done.1.refs_2_) | copy-start | bytes 638980
  45.3 13.0 %collective-permute-start.6 = (bf16[13,32,256]{2,1,0:T(8,128)(2,1)S(1)}, bf16[13,32,256]{2,1,0:T(8,128)(2,1)S(1)}, u32[]{:S(2)}, u32[]{:S(2)}) collective-permute-start(bf16[13,32,256]{2,1,0:T(8,128)(2,1)S(1)} %copy-done.15), channel_id=1, source_target_pairs={{0,97},{1,96},{2,99},{3,98},{4,101},{5,100},{6,103},{7,102},{8,105... | collective-permute-start | bytes 638984 | tf_op jit(solution)/shard_map/ppermute | solution.py:328
  47.6 14.5 %copy-start.9 = (bf16[13,32,256]{2,1,0:T(8,128)(2,1)}, bf16[13,32,256]{2,1,0:T(8,128)(2,1)S(1)}, u32[]{:S(2)}) copy-start(bf16[13,32,256]{2,1,0:T(8,128)(2,1)S(1)} %collective-permute-done.2.refs_3_) | copy-start | bytes 638980
  47.6 13.4 %collective-permute-start.7 = (bf16[20,32,256]{2,1,0:T(8,128)(2,1)}, bf16[20,32,256]{2,1,0:T(8,128)(2,1)S(1)}, u32[]{:S(2)}, u32[]{:S(2)}) collective-permute-start(bf16[20,32,256]{2,1,0:T(8,128)(2,1)} %get-tuple-element.39), channel_id=1, source_target_pairs={{0,32},{1,33},{2,34},{3,35},{4,36},{5,37},{6,38},{7,39},{8,40},{9,... | collective-permute-start | bytes 983048 | tf_op jit(solution)/shard_map/ppermute | solution.py:328
  47.8 14.3 %copy-start.10 = (bf16[13,32,256]{2,1,0:T(8,128)(2,1)}, bf16[13,32,256]{2,1,0:T(8,128)(2,1)S(1)}, u32[]{:S(2)}) copy-start(bf16[13,32,256]{2,1,0:T(8,128)(2,1)S(1)} %collective-permute-done.3.refs_4_) | copy-start | bytes 638980
  47.8 20.2 %collective-permute-start.8 = (bf16[20,32,256]{2,1,0:T(8,128)(2,1)}, bf16[20,32,256]{2,1,0:T(8,128)(2,1)S(1)}, u32[]{:S(2)}, u32[]{:S(2)}) collective-permute-start(bf16[20,32,256]{2,1,0:T(8,128)(2,1)} %get-tuple-element.48), channel_id=1, source_target_pairs={{0,64},{1,65},{2,66},{3,67},{4,68},{5,69},{6,70},{7,71},{8,72},{9,... | collective-permute-start | bytes 983048 | tf_op jit(solution)/shard_map/ppermute | solution.py:328
  49.7 12.5 %copy-start.11 = (bf16[13,32,256]{2,1,0:T(8,128)(2,1)}, bf16[13,32,256]{2,1,0:T(8,128)(2,1)S(1)}, u32[]{:S(2)}) copy-start(bf16[13,32,256]{2,1,0:T(8,128)(2,1)S(1)} %collective-permute-done.4.refs_5_) | copy-start | bytes 638980
  49.7 30.0 %collective-permute-start.9 = (bf16[20,32,256]{2,1,0:T(8,128)(2,1)}, bf16[20,32,256]{2,1,0:T(8,128)(2,1)S(1)}, u32[]{:S(2)}, u32[]{:S(2)}) collective-permute-start(bf16[20,32,256]{2,1,0:T(8,128)(2,1)} %get-tuple-element.49), channel_id=1, source_target_pairs={{0,96},{1,97},{2,98},{3,99},{4,100},{5,101},{6,102},{7,103},{8,104... | collective-permute-start | bytes 983048 | tf_op jit(solution)/shard_map/ppermute | solution.py:328
  54.2 8.0 %copy-start.12 = (bf16[13,32,256]{2,1,0:T(8,128)(2,1)}, bf16[13,32,256]{2,1,0:T(8,128)(2,1)S(1)}, u32[]{:S(2)}) copy-start(bf16[13,32,256]{2,1,0:T(8,128)(2,1)S(1)} %collective-permute-done.5.refs_6_) | copy-start | bytes 638980
  54.2 25.5 %collective-permute-start.11 = (bf16[20,32,256]{2,1,0:T(8,128)(2,1)}, bf16[20,32,256]{2,1,0:T(8,128)(2,1)S(1)}, u32[]{:S(2)}, u32[]{:S(2)}) collective-permute-start(bf16[20,32,256]{2,1,0:T(8,128)(2,1)} %get-tuple-element.51), channel_id=1, source_target_pairs={{0,33},{1,32},{2,35},{3,34},{4,37},{5,36},{6,39},{7,38},{8,41},{9,... | collective-permute-start | bytes 983048 | tf_op jit(solution)/shard_map/ppermute | solution.py:328
  58.3 3.9 %copy-start.13 = (bf16[13,32,256]{2,1,0:T(8,128)(2,1)}, bf16[13,32,256]{2,1,0:T(8,128)(2,1)S(1)}, u32[]{:S(2)}) copy-start(bf16[13,32,256]{2,1,0:T(8,128)(2,1)S(1)} %collective-permute-done.6.refs_7_) | copy-start | bytes 638980
  58.3 23.5 %collective-permute-start.12 = (bf16[20,32,256]{2,1,0:T(8,128)(2,1)}, bf16[20,32,256]{2,1,0:T(8,128)(2,1)S(1)}, u32[]{:S(2)}, u32[]{:S(2)}) collective-permute-start(bf16[20,32,256]{2,1,0:T(8,128)(2,1)} %get-tuple-element.52), channel_id=1, source_target_pairs={{0,65},{1,64},{2,67},{3,66},{4,69},{5,68},{6,71},{7,70},{8,73},{9,... | collective-permute-start | bytes 983048 | tf_op jit(solution)/shard_map/ppermute | solution.py:328
  61.0 18.7 %copy-start = (bf16[20,32,256]{2,1,0:T(8,128)(2,1)}, bf16[20,32,256]{2,1,0:T(8,128)(2,1)S(1)}, u32[]{:S(2)}) copy-start(bf16[20,32,256]{2,1,0:T(8,128)(2,1)S(1)} %collective-permute-done.7.refs_0_) | copy-start | bytes 983044
  61.0 25.0 %collective-permute-start.13 = (bf16[20,32,256]{2,1,0:T(8,128)(2,1)}, bf16[20,32,256]{2,1,0:T(8,128)(2,1)S(1)}, u32[]{:S(2)}, u32[]{:S(2)}) collective-permute-start(bf16[20,32,256]{2,1,0:T(8,128)(2,1)} %get-tuple-element.53), channel_id=1, source_target_pairs={{0,97},{1,96},{2,99},{3,98},{4,101},{5,100},{6,103},{7,102},{8,105... | collective-permute-start | bytes 983048 | tf_op jit(solution)/shard_map/ppermute | solution.py:328
  68.0 18.0 %copy-start.1 = (bf16[20,32,256]{2,1,0:T(8,128)(2,1)}, bf16[20,32,256]{2,1,0:T(8,128)(2,1)S(1)}, u32[]{:S(2)}) copy-start(bf16[20,32,256]{2,1,0:T(8,128)(2,1)S(1)} %collective-permute-done.8.refs_1_) | copy-start | bytes 983044
  68.0 18.0 %collective-permute-start.10 = (bf16[20,32,256]{2,1,0:T(8,128)(2,1)S(1)}, bf16[20,32,256]{2,1,0:T(8,128)(2,1)S(1)}, u32[]{:S(2)}, u32[]{:S(2)}) collective-permute-start(bf16[20,32,256]{2,1,0:T(8,128)(2,1)S(1)} %copy-done.14), channel_id=1, source_target_pairs={{0,1},{1,0},{2,3},{3,2},{4,5},{5,4},{6,7},{7,6},{8,9},{9,8},{10,11... | collective-permute-start | bytes 983048 | tf_op jit(solution)/shard_map/ppermute | solution.py:328
  79.7 6.3 %copy-start.2 = (bf16[20,32,256]{2,1,0:T(8,128)(2,1)}, bf16[20,32,256]{2,1,0:T(8,128)(2,1)S(1)}, u32[]{:S(2)}) copy-start(bf16[20,32,256]{2,1,0:T(8,128)(2,1)S(1)} %collective-permute-done.9.refs_2_) | copy-start | bytes 983044
  79.7 6.3 %copy-start.3 = (bf16[20,32,256]{2,1,0:T(8,128)(2,1)}, bf16[20,32,256]{2,1,0:T(8,128)(2,1)S(1)}, u32[]{:S(2)}) copy-start(bf16[20,32,256]{2,1,0:T(8,128)(2,1)S(1)} %collective-permute-done.11.refs_4_) | copy-start | bytes 983044
  81.8 4.2 %copy-start.4 = (bf16[20,32,256]{2,1,0:T(8,128)(2,1)}, bf16[20,32,256]{2,1,0:T(8,128)(2,1)S(1)}, u32[]{:S(2)}) copy-start(bf16[20,32,256]{2,1,0:T(8,128)(2,1)S(1)} %collective-permute-done.12.refs_5_) | copy-start | bytes 983044
  86.0 0.7 copy-start.5
  86.7 0.7 copy-start.6

commit v5 on v4

--- a/solution.py
+++ b/solution.py
@@ -232,18 +232,23 @@
     add_values(known_ref, z_ref, core_ref, shares, got, data_ref, out_ref, sems)
 
 
-def last_values_body(shares, known_ref, z_ref, core_ref, weight_ref, before_ref, *refs):
-    got, (out_ref, data_ref, first_ref, sums_ref, sems, first_sem) = refs[: len(shares)], refs[len(shares) :]
+def last_values_body(shares, known_ref, z_ref, core_ref, weight_ref, before_ref, middle_ref, *refs):
+    got, (out_ref, data_ref, first_ref, second_ref, sums_ref, sems, before_sems) = refs[: len(shares)], refs[len(shares) :]
     band = sums_ref.shape[3]
-    earlier = pltpu.make_async_copy(before_ref, first_ref, first_sem)
-    earlier.start()
+    earlier = [
+        pltpu.make_async_copy(before_ref, first_ref, before_sems.at[0]),
+        pltpu.make_async_copy(middle_ref, second_ref, before_sems.at[1]),
+    ]
+    for copy in earlier:
+        copy.start()
     add_values(known_ref, z_ref, core_ref, shares, got, data_ref, sums_ref, sems)
-    earlier.wait()
+    for copy in earlier:
+        copy.wait()
 
     def one_patch(p, unused):
         for quarter in range(4):
             for h in range(2):
-                both = sums_ref[p, quarter, h] + first_ref[p, quarter, h]
+                both = sums_ref[p, quarter, h] + first_ref[p, quarter, h] + second_ref[p, quarter, h]
                 out_ref[quarter, p, h * band : (h + 1) * band] = both.astype(jnp.bfloat16)
             out_ref[quarter, p, 2 * band :] = weight_ref[quarter, p]
         return unused
@@ -346,19 +351,22 @@
     known = ints(jnp.stack([g[FIRST, :3, :count] for g in got]))
     shares = [(m, 0, FIRST) for m in range(8)] + [(m, FIRST, count - FIRST) for m in EARLY]
     more[1], got[0], late_4 = lax.optimization_barrier((more[1], got[0], late[4]))
-    value_sums = pl.pallas_call(
-        functools.partial(first_values_body, shares),
-        in_specs=[smem] * 3 + [hbm] * len(shares),
-        out_specs=vmem,
-        out_shape=mine,
-        scratch_shapes=[
-            pltpu.VMEM((len(shares), count - FIRST, 32, side), jnp.bfloat16),
-            pltpu.SemaphoreType.DMA((len(shares),)),
-        ],
-        cost_estimate=pl.CostEstimate(flops=5 * pixels, bytes_accessed=3 * pixels, transcendentals=0),
-        compiler_params=pltpu.CompilerParams(vmem_limit_bytes=56 << 20),
-        name="first_value_sums",
-    )(known, *place[:2], *got, *[more[m] for m in EARLY])
+    def some_sums(shares, rows):
+        return pl.pallas_call(
+            functools.partial(first_values_body, shares),
+            in_specs=[smem] * 3 + [hbm] * len(shares),
+            out_specs=vmem,
+            out_shape=mine,
+            scratch_shapes=[
+                pltpu.VMEM((len(shares), count - FIRST, 32, side), jnp.bfloat16),
+                pltpu.SemaphoreType.DMA((len(shares),)),
+            ],
+            cost_estimate=pl.CostEstimate(flops=5 * pixels, bytes_accessed=3 * pixels, transcendentals=0),
+            compiler_params=pltpu.CompilerParams(vmem_limit_bytes=56 << 20),
+            name="value_sums",
+        )(known, *place[:2], *rows)
+
+    value_sums = some_sums(shares, [*got, *[more[m] for m in EARLY]])
 
     late_4, value_sums = lax.optimization_barrier((late_4, value_sums))
     more[4] = share(4, late_4)
@@ -377,23 +385,26 @@
         compiler_params=pltpu.CompilerParams(vmem_limit_bytes=60 << 20),
         name="weight_sums",
     )(ints(got_weights[:, count, :3, :count]), place[2], got_weights)
-    shares = [(m, FIRST, count - FIRST) for m in range(8) if m not in EARLY]
+    middle = (1, 3, 2, 7, 5)
+    later = {m: more[m] for m in middle}
+    later[1], weight_sums = lax.optimization_barrier((later[1], weight_sums))
+    middle_sums = some_sums([(m, FIRST, count - FIRST) for m in middle], [later[m] for m in middle])
+    shares = [(m, FIRST, count - FIRST) for m in (4, 6)]
     sums = pl.pallas_call(
         functools.partial(last_values_body, shares),
-        in_specs=[smem] * 3 + [vmem, hbm] + [hbm] * len(shares),
+        in_specs=[smem] * 3 + [vmem, hbm, hbm] + [hbm] * len(shares),
         out_specs=vmem,
         out_shape=jax.ShapeDtypeStruct((4, parts, 32 + height, side), jnp.bfloat16),
         scratch_shapes=[
             pltpu.VMEM((len(shares), count - FIRST, 32, side), jnp.bfloat16),
-            pltpu.VMEM(mine.shape, jnp.float32),
-            pltpu.VMEM(mine.shape, jnp.float32),
+            *[pltpu.VMEM(mine.shape, jnp.float32)] * 3,
             pltpu.SemaphoreType.DMA((len(shares),)),
-            pltpu.SemaphoreType.DMA,
+            pltpu.SemaphoreType.DMA((2,)),
         ],
         cost_estimate=pl.CostEstimate(flops=5 * pixels, bytes_accessed=3 * pixels, transcendentals=0),
         compiler_params=pltpu.CompilerParams(vmem_limit_bytes=56 << 20),
         name="last_value_sums",
-    )(known, *place[:2], weight_sums, value_sums, *[more[m] for m, _, _ in shares])
+    )(known, *place[:2], weight_sums, value_sums, middle_sums, *[more[m] for m, _, _ in shares])
 
     sums = sums.reshape(epochs * parts, 32 + height, side)
     got = lax.all_to_all(sums, ("epoch", "patch"), split_axis=0, concat_axis=0, tiled=True)

time: 141 us -> 144 us (1.021)
  waiting for transfers between devices: 16.4 us -> 8.73 us
  Pallas kernels: 48.2 us -> 54.5 us
  local copies, waits for them, and re-layouts: 2.26 us -> 3.87 us
    ppermute x14, waiting for transfers between devices: 14.7 us -> 7.42 us  [share(): return lax.ppermute(rows, ('epoch', 'patch'), pairs)]
    pallas_call x1 -> x2, Pallas kernels: 5.83 us -> 11.3 us  [some_sums(): pl.pallas_call(functools.partial(first_values_body, shares), in_specs=[sm...]
    unnamed x41, local copies, waits for them, and re-layouts: 2.25 us -> 3.86 us
  transfers between devices with their start and end apart: 15 -> 15, of which waited for: 6 -> 4; matrix products, arithmetic and copies ran while one was open for 2% -> 2% of each run, Pallas kernels for 24% -> 27%
where the time goes in v5:
time: 144 us; the launch traced here: 143 us
  Pallas kernels  54.5 us (38%)
  blocking collectives  46.3 us (32%)
  starting transfers between devices  26.5 us (18%)
  waiting for transfers between devices  8.73 us (6%)
  local copies, waits for them, and re-layouts  3.87 us (3%)
  other arithmetic  2.1 us (1%)
    all_to_all x1, blocking collectives, shards(): lax.all_to_all(sums, ('epoch', 'patch'), split_axis=0, concat_axis=0, til...  46.3 us
    pallas_call x2, Pallas kernels, some_values(): pl.pallas_call(functools.partial(value_body, begin, tables), grid=(steps...  19.8 us
    ppermute x14, starting transfers between devices, share(): return lax.ppermute(rows, ('epoch', 'patch'), pairs)  17.9 us
    pallas_call x2, Pallas kernels, some_sums(): pl.pallas_call(functools.partial(first_values_body, shares), in_specs=[sm...  11.3 us
    all_to_all x1, starting transfers between devices, shards(): lax.all_to_all(weights, 'patch', split_axis=0, concat_axis=0, tiled=True)  8.63 us
    pallas_call x1, Pallas kernels, shards(): pl.pallas_call(weight_sum_body, in_specs=[smem, smem, hbm], out_specs=vme...  7.86 us
    ppermute x14, waiting for transfers between devices, share(): return lax.ppermute(rows, ('epoch', 'patch'), pairs)  7.42 us
    pallas_call x1, Pallas kernels, shards(): pl.pallas_call(weight_body, grid=(steps + 1,), in_specs=[smem, smem, tile...  7.24 us
  transfers between devices with their start and end apart: 15, of which 4 were waited for; matrix products, arithmetic and copies ran while one was open for 2% of the time, Pallas kernels for 27%

profile of v5, /device:TPU:1, one launch (start us, length us, event | category | flops | bytes accessed | tf_op | source)
XLA Modules:
  0.0 142.8 jit_solution(15419818830089608644)
XLA Ops:
  0.6 7.2 %weights.1 = bf16[32,33,8,256]{3,2,1,0:T(8,128)(2,1)} custom-call(s32[1,32]{1,0:T(1,128)} %bitcast.15, s32[2,32]{1,0:T(2,128)} %bitcast.12, bf16[32,256,256]{2,1,0:T(8,128)(2,1)} %var_ref.5), custom_call_target="tpu_custom_call" | custom-call | flops 41943040 | bytes 8388608 | tf_op jit(solution)/shard_map/weights/pallas_call | solution.py:299
  7.9 8.6 %all-to-all-start = ((bf16[32,33,8,256]{3,2,1,0:T(8,128)(2,1)}), bf16[32,33,8,256]{3,2,1,0:T(8,128)(2,1)}, u32[]{:S(2)}, u32[]{:S(2)}) async-start(bf16[32,33,8,256]{3,2,1,0:T(8,128)(2,1)} %weights.1), calls=%async_computation | async-start | bytes 8650752 | tf_op jit(solution)/shard_map/all_to_all | solution.py:339
  16.5 8.1 %values.2 = (bf16[13,32,256]{2,1,0:T(8,128)(2,1)}, bf16[13,32,256]{2,1,0:T(8,128)(2,1)}, bf16[13,32,256]{2,1,0:T(8,128)(2,1)}, bf16[13,32,256]{2,1,0:T(8,128)(2,...) custom-call(s32[1]{0:T(128)} %bitcast.z_ref, ...), custom_call_target="tpu_custom_call" | custom-call | flops 3221225472 | bytes 6291456 | tf_op jit(solution)/shard_map/values/pallas_call | solution.py:313
  24.6 1.7 %collective-permute-start = (bf16[13,32,256]{2,1,0:T(8,128)(2,1)}, bf16[13,32,256]{2,1,0:T(8,128)(2,1)S(1)}, u32[]{:S(2)}, u32[]{:S(2)}) collective-permute-start(bf16[13,32,256]{2,1,0:T(8,128)(2,1)} %get-tuple-element.32), channel_id=1, source_target_pairs={{0,32},{1,33},{2,34},{3,35},{4,36},{5,37},{6,38},{7,39},{8,40},{9,... | collective-permute-start | bytes 638984 | tf_op jit(solution)/shard_map/ppermute | solution.py:333
  26.3 3.3 %collective-permute-start.1 = (bf16[13,32,256]{2,1,0:T(8,128)(2,1)}, bf16[13,32,256]{2,1,0:T(8,128)(2,1)S(1)}, u32[]{:S(2)}, u32[]{:S(2)}) collective-permute-start(bf16[13,32,256]{2,1,0:T(8,128)(2,1)} %get-tuple-element.33), channel_id=1, source_target_pairs={{0,64},{1,65},{2,66},{3,67},{4,68},{5,69},{6,70},{7,71},{8,72},{9,... | collective-permute-start | bytes 638984 | tf_op jit(solution)/shard_map/ppermute | solution.py:333
  29.6 0.7 collective-permute-start.2
  30.4 1.2 collective-permute-start.3
  31.5 0.6 collective-permute-start.4
  32.1 11.7 %values.3 = (bf16[20,32,256]{2,1,0:T(8,128)(2,1)}, bf16[20,32,256]{2,1,0:T(8,128)(2,1)}, bf16[20,32,256]{2,1,0:T(8,128)(2,1)}, bf16[20,32,256]{2,1,0:T(8,128)(2,...) custom-call(s32[1]{0:T(128)} %bitcast.z_ref, ...), custom_call_target="tpu_custom_call" | custom-call | flops 3221225472 | bytes 6291456 | tf_op jit(solution)/shard_map/values/pallas_call | solution.py:313
  43.8 0.0 copy-start.14
  43.8 0.7 constant_dynamic-update-slice_fusion.7
  44.6 0.0 collective-permute-done.refs_1_
  44.6 0.0 copy-done.16
  44.6 0.7 collective-permute-start.5
  45.3 0.0 collective-permute-done.1.refs_2_
  45.3 0.0 copy-done.15
  45.3 2.3 %collective-permute-start.6 = (bf16[13,32,256]{2,1,0:T(8,128)(2,1)S(1)}, bf16[13,32,256]{2,1,0:T(8,128)(2,1)S(1)}, u32[]{:S(2)}, u32[]{:S(2)}) collective-permute-start(bf16[13,32,256]{2,1,0:T(8,128)(2,1)S(1)} %copy-done.15), channel_id=1, source_target_pairs={{0,97},{1,96},{2,99},{3,98},{4,101},{5,100},{6,103},{7,102},{8,105... | collective-permute-start | bytes 638984 | tf_op jit(solution)/shard_map/ppermute | solution.py:333
  47.6 0.0 collective-permute-done.2.refs_3_
  47.6 0.2 collective-permute-start.7
  47.8 0.0 collective-permute-done.3.refs_4_
  47.8 2.6 %collective-permute-start.8 = (bf16[20,32,256]{2,1,0:T(8,128)(2,1)}, bf16[20,32,256]{2,1,0:T(8,128)(2,1)S(1)}, u32[]{:S(2)}, u32[]{:S(2)}) collective-permute-start(bf16[20,32,256]{2,1,0:T(8,128)(2,1)} %get-tuple-element.52), channel_id=1, source_target_pairs={{0,96},{1,97},{2,98},{3,99},{4,100},{5,101},{6,102},{7,103},{8,104... | collective-permute-start | bytes 983048 | tf_op jit(solution)/shard_map/ppermute | solution.py:333
  50.5 0.0 collective-permute-done.4.refs_5_
  50.5 0.6 collective-permute-start.9
  51.1 3.1 %collective-permute-done.5.refs_6_ = bf16[13,32,256]{2,1,0:T(8,128)(2,1)S(1)} collective-permute-done((bf16[13,32,256]{2,1,0:T(8,128)(2,1)S(1)}, bf16[13,32,256]{2,1,0:T(8,128)(2,1)S(1)}, u32[]{:S(2)}, u32[]{:S(2)}) %collective-permute-start.5) | collective-permute-done | bytes 213024 | tf_op jit(solution)/shard_map/ppermute | solution.py:333
  54.2 1.8 %collective-permute-start.10 = (bf16[20,32,256]{2,1,0:T(8,128)(2,1)}, bf16[20,32,256]{2,1,0:T(8,128)(2,1)S(1)}, u32[]{:S(2)}, u32[]{:S(2)}) collective-permute-start(bf16[20,32,256]{2,1,0:T(8,128)(2,1)} %get-tuple-element.54), channel_id=1, source_target_pairs={{0,97},{1,96},{2,99},{3,98},{4,101},{5,100},{6,103},{7,102},{8,105... | collective-permute-start | bytes 983048 | tf_op jit(solution)/shard_map/ppermute | solution.py:333
  56.0 2.3 %collective-permute-done.6.refs_7_ = bf16[13,32,256]{2,1,0:T(8,128)(2,1)S(1)} collective-permute-done((bf16[13,32,256]{2,1,0:T(8,128)(2,1)S(1)}, bf16[13,32,256]{2,1,0:T(8,128)(2,1)S(1)}, u32[]{:S(2)}, u32[]{:S(2)}) %collective-permute-start.6) | collective-permute-done | bytes 213024 | tf_op jit(solution)/shard_map/ppermute | solution.py:333
  58.3 0.0 collective-permute-start.11
  58.4 0.6 convert_convert_fusion.known_ref
  59.0 2.0 %collective-permute-done.7.refs_0_ = bf16[20,32,256]{2,1,0:T(8,128)(2,1)S(1)} collective-permute-done((bf16[20,32,256]{2,1,0:T(8,128)(2,1)}, bf16[20,32,256]{2,1,0:T(8,128)(2,1)S(1)}, u32[]{:S(2)}, u32[]{:S(2)}) %collective-permute-start.7) | collective-permute-done | bytes 327712 | tf_op jit(solution)/shard_map/ppermute | solution.py:333
  61.0 1.6 %collective-permute-start.13 = (bf16[20,32,256]{2,1,0:T(8,128)(2,1)}, bf16[20,32,256]{2,1,0:T(8,128)(2,1)S(1)}, u32[]{:S(2)}, u32[]{:S(2)}) collective-permute-start(bf16[20,32,256]{2,1,0:T(8,128)(2,1)} %get-tuple-element.57), channel_id=1, source_target_pairs={{0,65},{1,64},{2,67},{3,66},{4,69},{5,68},{6,71},{7,70},{8,73},{9,... | collective-permute-start | bytes 983048 | tf_op jit(solution)/shard_map/ppermute | solution.py:333
  62.6 0.0 copy-done.7
  62.6 0.0 copy-done.8
  62.6 0.0 copy-done.9
  62.6 0.0 copy-done.10
  62.6 0.0 copy-done.11
  62.6 0.0 copy-done.12
  62.6 0.0 copy-done.13
  62.6 5.8 %value_sums.2.before_ref = f32[32,4,2,16,256]{4,3,2,1,0:T(8,128)} custom-call(s32[8,3,32]{2,1,0:T(4,128)} %convert_convert_fusion.known_ref, s32[1]{0:T(128)} %bitcast.z_ref, s32[1]{0:T(128)} %bitcast.1.core_ref, bf16[13,32,256]{2,1,0:T(8,128)(2,1)} %get-tuple-element.45.refs_0_, bf16[13,32,256]{2,1,0:T(8,128)(2,1)} %copy-done.7, ...), custom_call_target="tpu_custom_call" | custom-call | flops 10485760 | bytes 6291456 | tf_op jit(solution)/shard_map/value_sums/pallas_call | solution.py:355
  68.5 0.0 collective-permute-done.8.refs_1_
  68.5 0.0 copy-done.14
  68.5 0.0 copy-start.1
  68.5 0.5 collective-permute-start.12
  69.0 1.3 all-to-all-done.got_ref
  70.3 1.5 %convert_bitcast_fusion.known_ref = s32[32,3,32]{2,1,0:T(4,128)} fusion(bf16[32,33,8,256]{3,2,1,0:T(8,128)(2,1)} %all-to-all-done.got_ref), kind=kLoop, calls=%fused_computation | loop fusion | flops 6144 | bytes 18432 | tf_op jit(solution)/shard_map/convert_element_type | solution.py:335
  71.8 7.9 %weight_sums.1.weight_ref = bf16[4,32,8,256]{3,2,1,0:T(8,128)(2,1)} custom-call(s32[32,3,32]{2,1,0:T(4,128)} %convert_bitcast_fusion.known_ref, s32[1]{0:T(128)} %bitcast.6.part_ref, bf16[32,33,8,256]{3,2,1,0:T(8,128)(2,1)} %all-to-all-done.got_ref), custom_call_target="tpu_custom_call" | custom-call | flops 20971520 | bytes 6291456 | tf_op jit(solution)/shard_map/weight_sums/pallas_call | solution.py:374
  79.7 0.0 copy-done
  79.7 0.0 collective-permute-done.9.refs_2_
  79.7 0.0 copy-start.2
  79.7 0.0 collective-permute-done.10.refs_3_
  79.7 0.0 copy-start.3
  79.7 0.0 collective-permute-done.11.refs_4_
  79.7 0.0 copy-done.1
  79.7 0.7 copy-done.2
  80.4 0.1 copy-done.3
  80.6 0.7 copy-done.5
  81.3 5.5 %value_sums.3.middle_ref = f32[32,4,2,16,256]{4,3,2,1,0:T(8,128)} custom-call(s32[8,3,32]{2,1,0:T(4,128)} %convert_convert_fusion.known_ref, s32[1]{0:T(128)} %bitcast.z_ref, s32[1]{0:T(128)} %bitcast.1.core_ref, bf16[20,32,256]{2,1,0:T(8,128)(2,1)} %copy-done, bf16[20,32,256]{2,1,0:T(8,128)(2,1)} %copy-done.1, bf16[20,32,256]{2,1,0:T(8,128)(2,1)} %copy-done.2, ...), custom_call_target="tpu_custom_call" | custom-call | flops 10485760 | bytes 6291456 | tf_op jit(solution)/shard_map/value_sums/pallas_call | solution.py:355
  86.8 0.0 collective-permute-done.13.refs_1_
  86.8 0.0 copy-start.4
  86.8 0.0 collective-permute-done.12.refs_0_
  86.8 0.8 copy-done.4
  87.6 0.7 copy-done.6
  88.3 7.2 %last_value_sums.1 = bf16[4,32,40,256]{3,2,1,0:T(8,128)(2,1)} custom-call(s32[8,3,32]{2,1,0:T(4,128)} %convert_convert_fusion.known_ref, s32[1]{0:T(128)} %bitcast.z_ref, s32[1]{0:T(128)} %bitcast.1.core_ref, bf16[4,32,8,256]{3,2,1,0:T(8,128)(2,1)} %weight_sums.1.weight_ref, f32[32,4,2,16,256]{4,3,2,1,0:T(8,128)} %value_sums.2.before_ref, ...), custom_call_target="tpu_custom_call" | custom-call | flops 10485760 | bytes 6291456 | tf_op jit(solution)/shard_map/last_value_sums/pallas_call | solution.py:393
  95.5 46.3 %all_to_all.10 = bf16[128,40,256]{2,1,0:T(8,128)(2,1)S(1)} all-to-all(bf16[128,40,256]{2,1,0:T(8,128)(2,1)} %bitcast.11), channel_id=1, replica_groups=mesh['epoch'=4,'patch'=32] {'epoch','patch'}, dimensions={0} | all-to-all | bytes 5242880 | tf_op jit(solution)/shard_map/all_to_all | solution.py:410
  141.7 1.1 final.1
  (19 shorter events, 0.1 us)
Async XLA Ops:
  7.9 62.4 %all-to-all-start = ((bf16[32,33,8,256]{3,2,1,0:T(8,128)(2,1)}), bf16[32,33,8,256]{3,2,1,0:T(8,128)(2,1)}, u32[]{:S(2)}, u32[]{:S(2)}) async-start(bf16[32,33,8,256]{3,2,1,0:T(8,128)(2,1)} %weights.1), calls=%async_computation | async-start | bytes 8650752 | tf_op jit(solution)/shard_map/all_to_all | solution.py:339
  24.6 19.9 %collective-permute-start = (bf16[13,32,256]{2,1,0:T(8,128)(2,1)}, bf16[13,32,256]{2,1,0:T(8,128)(2,1)S(1)}, u32[]{:S(2)}, u32[]{:S(2)}) collective-permute-start(bf16[13,32,256]{2,1,0:T(8,128)(2,1)} %get-tuple-element.32), channel_id=1, source_target_pairs={{0,32},{1,33},{2,34},{3,35},{4,36},{5,37},{6,38},{7,39},{8,40},{9,... | collective-permute-start | bytes 638984 | tf_op jit(solution)/shard_map/ppermute | solution.py:333
  26.3 18.9 %collective-permute-start.1 = (bf16[13,32,256]{2,1,0:T(8,128)(2,1)}, bf16[13,32,256]{2,1,0:T(8,128)(2,1)S(1)}, u32[]{:S(2)}, u32[]{:S(2)}) collective-permute-start(bf16[13,32,256]{2,1,0:T(8,128)(2,1)} %get-tuple-element.33), channel_id=1, source_target_pairs={{0,64},{1,65},{2,66},{3,67},{4,68},{5,69},{6,70},{7,71},{8,72},{9,... | collective-permute-start | bytes 638984 | tf_op jit(solution)/shard_map/ppermute | solution.py:333
  29.6 18.0 %collective-permute-start.2 = (bf16[13,32,256]{2,1,0:T(8,128)(2,1)}, bf16[13,32,256]{2,1,0:T(8,128)(2,1)S(1)}, u32[]{:S(2)}, u32[]{:S(2)}) collective-permute-start(bf16[13,32,256]{2,1,0:T(8,128)(2,1)} %get-tuple-element.34), channel_id=1, source_target_pairs={{0,96},{1,97},{2,98},{3,99},{4,100},{5,101},{6,102},{7,103},{8,104... | collective-permute-start | bytes 638984 | tf_op jit(solution)/shard_map/ppermute | solution.py:333
  30.4 17.4 %collective-permute-start.3 = (bf16[13,32,256]{2,1,0:T(8,128)(2,1)}, bf16[13,32,256]{2,1,0:T(8,128)(2,1)S(1)}, u32[]{:S(2)}, u32[]{:S(2)}) collective-permute-start(bf16[13,32,256]{2,1,0:T(8,128)(2,1)} %get-tuple-element.35), channel_id=1, source_target_pairs={{0,1},{1,0},{2,3},{3,2},{4,5},{5,4},{6,7},{7,6},{8,9},{9,8},{10,11... | collective-permute-start | bytes 638984 | tf_op jit(solution)/shard_map/ppermute | solution.py:333
  31.5 18.9 %collective-permute-start.4 = (bf16[13,32,256]{2,1,0:T(8,128)(2,1)}, bf16[13,32,256]{2,1,0:T(8,128)(2,1)S(1)}, u32[]{:S(2)}, u32[]{:S(2)}) collective-permute-start(bf16[13,32,256]{2,1,0:T(8,128)(2,1)} %get-tuple-element.36), channel_id=1, source_target_pairs={{0,33},{1,32},{2,35},{3,34},{4,37},{5,36},{6,39},{7,38},{8,41},{9,... | collective-permute-start | bytes 638984 | tf_op jit(solution)/shard_map/ppermute | solution.py:333
  32.1 12.4 %copy-start.16 = (bf16[13,32,256]{2,1,0:T(8,128)(2,1)S(1)}, bf16[13,32,256]{2,1,0:T(8,128)(2,1)}, u32[]{:S(2)}) copy-start(bf16[13,32,256]{2,1,0:T(8,128)(2,1)} %get-tuple-element.37) | copy-start | bytes 638980
  32.1 13.1 %copy-start.15 = (bf16[13,32,256]{2,1,0:T(8,128)(2,1)S(1)}, bf16[13,32,256]{2,1,0:T(8,128)(2,1)}, u32[]{:S(2)}) copy-start(bf16[13,32,256]{2,1,0:T(8,128)(2,1)} %get-tuple-element.38) | copy-start | bytes 638980
  43.8 24.6 %copy-start.14 = (bf16[20,32,256]{2,1,0:T(8,128)(2,1)S(1)}, bf16[20,32,256]{2,1,0:T(8,128)(2,1)}, u32[]{:S(2)}) copy-start(bf16[20,32,256]{2,1,0:T(8,128)(2,1)} %get-tuple-element.56) | copy-start | bytes 983044
  44.6 18.0 %copy-start.7 = (bf16[13,32,256]{2,1,0:T(8,128)(2,1)}, bf16[13,32,256]{2,1,0:T(8,128)(2,1)S(1)}, u32[]{:S(2)}) copy-start(bf16[13,32,256]{2,1,0:T(8,128)(2,1)S(1)} %collective-permute-done.refs_1_) | copy-start | bytes 638980
  44.6 9.6 %collective-permute-start.5 = (bf16[13,32,256]{2,1,0:T(8,128)(2,1)S(1)}, bf16[13,32,256]{2,1,0:T(8,128)(2,1)S(1)}, u32[]{:S(2)}, u32[]{:S(2)}) collective-permute-start(bf16[13,32,256]{2,1,0:T(8,128)(2,1)S(1)} %copy-done.16), channel_id=1, source_target_pairs={{0,65},{1,64},{2,67},{3,66},{4,69},{5,68},{6,71},{7,70},{8,73},{9,... | collective-permute-start | bytes 638984 | tf_op jit(solution)/shard_map/ppermute | solution.py:333
  45.3 17.3 %copy-start.8 = (bf16[13,32,256]{2,1,0:T(8,128)(2,1)}, bf16[13,32,256]{2,1,0:T(8,128)(2,1)S(1)}, u32[]{:S(2)}) copy-start(bf16[13,32,256]{2,1,0:T(8,128)(2,1)S(1)} %collective-permute-done.1.refs_2_) | copy-start | bytes 638980
  45.3 13.0 %collective-permute-start.6 = (bf16[13,32,256]{2,1,0:T(8,128)(2,1)S(1)}, bf16[13,32,256]{2,1,0:T(8,128)(2,1)S(1)}, u32[]{:S(2)}, u32[]{:S(2)}) collective-permute-start(bf16[13,32,256]{2,1,0:T(8,128)(2,1)S(1)} %copy-done.15), channel_id=1, source_target_pairs={{0,97},{1,96},{2,99},{3,98},{4,101},{5,100},{6,103},{7,102},{8,105... | collective-permute-start | bytes 638984 | tf_op jit(solution)/shard_map/ppermute | solution.py:333
  47.6 15.0 %copy-start.9 = (bf16[13,32,256]{2,1,0:T(8,128)(2,1)}, bf16[13,32,256]{2,1,0:T(8,128)(2,1)S(1)}, u32[]{:S(2)}) copy-start(bf16[13,32,256]{2,1,0:T(8,128)(2,1)S(1)} %collective-permute-done.2.refs_3_) | copy-start | bytes 638980
  47.6 13.4 %collective-permute-start.7 = (bf16[20,32,256]{2,1,0:T(8,128)(2,1)}, bf16[20,32,256]{2,1,0:T(8,128)(2,1)S(1)}, u32[]{:S(2)}, u32[]{:S(2)}) collective-permute-start(bf16[20,32,256]{2,1,0:T(8,128)(2,1)} %get-tuple-element.40), channel_id=1, source_target_pairs={{0,32},{1,33},{2,34},{3,35},{4,36},{5,37},{6,38},{7,39},{8,40},{9,... | collective-permute-start | bytes 983048 | tf_op jit(solution)/shard_map/ppermute | solution.py:333
  47.8 14.8 %copy-start.10 = (bf16[13,32,256]{2,1,0:T(8,128)(2,1)}, bf16[13,32,256]{2,1,0:T(8,128)(2,1)S(1)}, u32[]{:S(2)}) copy-start(bf16[13,32,256]{2,1,0:T(8,128)(2,1)S(1)} %collective-permute-done.3.refs_4_) | copy-start | bytes 638980
  47.8 20.6 %collective-permute-start.8 = (bf16[20,32,256]{2,1,0:T(8,128)(2,1)}, bf16[20,32,256]{2,1,0:T(8,128)(2,1)S(1)}, u32[]{:S(2)}, u32[]{:S(2)}) collective-permute-start(bf16[20,32,256]{2,1,0:T(8,128)(2,1)} %get-tuple-element.52), channel_id=1, source_target_pairs={{0,96},{1,97},{2,98},{3,99},{4,100},{5,101},{6,102},{7,103},{8,104... | collective-permute-start | bytes 983048 | tf_op jit(solution)/shard_map/ppermute | solution.py:333
  50.5 12.1 %copy-start.11 = (bf16[13,32,256]{2,1,0:T(8,128)(2,1)}, bf16[13,32,256]{2,1,0:T(8,128)(2,1)S(1)}, u32[]{:S(2)}) copy-start(bf16[13,32,256]{2,1,0:T(8,128)(2,1)S(1)} %collective-permute-done.4.refs_5_) | copy-start | bytes 638980
  50.5 29.2 %collective-permute-start.9 = (bf16[20,32,256]{2,1,0:T(8,128)(2,1)}, bf16[20,32,256]{2,1,0:T(8,128)(2,1)S(1)}, u32[]{:S(2)}, u32[]{:S(2)}) collective-permute-start(bf16[20,32,256]{2,1,0:T(8,128)(2,1)} %get-tuple-element.53), channel_id=1, source_target_pairs={{0,64},{1,65},{2,66},{3,67},{4,68},{5,69},{6,70},{7,71},{8,72},{9,... | collective-permute-start | bytes 983048 | tf_op jit(solution)/shard_map/ppermute | solution.py:333
  54.2 8.4 %copy-start.12 = (bf16[13,32,256]{2,1,0:T(8,128)(2,1)}, bf16[13,32,256]{2,1,0:T(8,128)(2,1)S(1)}, u32[]{:S(2)}) copy-start(bf16[13,32,256]{2,1,0:T(8,128)(2,1)S(1)} %collective-permute-done.5.refs_6_) | copy-start | bytes 638980
  54.2 25.5 %collective-permute-start.10 = (bf16[20,32,256]{2,1,0:T(8,128)(2,1)}, bf16[20,32,256]{2,1,0:T(8,128)(2,1)S(1)}, u32[]{:S(2)}, u32[]{:S(2)}) collective-permute-start(bf16[20,32,256]{2,1,0:T(8,128)(2,1)} %get-tuple-element.54), channel_id=1, source_target_pairs={{0,97},{1,96},{2,99},{3,98},{4,101},{5,100},{6,103},{7,102},{8,105... | collective-permute-start | bytes 983048 | tf_op jit(solution)/shard_map/ppermute | solution.py:333
  58.3 4.3 %copy-start.13 = (bf16[13,32,256]{2,1,0:T(8,128)(2,1)}, bf16[13,32,256]{2,1,0:T(8,128)(2,1)S(1)}, u32[]{:S(2)}) copy-start(bf16[13,32,256]{2,1,0:T(8,128)(2,1)S(1)} %collective-permute-done.6.refs_7_) | copy-start | bytes 638980
  58.3 21.4 %collective-permute-start.11 = (bf16[20,32,256]{2,1,0:T(8,128)(2,1)}, bf16[20,32,256]{2,1,0:T(8,128)(2,1)S(1)}, u32[]{:S(2)}, u32[]{:S(2)}) collective-permute-start(bf16[20,32,256]{2,1,0:T(8,128)(2,1)} %get-tuple-element.55), channel_id=1, source_target_pairs={{0,33},{1,32},{2,35},{3,34},{4,37},{5,36},{6,39},{7,38},{8,41},{9,... | collective-permute-start | bytes 983048 | tf_op jit(solution)/shard_map/ppermute | solution.py:333
  61.0 18.7 %copy-start = (bf16[20,32,256]{2,1,0:T(8,128)(2,1)}, bf16[20,32,256]{2,1,0:T(8,128)(2,1)S(1)}, u32[]{:S(2)}) copy-start(bf16[20,32,256]{2,1,0:T(8,128)(2,1)S(1)} %collective-permute-done.7.refs_0_) | copy-start | bytes 983044
  61.0 25.8 %collective-permute-start.13 = (bf16[20,32,256]{2,1,0:T(8,128)(2,1)}, bf16[20,32,256]{2,1,0:T(8,128)(2,1)S(1)}, u32[]{:S(2)}, u32[]{:S(2)}) collective-permute-start(bf16[20,32,256]{2,1,0:T(8,128)(2,1)} %get-tuple-element.57), channel_id=1, source_target_pairs={{0,65},{1,64},{2,67},{3,66},{4,69},{5,68},{6,71},{7,70},{8,73},{9,... | collective-permute-start | bytes 983048 | tf_op jit(solution)/shard_map/ppermute | solution.py:333
  68.5 11.2 %copy-start.1 = (bf16[20,32,256]{2,1,0:T(8,128)(2,1)}, bf16[20,32,256]{2,1,0:T(8,128)(2,1)S(1)}, u32[]{:S(2)}) copy-start(bf16[20,32,256]{2,1,0:T(8,128)(2,1)S(1)} %collective-permute-done.8.refs_1_) | copy-start | bytes 983044
  68.5 18.3 %collective-permute-start.12 = (bf16[20,32,256]{2,1,0:T(8,128)(2,1)S(1)}, bf16[20,32,256]{2,1,0:T(8,128)(2,1)S(1)}, u32[]{:S(2)}, u32[]{:S(2)}) collective-permute-start(bf16[20,32,256]{2,1,0:T(8,128)(2,1)S(1)} %copy-done.14), channel_id=1, source_target_pairs={{0,1},{1,0},{2,3},{3,2},{4,5},{5,4},{6,7},{7,6},{8,9},{9,8},{10,11... | collective-permute-start | bytes 983048 | tf_op jit(solution)/shard_map/ppermute | solution.py:333
  79.7 0.7 copy-start.2
  79.7 0.9 copy-start.3
  80.5 0.7 copy-start.5
  86.8 0.8 copy-start.4
  87.6 0.7 copy-start.6

commit v6 on v4

--- a/solution.py
+++ b/solution.py
@@ -13,7 +13,7 @@
 GROUP = 4
 WEIGHT_GROUP = 8
 FIRST = 12
-EARLY = (0,)
+EARLY = (0, 1, 3)
 
 
 def blur_kernels(side):
@@ -345,7 +345,7 @@
         more[m] = share(m, late[m])
     known = ints(jnp.stack([g[FIRST, :3, :count] for g in got]))
     shares = [(m, 0, FIRST) for m in range(8)] + [(m, FIRST, count - FIRST) for m in EARLY]
-    more[1], got[0], late_4 = lax.optimization_barrier((more[1], got[0], late[4]))
+    more[1], more[3], late_4 = lax.optimization_barrier((more[1], more[3], late[4]))
     value_sums = pl.pallas_call(
         functools.partial(first_values_body, shares),
         in_specs=[smem] * 3 + [hbm] * len(shares),

time: 141 us -> 140 us (level)
    all_to_all x1, waiting for transfers between devices: 1.74 us -> 0.01 us  [shards(): lax.all_to_all(weights, 'patch', split_axis=0, concat_axis=0, tiled=True)]
  transfers between devices with their start and end apart: 15 -> 15, of which waited for: 6 -> 5; matrix products, arithmetic and copies ran while one was open for 2% -> 2% of each run, Pallas kernels for 24% -> 24%
where the time goes in v6:
time: 140 us
  Pallas kernels  48.5 us (35%)
  blocking collectives  45.2 us (32%)
  starting transfers between devices  24.4 us (17%)
  waiting for transfers between devices  15.7 us (11%)
  local copies, waits for them, and re-layouts  2.93 us (2%)
  other arithmetic  2.09 us (1%)
    all_to_all x1, blocking collectives, shards(): lax.all_to_all(sums, ('epoch', 'patch'), split_axis=0, concat_axis=0, til...  45.2 us
    pallas_call x2, Pallas kernels, some_values(): pl.pallas_call(functools.partial(value_body, begin, tables), grid=(steps...  19.8 us
    ppermute x14, starting transfers between devices, share(): return lax.ppermute(rows, ('epoch', 'patch'), pairs)  15.8 us
    ppermute x14, waiting for transfers between devices, share(): return lax.ppermute(rows, ('epoch', 'patch'), pairs)  15.7 us
    all_to_all x1, starting transfers between devices, shards(): lax.all_to_all(weights, 'patch', split_axis=0, concat_axis=0, tiled=True)  8.63 us
    pallas_call x1, Pallas kernels, shards(): pl.pallas_call(weight_sum_body, in_specs=[smem, smem, hbm], out_specs=vme...  7.87 us
    pallas_call x1, Pallas kernels, shards(): pl.pallas_call(weight_body, grid=(steps + 1,), in_specs=[smem, smem, tile...  7.24 us
    pallas_call x1, Pallas kernels, shards(): pl.pallas_call(functools.partial(first_values_body, shares), in_specs=[sm...  6.48 us
  transfers between devices with their start and end apart: 15, of which 5 were waited for; matrix products, arithmetic and copies ran while one was open for 2% of the time, Pallas kernels for 24%

profile of v6, /device:TPU:1, one launch (start us, length us, event | category | flops | bytes accessed | tf_op | source)
XLA Modules:
  0.0 139.8 jit_solution(5882990749589608002)
XLA Ops:
  0.6 7.2 %weights.1 = bf16[32,33,8,256]{3,2,1,0:T(8,128)(2,1)} custom-call(s32[1,32]{1,0:T(1,128)} %bitcast.15, s32[2,32]{1,0:T(2,128)} %bitcast.12, bf16[32,256,256]{2,1,0:T(8,128)(2,1)} %var_ref.5), custom_call_target="tpu_custom_call" | custom-call | flops 41943040 | bytes 8388608 | tf_op jit(solution)/shard_map/weights/pallas_call | solution.py:294
  7.9 8.6 %all-to-all-start = ((bf16[32,33,8,256]{3,2,1,0:T(8,128)(2,1)}), bf16[32,33,8,256]{3,2,1,0:T(8,128)(2,1)}, u32[]{:S(2)}, u32[]{:S(2)}) async-start(bf16[32,33,8,256]{3,2,1,0:T(8,128)(2,1)} %weights.1), calls=%async_computation | async-start | bytes 8650752 | tf_op jit(solution)/shard_map/all_to_all | solution.py:334
  16.5 8.1 %values.2 = (bf16[13,32,256]{2,1,0:T(8,128)(2,1)}, bf16[13,32,256]{2,1,0:T(8,128)(2,1)}, bf16[13,32,256]{2,1,0:T(8,128)(2,1)}, bf16[13,32,256]{2,1,0:T(8,128)(2,...) custom-call(s32[1]{0:T(128)} %bitcast.z_ref, ...), custom_call_target="tpu_custom_call" | custom-call | flops 3221225472 | bytes 6291456 | tf_op jit(solution)/shard_map/values/pallas_call | solution.py:308
  24.6 1.7 %collective-permute-start = (bf16[13,32,256]{2,1,0:T(8,128)(2,1)}, bf16[13,32,256]{2,1,0:T(8,128)(2,1)S(1)}, u32[]{:S(2)}, u32[]{:S(2)}) collective-permute-start(bf16[13,32,256]{2,1,0:T(8,128)(2,1)} %get-tuple-element.30), channel_id=1, source_target_pairs={{0,32},{1,33},{2,34},{3,35},{4,36},{5,37},{6,38},{7,39},{8,40},{9,... | collective-permute-start | bytes 638984 | tf_op jit(solution)/shard_map/ppermute | solution.py:328
  26.4 3.3 %collective-permute-start.1 = (bf16[13,32,256]{2,1,0:T(8,128)(2,1)}, bf16[13,32,256]{2,1,0:T(8,128)(2,1)S(1)}, u32[]{:S(2)}, u32[]{:S(2)}) collective-permute-start(bf16[13,32,256]{2,1,0:T(8,128)(2,1)} %get-tuple-element.31), channel_id=1, source_target_pairs={{0,64},{1,65},{2,66},{3,67},{4,68},{5,69},{6,70},{7,71},{8,72},{9,... | collective-permute-start | bytes 638984 | tf_op jit(solution)/shard_map/ppermute | solution.py:328
  29.7 0.7 collective-permute-start.2
  30.4 1.1 collective-permute-start.3
  31.5 0.6 collective-permute-start.4
  32.1 0.0 copy-start.16
  32.1 0.0 copy-start.15
  32.2 11.7 %values.3 = (bf16[20,32,256]{2,1,0:T(8,128)(2,1)}, bf16[20,32,256]{2,1,0:T(8,128)(2,1)}, bf16[20,32,256]{2,1,0:T(8,128)(2,1)}, bf16[20,32,256]{2,1,0:T(8,128)(2,...) custom-call(s32[1]{0:T(128)} %bitcast.z_ref, ...), custom_call_target="tpu_custom_call" | custom-call | flops 3221225472 | bytes 6291456 | tf_op jit(solution)/shard_map/values/pallas_call | solution.py:308
  43.8 0.0 copy-start.14
  43.8 0.7 constant_dynamic-update-slice_fusion.7
  44.6 0.0 collective-permute-done.refs_1_
  44.6 0.0 copy-done.16
  44.6 0.7 collective-permute-start.5
  45.2 0.0 collective-permute-done.1.refs_2_
  45.3 0.0 copy-done.15
  45.3 2.3 %collective-permute-start.6 = (bf16[13,32,256]{2,1,0:T(8,128)(2,1)S(1)}, bf16[13,32,256]{2,1,0:T(8,128)(2,1)S(1)}, u32[]{:S(2)}, u32[]{:S(2)}) collective-permute-start(bf16[13,32,256]{2,1,0:T(8,128)(2,1)S(1)} %copy-done.15), channel_id=1, source_target_pairs={{0,97},{1,96},{2,99},{3,98},{4,101},{5,100},{6,103},{7,102},{8,105... | collective-permute-start | bytes 638984 | tf_op jit(solution)/shard_map/ppermute | solution.py:328
  47.5 0.0 collective-permute-done.2.refs_3_
  47.6 0.2 collective-permute-start.7
  47.8 0.0 collective-permute-done.3.refs_4_
  47.8 2.6 %collective-permute-start.8 = (bf16[20,32,256]{2,1,0:T(8,128)(2,1)}, bf16[20,32,256]{2,1,0:T(8,128)(2,1)S(1)}, u32[]{:S(2)}, u32[]{:S(2)}) collective-permute-start(bf16[20,32,256]{2,1,0:T(8,128)(2,1)} %get-tuple-element.40), channel_id=1, source_target_pairs={{0,96},{1,97},{2,98},{3,99},{4,100},{5,101},{6,102},{7,103},{8,104... | collective-permute-start | bytes 983048 | tf_op jit(solution)/shard_map/ppermute | solution.py:328
  50.4 0.0 collective-permute-done.4.refs_5_
  50.4 0.7 collective-permute-start.9
  51.1 3.1 %collective-permute-done.5.refs_6_ = bf16[13,32,256]{2,1,0:T(8,128)(2,1)S(1)} collective-permute-done((bf16[13,32,256]{2,1,0:T(8,128)(2,1)S(1)}, bf16[13,32,256]{2,1,0:T(8,128)(2,1)S(1)}, u32[]{:S(2)}, u32[]{:S(2)}) %collective-permute-start.5) | collective-permute-done | bytes 213024 | tf_op jit(solution)/shard_map/ppermute | solution.py:328
  54.2 0.0 collective-permute-start.11
  54.2 4.1 %collective-permute-done.6.refs_7_ = bf16[13,32,256]{2,1,0:T(8,128)(2,1)S(1)} collective-permute-done((bf16[13,32,256]{2,1,0:T(8,128)(2,1)S(1)}, bf16[13,32,256]{2,1,0:T(8,128)(2,1)S(1)}, u32[]{:S(2)}, u32[]{:S(2)}) %collective-permute-start.6) | collective-permute-done | bytes 213024 | tf_op jit(solution)/shard_map/ppermute | solution.py:328
  58.3 0.3 collective-permute-start.12
  58.6 0.6 convert_convert_fusion.known_ref
  59.2 1.8 %collective-permute-done.7.refs_9_ = bf16[20,32,256]{2,1,0:T(8,128)(2,1)S(1)} collective-permute-done((bf16[20,32,256]{2,1,0:T(8,128)(2,1)}, bf16[20,32,256]{2,1,0:T(8,128)(2,1)S(1)}, u32[]{:S(2)}, u32[]{:S(2)}) %collective-permute-start.7) | collective-permute-done | bytes 327712 | tf_op jit(solution)/shard_map/ppermute | solution.py:328
  61.0 0.7 collective-permute-start.13
  61.6 3.3 %collective-permute-done.8.refs_10_ = bf16[20,32,256]{2,1,0:T(8,128)(2,1)S(1)} collective-permute-done((bf16[20,32,256]{2,1,0:T(8,128)(2,1)}, bf16[20,32,256]{2,1,0:T(8,128)(2,1)S(1)}, u32[]{:S(2)}, u32[]{:S(2)}) %collective-permute-start.8) | collective-permute-done | bytes 327712 | tf_op jit(solution)/shard_map/ppermute | solution.py:328
  64.9 0.0 copy-done.7
  64.9 0.0 copy-done.8
  64.9 0.0 copy-done.9
  65.0 0.0 copy-done.10
  65.0 0.0 copy-done.11
  65.0 0.0 copy-done.12
  65.0 0.0 copy-done.13
  65.0 0.0 copy-done.3
  65.0 0.7 copy-done.4
  65.7 6.5 %first_value_sums.1.before_ref = f32[32,4,2,16,256]{4,3,2,1,0:T(8,128)} custom-call(s32[8,3,32]{2,1,0:T(4,128)} %convert_convert_fusion.known_ref, s32[1]{0:T(128)} %bitcast.z_ref, s32[1]{0:T(128)} %bitcast.1.core_ref, bf16[13,32,256]{2,1,0:T(8,128)(2,1)} %get-tuple-element.29.refs_0_, bf16[13,32,256]{2,1,0:T(8,128)(2,1)} %copy-done.7, ...), custom_call_target="tpu_custom_call" | custom-call | flops 10485760 | bytes 6291456 | tf_op jit(solution)/shard_map/first_value_sums/pallas_call | solution.py:349
  72.2 0.0 copy-done.14
  72.2 0.9 collective-permute-start.10
  73.1 0.0 all-to-all-done.got_ref
  73.1 1.5 %convert_bitcast_fusion.known_ref = s32[32,3,32]{2,1,0:T(4,128)} fusion(bf16[32,33,8,256]{3,2,1,0:T(8,128)(2,1)} %all-to-all-done.got_ref), kind=kLoop, calls=%fused_computation | loop fusion | flops 6144 | bytes 18432 | tf_op jit(solution)/shard_map/convert_element_type | solution.py:330
  74.6 7.9 %weight_sums.1.weight_ref = bf16[4,32,8,256]{3,2,1,0:T(8,128)(2,1)} custom-call(s32[32,3,32]{2,1,0:T(4,128)} %convert_bitcast_fusion.known_ref, s32[1]{0:T(128)} %bitcast.6.part_ref, bf16[32,33,8,256]{3,2,1,0:T(8,128)(2,1)} %all-to-all-done.got_ref), custom_call_target="tpu_custom_call" | custom-call | flops 20971520 | bytes 6291456 | tf_op jit(solution)/shard_map/weight_sums/pallas_call | solution.py:366
  82.4 0.0 collective-permute-done.9.refs_0_
  82.4 0.0 copy-start
  82.5 0.0 collective-permute-done.11.refs_2_
  82.5 0.0 copy-start.1
  82.5 0.0 collective-permute-done.12.refs_3_
  82.5 0.0 copy-start.2
  82.5 3.4 %collective-permute-done.13.refs_4_ = bf16[20,32,256]{2,1,0:T(8,128)(2,1)S(1)} collective-permute-done((bf16[20,32,256]{2,1,0:T(8,128)(2,1)}, bf16[20,32,256]{2,1,0:T(8,128)(2,1)S(1)}, u32[]{:S(2)}, u32[]{:S(2)}) %collective-permute-start.13) | collective-permute-done | bytes 327712 | tf_op jit(solution)/shard_map/ppermute | solution.py:328
  85.9 0.0 collective-permute-done.10.refs_1_
  86.0 0.0 copy-done
  86.0 0.0 copy-done.1
  86.0 0.0 copy-done.2
  86.0 0.7 copy-done.5
  86.7 0.7 copy-done.6
  87.4 6.1 %last_value_sums.1 = bf16[4,32,40,256]{3,2,1,0:T(8,128)(2,1)} custom-call(s32[8,3,32]{2,1,0:T(4,128)} %convert_convert_fusion.known_ref, s32[1]{0:T(128)} %bitcast.z_ref, s32[1]{0:T(128)} %bitcast.1.core_ref, bf16[4,32,8,256]{3,2,1,0:T(8,128)(2,1)} %weight_sums.1.weight_ref, f32[32,4,2,16,256]{4,3,2,1,0:T(8,128)} %first_value_sums.1.before_ref, ...), custom_call_target="tpu_custom_call" | custom-call | flops 10485760 | bytes 6291456 | tf_op jit(solution)/shard_map/last_value_sums/pallas_call | solution.py:381
  93.5 45.2 %all_to_all.10 = bf16[128,40,256]{2,1,0:T(8,128)(2,1)S(1)} all-to-all(bf16[128,40,256]{2,1,0:T(8,128)(2,1)} %bitcast.11), channel_id=1, replica_groups=mesh['epoch'=4,'patch'=32] {'epoch','patch'}, dimensions={0} | all-to-all | bytes 5242880 | tf_op jit(solution)/shard_map/all_to_all | solution.py:399
  138.7 1.1 final.1
  (18 shorter events, 0.1 us)
Async XLA Ops:
  7.9 65.2 %all-to-all-start = ((bf16[32,33,8,256]{3,2,1,0:T(8,128)(2,1)}), bf16[32,33,8,256]{3,2,1,0:T(8,128)(2,1)}, u32[]{:S(2)}, u32[]{:S(2)}) async-start(bf16[32,33,8,256]{3,2,1,0:T(8,128)(2,1)} %weights.1), calls=%async_computation | async-start | bytes 8650752 | tf_op jit(solution)/shard_map/all_to_all | solution.py:334
  24.6 19.9 %collective-permute-start = (bf16[13,32,256]{2,1,0:T(8,128)(2,1)}, bf16[13,32,256]{2,1,0:T(8,128)(2,1)S(1)}, u32[]{:S(2)}, u32[]{:S(2)}) collective-permute-start(bf16[13,32,256]{2,1,0:T(8,128)(2,1)} %get-tuple-element.30), channel_id=1, source_target_pairs={{0,32},{1,33},{2,34},{3,35},{4,36},{5,37},{6,38},{7,39},{8,40},{9,... | collective-permute-start | bytes 638984 | tf_op jit(solution)/shard_map/ppermute | solution.py:328
  26.4 18.9 %collective-permute-start.1 = (bf16[13,32,256]{2,1,0:T(8,128)(2,1)}, bf16[13,32,256]{2,1,0:T(8,128)(2,1)S(1)}, u32[]{:S(2)}, u32[]{:S(2)}) collective-permute-start(bf16[13,32,256]{2,1,0:T(8,128)(2,1)} %get-tuple-element.31), channel_id=1, source_target_pairs={{0,64},{1,65},{2,66},{3,67},{4,68},{5,69},{6,70},{7,71},{8,72},{9,... | collective-permute-start | bytes 638984 | tf_op jit(solution)/shard_map/ppermute | solution.py:328
  29.7 17.9 %collective-permute-start.2 = (bf16[13,32,256]{2,1,0:T(8,128)(2,1)}, bf16[13,32,256]{2,1,0:T(8,128)(2,1)S(1)}, u32[]{:S(2)}, u32[]{:S(2)}) collective-permute-start(bf16[13,32,256]{2,1,0:T(8,128)(2,1)} %get-tuple-element.32), channel_id=1, source_target_pairs={{0,96},{1,97},{2,98},{3,99},{4,100},{5,101},{6,102},{7,103},{8,104... | collective-permute-start | bytes 638984 | tf_op jit(solution)/shard_map/ppermute | solution.py:328
  30.4 17.4 %collective-permute-start.3 = (bf16[13,32,256]{2,1,0:T(8,128)(2,1)}, bf16[13,32,256]{2,1,0:T(8,128)(2,1)S(1)}, u32[]{:S(2)}, u32[]{:S(2)}) collective-permute-start(bf16[13,32,256]{2,1,0:T(8,128)(2,1)} %get-tuple-element.33), channel_id=1, source_target_pairs={{0,1},{1,0},{2,3},{3,2},{4,5},{5,4},{6,7},{7,6},{8,9},{9,8},{10,11... | collective-permute-start | bytes 638984 | tf_op jit(solution)/shard_map/ppermute | solution.py:328
  31.5 18.9 %collective-permute-start.4 = (bf16[13,32,256]{2,1,0:T(8,128)(2,1)}, bf16[13,32,256]{2,1,0:T(8,128)(2,1)S(1)}, u32[]{:S(2)}, u32[]{:S(2)}) collective-permute-start(bf16[13,32,256]{2,1,0:T(8,128)(2,1)} %get-tuple-element.34), channel_id=1, source_target_pairs={{0,33},{1,32},{2,35},{3,34},{4,37},{5,36},{6,39},{7,38},{8,41},{9,... | collective-permute-start | bytes 638984 | tf_op jit(solution)/shard_map/ppermute | solution.py:328
  32.1 12.4 %copy-start.16 = (bf16[13,32,256]{2,1,0:T(8,128)(2,1)S(1)}, bf16[13,32,256]{2,1,0:T(8,128)(2,1)}, u32[]{:S(2)}) copy-start(bf16[13,32,256]{2,1,0:T(8,128)(2,1)} %get-tuple-element.35) | copy-start | bytes 638980
  32.1 13.1 %copy-start.15 = (bf16[13,32,256]{2,1,0:T(8,128)(2,1)S(1)}, bf16[13,32,256]{2,1,0:T(8,128)(2,1)}, u32[]{:S(2)}) copy-start(bf16[13,32,256]{2,1,0:T(8,128)(2,1)} %get-tuple-element.36) | copy-start | bytes 638980
  43.8 28.3 %copy-start.14 = (bf16[20,32,256]{2,1,0:T(8,128)(2,1)S(1)}, bf16[20,32,256]{2,1,0:T(8,128)(2,1)}, u32[]{:S(2)}) copy-start(bf16[20,32,256]{2,1,0:T(8,128)(2,1)} %get-tuple-element.50) | copy-start | bytes 983044
  44.6 20.4 %copy-start.7 = (bf16[13,32,256]{2,1,0:T(8,128)(2,1)}, bf16[13,32,256]{2,1,0:T(8,128)(2,1)S(1)}, u32[]{:S(2)}) copy-start(bf16[13,32,256]{2,1,0:T(8,128)(2,1)S(1)} %collective-permute-done.refs_1_) | copy-start | bytes 638980
  44.6 9.6 %collective-permute-start.5 = (bf16[13,32,256]{2,1,0:T(8,128)(2,1)S(1)}, bf16[13,32,256]{2,1,0:T(8,128)(2,1)S(1)}, u32[]{:S(2)}, u32[]{:S(2)}) collective-permute-start(bf16[13,32,256]{2,1,0:T(8,128)(2,1)S(1)} %copy-done.16), channel_id=1, source_target_pairs={{0,65},{1,64},{2,67},{3,66},{4,69},{5,68},{6,71},{7,70},{8,73},{9,... | collective-permute-start | bytes 638984 | tf_op jit(solution)/shard_map/ppermute | solution.py:328
  45.2 19.7 %copy-start.8 = (bf16[13,32,256]{2,1,0:T(8,128)(2,1)}, bf16[13,32,256]{2,1,0:T(8,128)(2,1)S(1)}, u32[]{:S(2)}) copy-start(bf16[13,32,256]{2,1,0:T(8,128)(2,1)S(1)} %collective-permute-done.1.refs_2_) | copy-start | bytes 638980
  45.3 13.0 %collective-permute-start.6 = (bf16[13,32,256]{2,1,0:T(8,128)(2,1)S(1)}, bf16[13,32,256]{2,1,0:T(8,128)(2,1)S(1)}, u32[]{:S(2)}, u32[]{:S(2)}) collective-permute-start(bf16[13,32,256]{2,1,0:T(8,128)(2,1)S(1)} %copy-done.15), channel_id=1, source_target_pairs={{0,97},{1,96},{2,99},{3,98},{4,101},{5,100},{6,103},{7,102},{8,105... | collective-permute-start | bytes 638984 | tf_op jit(solution)/shard_map/ppermute | solution.py:328
  47.6 17.4 %copy-start.9 = (bf16[13,32,256]{2,1,0:T(8,128)(2,1)}, bf16[13,32,256]{2,1,0:T(8,128)(2,1)S(1)}, u32[]{:S(2)}) copy-start(bf16[13,32,256]{2,1,0:T(8,128)(2,1)S(1)} %collective-permute-done.2.refs_3_) | copy-start | bytes 638980
  47.6 13.4 %collective-permute-start.7 = (bf16[20,32,256]{2,1,0:T(8,128)(2,1)}, bf16[20,32,256]{2,1,0:T(8,128)(2,1)S(1)}, u32[]{:S(2)}, u32[]{:S(2)}) collective-permute-start(bf16[20,32,256]{2,1,0:T(8,128)(2,1)} %get-tuple-element.39), channel_id=1, source_target_pairs={{0,32},{1,33},{2,34},{3,35},{4,36},{5,37},{6,38},{7,39},{8,40},{9,... | collective-permute-start | bytes 983048 | tf_op jit(solution)/shard_map/ppermute | solution.py:328
  47.8 17.2 %copy-start.10 = (bf16[13,32,256]{2,1,0:T(8,128)(2,1)}, bf16[13,32,256]{2,1,0:T(8,128)(2,1)S(1)}, u32[]{:S(2)}) copy-start(bf16[13,32,256]{2,1,0:T(8,128)(2,1)S(1)} %collective-permute-done.3.refs_4_) | copy-start | bytes 638980
  47.8 17.1 %collective-permute-start.8 = (bf16[20,32,256]{2,1,0:T(8,128)(2,1)}, bf16[20,32,256]{2,1,0:T(8,128)(2,1)S(1)}, u32[]{:S(2)}, u32[]{:S(2)}) collective-permute-start(bf16[20,32,256]{2,1,0:T(8,128)(2,1)} %get-tuple-element.40), channel_id=1, source_target_pairs={{0,96},{1,97},{2,98},{3,99},{4,100},{5,101},{6,102},{7,103},{8,104... | collective-permute-start | bytes 983048 | tf_op jit(solution)/shard_map/ppermute | solution.py:328
  50.4 14.6 %copy-start.11 = (bf16[13,32,256]{2,1,0:T(8,128)(2,1)}, bf16[13,32,256]{2,1,0:T(8,128)(2,1)S(1)}, u32[]{:S(2)}) copy-start(bf16[13,32,256]{2,1,0:T(8,128)(2,1)S(1)} %collective-permute-done.4.refs_5_) | copy-start | bytes 638980
  50.4 32.0 %collective-permute-start.9 = (bf16[20,32,256]{2,1,0:T(8,128)(2,1)}, bf16[20,32,256]{2,1,0:T(8,128)(2,1)S(1)}, u32[]{:S(2)}, u32[]{:S(2)}) collective-permute-start(bf16[20,32,256]{2,1,0:T(8,128)(2,1)} %get-tuple-element.49), channel_id=1, source_target_pairs={{0,64},{1,65},{2,66},{3,67},{4,68},{5,69},{6,70},{7,71},{8,72},{9,... | collective-permute-start | bytes 983048 | tf_op jit(solution)/shard_map/ppermute | solution.py:328
  54.2 10.8 %copy-start.12 = (bf16[13,32,256]{2,1,0:T(8,128)(2,1)}, bf16[13,32,256]{2,1,0:T(8,128)(2,1)S(1)}, u32[]{:S(2)}) copy-start(bf16[13,32,256]{2,1,0:T(8,128)(2,1)S(1)} %collective-permute-done.5.refs_6_) | copy-start | bytes 638980
  54.2 28.3 %collective-permute-start.11 = (bf16[20,32,256]{2,1,0:T(8,128)(2,1)}, bf16[20,32,256]{2,1,0:T(8,128)(2,1)S(1)}, u32[]{:S(2)}, u32[]{:S(2)}) collective-permute-start(bf16[20,32,256]{2,1,0:T(8,128)(2,1)} %get-tuple-element.51), channel_id=1, source_target_pairs={{0,33},{1,32},{2,35},{3,34},{4,37},{5,36},{6,39},{7,38},{8,41},{9,... | collective-permute-start | bytes 983048 | tf_op jit(solution)/shard_map/ppermute | solution.py:328
  58.3 6.7 %copy-start.13 = (bf16[13,32,256]{2,1,0:T(8,128)(2,1)}, bf16[13,32,256]{2,1,0:T(8,128)(2,1)S(1)}, u32[]{:S(2)}) copy-start(bf16[13,32,256]{2,1,0:T(8,128)(2,1)S(1)} %collective-permute-done.6.refs_7_) | copy-start | bytes 638980
  58.3 24.2 %collective-permute-start.12 = (bf16[20,32,256]{2,1,0:T(8,128)(2,1)}, bf16[20,32,256]{2,1,0:T(8,128)(2,1)S(1)}, u32[]{:S(2)}, u32[]{:S(2)}) collective-permute-start(bf16[20,32,256]{2,1,0:T(8,128)(2,1)} %get-tuple-element.52), channel_id=1, source_target_pairs={{0,65},{1,64},{2,67},{3,66},{4,69},{5,68},{6,71},{7,70},{8,73},{9,... | collective-permute-start | bytes 983048 | tf_op jit(solution)/shard_map/ppermute | solution.py:328
  61.0 4.0 %copy-start.3 = (bf16[20,32,256]{2,1,0:T(8,128)(2,1)}, bf16[20,32,256]{2,1,0:T(8,128)(2,1)S(1)}, u32[]{:S(2)}) copy-start(bf16[20,32,256]{2,1,0:T(8,128)(2,1)S(1)} %collective-permute-done.7.refs_9_) | copy-start | bytes 983044
  61.0 25.0 %collective-permute-start.13 = (bf16[20,32,256]{2,1,0:T(8,128)(2,1)}, bf16[20,32,256]{2,1,0:T(8,128)(2,1)S(1)}, u32[]{:S(2)}, u32[]{:S(2)}) collective-permute-start(bf16[20,32,256]{2,1,0:T(8,128)(2,1)} %get-tuple-element.53), channel_id=1, source_target_pairs={{0,97},{1,96},{2,99},{3,98},{4,101},{5,100},{6,103},{7,102},{8,105... | collective-permute-start | bytes 983048 | tf_op jit(solution)/shard_map/ppermute | solution.py:328
  64.9 0.7 copy-start.4
  72.2 13.8 %collective-permute-start.10 = (bf16[20,32,256]{2,1,0:T(8,128)(2,1)S(1)}, bf16[20,32,256]{2,1,0:T(8,128)(2,1)S(1)}, u32[]{:S(2)}, u32[]{:S(2)}) collective-permute-start(bf16[20,32,256]{2,1,0:T(8,128)(2,1)S(1)} %copy-done.14), channel_id=1, source_target_pairs={{0,1},{1,0},{2,3},{3,2},{4,5},{5,4},{6,7},{7,6},{8,9},{9,8},{10,11... | collective-permute-start | bytes 983048 | tf_op jit(solution)/shard_map/ppermute | solution.py:328
  82.4 3.5 %copy-start = (bf16[20,32,256]{2,1,0:T(8,128)(2,1)}, bf16[20,32,256]{2,1,0:T(8,128)(2,1)S(1)}, u32[]{:S(2)}) copy-start(bf16[20,32,256]{2,1,0:T(8,128)(2,1)S(1)} %collective-permute-done.9.refs_0_) | copy-start | bytes 983044
  82.5 3.5 %copy-start.1 = (bf16[20,32,256]{2,1,0:T(8,128)(2,1)}, bf16[20,32,256]{2,1,0:T(8,128)(2,1)S(1)}, u32[]{:S(2)}) copy-start(bf16[20,32,256]{2,1,0:T(8,128)(2,1)S(1)} %collective-permute-done.11.refs_2_) | copy-start | bytes 983044
  82.5 3.5 %copy-start.2 = (bf16[20,32,256]{2,1,0:T(8,128)(2,1)}, bf16[20,32,256]{2,1,0:T(8,128)(2,1)S(1)}, u32[]{:S(2)}) copy-start(bf16[20,32,256]{2,1,0:T(8,128)(2,1)S(1)} %collective-permute-done.12.refs_3_) | copy-start | bytes 983044
  85.9 0.7 copy-start.5
  86.7 0.7 copy-start.6
